TPU v7x, 128 devices: a whole 4x4x4 slice. The times are simulated.
128 devices in a mesh: rows: 16 (over y, z), grp: 8 (over x, core).
Axes of the slice: x: 4, y: 4, z: 4, core: 2. Of those that a mesh axis runs over, the one named last changes fastest.
Arguments:
- hamiltonian: float32 [13824, 13824], P(('rows', 'grp')), as said below
- current: float32 [13824, 16], P(('rows', 'grp')), may hold values from -6 to 6
- previous: float32 [13824, 16], P(('rows', 'grp')), may hold values from -6 to 6
Outputs:
- new_current: float32 [13824, 16], P(('rows', 'grp'))
- new_previous: float32 [13824, 16], P(('rows', 'grp'))
- residual_rms: float32 [16], replicated
Inputs may be any that keep to these rules, and one draw needn't show every extreme that they name: hamiltonian is symmetric: hamiltonian[i, j] equals hamiltonian[j, i].
All inputs are finite; a program needn't handle non-finite values.
Results may differ from a plain program's by a relative error of at most 0.0003.
Values sent between devices are 32-bit elements; how exact they have to be, the bound alone decides.
No kernel may reach another device: no remote copies, remote signals or barrier semaphores. Data moves between devices by JAX's collectives and lax.ppermute only.
A program may use at most 64 MiB of HBM per device.

v0:
```python
import math

import jax
import jax.numpy as jnp
from jax import lax
from jax.sharding import Mesh
from jax.sharding import PartitionSpec as P

NEIG = 16
SIGN_STEPS = 6
ORDER = 13824
ROWS_GRP = ("rows_0", "rows_1", "grp_0", "grp_1")


highest = lax.Precision.HIGHEST
eps_value = 1e-06


def sent_to_all(x, axis):
    length = lax.axis_size(axis)
    return lax.all_to_all(jnp.broadcast_to(x[None], (length, *x.shape)), axis, 0, 0, tiled=True)


def laid_out(blocks, dim):
    blocks = jnp.moveaxis(blocks, 0, dim)
    shape = blocks.shape
    return blocks.reshape(*shape[:dim], shape[dim] * shape[dim + 1], *shape[dim + 2 :])


def gather_axes(x, axes, dim):
    far, near = axes
    initial = sent_to_all(x, far)
    blocks = jnp.swapaxes(sent_to_all(initial, near), 0, 1)
    return laid_out(blocks.reshape(-1, *x.shape), dim)


def taken_together(x, axis):
    return sent_to_all(x, axis).sum(axis=0)


def one_axis_at_a_time(x, axes):
    far, near = axes
    return taken_together(taken_together(x, near), far)


def in_one(arrays, axis):
    line, at, outs = (jnp.concatenate([a.reshape(-1) for a in arrays]), 0, [])
    running = one_axis_at_a_time(line, axis)
    for a in arrays:
        outs.append(running[at : at + a.size].reshape(a.shape))
        at += a.size
    return tuple(outs)


def mat_mul(left, right):
    return jnp.dot(left, right, precision=highest, preferred_element_type=jnp.float32)


def diag_of(matrix):
    mask = jnp.eye(matrix.shape[0], dtype=matrix.dtype)
    return jnp.sum(matrix * mask, axis=1)


def ritz_update(stiff, mass):
    stiff_sym = 0.5 * (stiff + stiff.T)
    lower = jnp.linalg.cholesky(mass)
    half_way = jax.scipy.linalg.solve_triangular(lower, stiff_sym, lower=True)
    reduced = jax.scipy.linalg.solve_triangular(lower, half_way.T, lower=True)
    identity = jnp.eye(reduced.shape[0], dtype=reduced.dtype)
    level = jnp.max(diag_of(reduced)[:NEIG])
    signed = level * identity - reduced
    signed = signed / jnp.sqrt(jnp.sum(signed * signed))
    for sweep_index in range(SIGN_STEPS):
        signed = 1.5 * signed - 0.5 * mat_mul(signed, mat_mul(signed, signed))
    projector = 0.5 * (identity + signed)
    coeffs = jax.scipy.linalg.solve_triangular(lower, projector[:, :NEIG], trans=1, lower=True)
    return coeffs * math.sqrt(ORDER)


def body(hamiltonian, current, previous):
    row_count = current.shape[0]
    offset = lax.axis_index(ROWS_GRP) * row_count
    own_block = lax.dynamic_slice_in_dim(hamiltonian, offset, row_count, 1)
    diag_vals = diag_of(own_block)

    def apply_ham(block):
        return mat_mul(hamiltonian, gather_axes(block, (("rows_0", "rows_1", "grp_0"), "grp_1"), 0))

    paired = jnp.concatenate([current, previous], axis=1)
    hpaired = apply_ham(paired)
    image = hpaired[:, :NEIG]
    hprev = hpaired[:, NEIG:]
    cross_sum, gram_sum, image_sq = in_one(
        (mat_mul(current.T, image), mat_mul(current.T, current), jnp.sum(image * image, axis=0)),
        (("rows_0", "rows_1", "grp_0"), "grp_1"),
    )
    ritz = cross_sum / ORDER
    resid = image - mat_mul(current, ritz)
    squares = (
        image_sq
        - 2.0 * jnp.sum(cross_sum * ritz, axis=0)
        + jnp.sum(ritz * mat_mul(gram_sum, ritz), axis=0)
    )
    residual_rms = jnp.sqrt(squares / ORDER + eps_value)
    shift = jnp.maximum(jnp.abs(diag_vals[:, None] - diag_of(ritz)[None, :]), 1.0)
    search = resid / (shift * residual_rms[None, :])
    hsearch = apply_ham(search)
    basis = jnp.concatenate([current, search, previous], axis=1)
    himage = jnp.concatenate([image, hsearch, hprev], axis=1)
    stiff, mass = in_one(
        (mat_mul(basis.T, himage), mat_mul(basis.T, basis)),
        (("rows_0", "rows_1"), ("grp_0", "grp_1")),
    )
    coeffs = ritz_update(stiff, mass)
    new_current = mat_mul(basis, coeffs)
    new_previous = mat_mul(basis[:, NEIG:], coeffs[NEIG:])
    return (new_current, new_previous, residual_rms)


def solution(mesh):
    finer = Mesh(mesh.devices.reshape(4, 4, 4, 2), ("rows_0", "rows_1", "grp_0", "grp_1"))
    return jax.shard_map(
        body,
        mesh=finer,
        in_specs=(P(ROWS_GRP, None), P(ROWS_GRP, None), P(ROWS_GRP, None)),
        out_specs=(P(ROWS_GRP, None), P(ROWS_GRP, None), P()),
        check_vma=False,
    )
```

profile of v0, /device:TPU:1, one launch (start us, length us, event | category | flops | bytes accessed | tf_op | source)
XLA Modules:
  0.0 147.5 jit_solution(7837081522644723171)
XLA Ops:
  1.4 1.1 broadcast_in_dim.17
  2.5 12.0 %all-to-all-start = ((f32[64,108,32]{1,2,0:T(8,128)}), f32[64,108,32]{1,2,0:T(8,128)S(1)}, u32[]{:S(2)}, u32[]{:S(2)}) async-start(f32[64,108,32]{1,2,0:T(8,128)} %broadcast_in_dim.17), calls=%async_computation | async-start | bytes 2097152 | tf_op jit(solution)/shard_map/all_to_all | solution.py:21
  14.4 0.9 fusion.61
  15.4 16.5 %all-to-all-done = f32[64,108,32]{1,2,0:T(8,128)S(1)} async-done(((f32[64,108,32]{1,2,0:T(8,128)}), f32[64,108,32]{1,2,0:T(8,128)S(1)}, u32[]{:S(2)}, u32[]{:S(2)}) %all-to-all-start) | async-done | bytes 884768 | tf_op jit(solution)/shard_map/all_to_all | solution.py:21
  32.8 7.4 %all_to_all.44 = f32[2,64,108,32]{2,1,3,0:T(8,128)S(1)} all-to-all(f32[2,64,108,32]{2,1,3,0:T(8,128)S(1)} %broadcast_in_dim.18), channel_id=1, replica_groups=mesh['rows_0'=4,'rows_1'=4,'grp_0'=4,'grp_1'=2] {'grp_1'}, dimensions={0} | all-to-all | bytes 3538944 | tf_op jit(solution)/shard_map/all_to_all | solution.py:21
  40.3 1.7 %copy.58 = f32[64,2,108,32]{2,1,0,3:T(2,128)S(1)} copy(f32[64,2,108,32]{2,0,3,1:T(8,128)S(1)} %bitcast.76) | data formatting | bytes 3538944 | tf_op jit(solution)/shard_map/transpose | solution.py:33
  42.0 4.3 %reshape_reshape.6 = f32[13824,32]{0,1:T(8,128)} reshape(f32[64,2,108,32]{2,1,0,3:T(2,128)S(1)} %copy.58) | data formatting | bytes 3538944 | tf_op jit(solution)/shard_map/reshape;reshape | solution.py:27
  46.3 9.5 %convolution_bitcast_fusion.1 = f32[108,32]{0,1:T(8,128)S(1)} fusion(f32[13824,32]{0,1:T(8,128)} %reshape_reshape.6, f32[108,13824]{1,0:T(8,128)} %param.5), kind=kOutput, calls=%fused_computation.11 | convolution fusion | flops 573308928 | bytes 7755264 | tf_op jit(solution)/shard_map/dot_general | solution.py:56
  56.2 3.7 %all_to_all.45 = f32[2,1,528]{2,1,0:T(1,128)S(1)} all-to-all(f32[2,1,528]{2,1,0:T(1,128)S(1)} %broadcast_in_dim.19), channel_id=1, replica_groups=mesh['rows_0'=4,'rows_1'=4,'grp_0'=4,'grp_1'=2] {'grp_1'}, dimensions={0} | all-to-all | bytes 8448 | tf_op jit(solution)/shard_map/all_to_all | solution.py:21
  60.7 4.8 %all-to-all-start.3 = ((f32[64,1,528]{2,1,0:T(1,128)}), f32[64,1,528]{2,1,0:T(1,128)S(1)}, u32[]{:S(2)}, u32[]{:S(2)}) async-start(f32[64,1,528]{2,1,0:T(1,128)} %broadcast_in_dim.20), calls=%async_computation.3 | async-start | bytes 327680 | tf_op jit(solution)/shard_map/all_to_all | solution.py:21
  65.5 1.1 select_reduce_fusion
  66.6 8.0 %all-to-all-done.3 = f32[64,1,528]{2,1,0:T(1,128)S(1)} async-done(((f32[64,1,528]{2,1,0:T(1,128)}), f32[64,1,528]{2,1,0:T(1,128)S(1)}, u32[]{:S(2)}, u32[]{:S(2)}) %all-to-all-start.3) | async-done | bytes 135200 | tf_op jit(solution)/shard_map/all_to_all | solution.py:21
  76.3 4.6 %all-to-all-start.4 = ((f32[64,108,16]{1,2,0:T(8,128)}), f32[64,108,16]{1,2,0:T(8,128)S(1)}, u32[]{:S(2)}, u32[]{:S(2)}) async-start(f32[64,108,16]{1,2,0:T(8,128)} %broadcast_in_dim.21), calls=%async_computation.4 | async-start | bytes 1048576 | tf_op jit(solution)/shard_map/all_to_all | solution.py:21
  81.2 11.6 %all-to-all-done.4 = f32[64,108,16]{1,2,0:T(8,128)S(1)} async-done(((f32[64,108,16]{1,2,0:T(8,128)}), f32[64,108,16]{1,2,0:T(8,128)S(1)}, u32[]{:S(2)}, u32[]{:S(2)}) %all-to-all-start.4) | async-done | bytes 442400 | tf_op jit(solution)/shard_map/all_to_all | solution.py:21
  93.0 6.8 %all_to_all.46 = f32[2,64,108,16]{2,1,3,0:T(8,128)S(1)} all-to-all(f32[2,64,108,16]{2,1,3,0:T(8,128)S(1)} %broadcast_in_dim.22), channel_id=1, replica_groups=mesh['rows_0'=4,'rows_1'=4,'grp_0'=4,'grp_1'=2] {'grp_1'}, dimensions={0} | all-to-all | bytes 1769472 | tf_op jit(solution)/shard_map/all_to_all | solution.py:21
  100.6 1.3 reshape_reshape.7
  102.0 6.9 %convolution_bitcast_fusion.2 = f32[108,16]{0,1:T(8,128)S(1)} fusion(f32[13824,16]{0,1:T(8,128)S(1)} %reshape_reshape.7, f32[108,13824]{1,0:T(8,128)} %param.5), kind=kOutput, calls=%fused_computation.14 | convolution fusion | flops 286654464 | bytes 6863616 | tf_op jit(solution)/shard_map/dot_general | solution.py:56
  109.2 8.2 %all_to_all.47 = f32[8,1,4608]{2,1,0:T(1,128)S(1)} all-to-all(f32[8,1,4608]{2,1,0:T(1,128)S(1)} %broadcast_in_dim.23), channel_id=1, replica_groups=mesh['rows_0'=4,'rows_1'=4,'grp_0'=4,'grp_1'=2] {'grp_0','grp_1'}, dimensions={0} | all-to-all | bytes 294912 | tf_op jit(solution)/shard_map/all_to_all | solution.py:21
  117.5 0.9 broadcast_in_dim.24
  118.4 3.5 %all-to-all-start.7 = ((f32[16,1,4608]{2,1,0:T(1,128)}), f32[16,1,4608]{2,1,0:T(1,128)S(1)}, u32[]{:S(2)}, u32[]{:S(2)}) async-start(f32[16,1,4608]{2,1,0:T(1,128)} %broadcast_in_dim.24), calls=%async_computation.7 | async-start | bytes 589824 | tf_op jit(solution)/shard_map/all_to_all | solution.py:21
  121.9 7.5 %all-to-all-done.7 = f32[16,1,4608]{2,1,0:T(1,128)S(1)} async-done(((f32[16,1,4608]{2,1,0:T(1,128)}), f32[16,1,4608]{2,1,0:T(1,128)S(1)}, u32[]{:S(2)}, u32[]{:S(2)}) %all-to-all-start.7) | async-done | bytes 294944 | tf_op jit(solution)/shard_map/all_to_all | solution.py:21
  130.0 4.4 %cholesky.19 = f32[48,48]{1,0:T(8,128)S(1)} custom-call(f32[48,48]{1,0:T(8,128)S(1)} %fusion.25), custom_call_target="Cholesky" | custom-call | tf_op jit(solution)/shard_map/jit(cholesky)/cholesky | solution.py:66
  135.7 3.7 %custom-call.10 = f32[1,48,48]{1,2,0:T(8,128)S(1)} custom-call(f32[1,48,48]{2,1,0:T(8,128)S(1)} %fusion.8), custom_call_target="InvertDiagBlocksLowerTriangular" | custom-call | tf_op jit(solution)/shard_map/jit(_solve_triangular)/triangular_solve | solution.py:76
  140.5 1.3 multiply_reduce_fusion
  (66 shorter events, 14.2 us)
Async XLA Ops:
  2.5 29.5 %all-to-all-start = ((f32[64,108,32]{1,2,0:T(8,128)}), f32[64,108,32]{1,2,0:T(8,128)S(1)}, u32[]{:S(2)}, u32[]{:S(2)}) async-start(f32[64,108,32]{1,2,0:T(8,128)} %broadcast_in_dim.17), calls=%async_computation | async-start | bytes 2097152 | tf_op jit(solution)/shard_map/all_to_all | solution.py:21
  41.9 13.9 %copy-start = (f32[108,16]{0,1:T(8,128)S(1)}, f32[108,16]{0,1:T(8,128)}, u32[]{:S(2)}) copy-start(f32[108,16]{0,1:T(8,128)} %param.6) | copy-start | bytes 20740
  46.3 34.7 %copy-start.1 = (f32[108,16]{0,1:T(8,128)S(1)}, f32[108,16]{0,1:T(8,128)}, u32[]{:S(2)}) copy-start(f32[108,16]{0,1:T(8,128)} %param.7) | copy-start | bytes 20740
  60.7 13.9 %all-to-all-start.3 = ((f32[64,1,528]{2,1,0:T(1,128)}), f32[64,1,528]{2,1,0:T(1,128)S(1)}, u32[]{:S(2)}, u32[]{:S(2)}) async-start(f32[64,1,528]{2,1,0:T(1,128)} %broadcast_in_dim.20), calls=%async_computation.3 | async-start | bytes 327680 | tf_op jit(solution)/shard_map/all_to_all | solution.py:21
  75.2 33.7 %copy-start.2 = (f32[16]{0:T(128)}, f32[16]{0:T(128)S(1)}, u32[]{:S(2)}) copy-start(f32[16]{0:T(128)S(1)} %add_sqrt_fusion) | copy-start | bytes 196
  76.3 16.5 %all-to-all-start.4 = ((f32[64,108,16]{1,2,0:T(8,128)}), f32[64,108,16]{1,2,0:T(8,128)S(1)}, u32[]{:S(2)}, u32[]{:S(2)}) async-start(f32[64,108,16]{1,2,0:T(8,128)} %broadcast_in_dim.21), calls=%async_computation.4 | async-start | bytes 1048576 | tf_op jit(solution)/shard_map/all_to_all | solution.py:21
  118.4 11.1 %all-to-all-start.7 = ((f32[16,1,4608]{2,1,0:T(1,128)}), f32[16,1,4608]{2,1,0:T(1,128)S(1)}, u32[]{:S(2)}, u32[]{:S(2)}) async-start(f32[16,1,4608]{2,1,0:T(1,128)} %broadcast_in_dim.24), calls=%async_computation.7 | async-start | bytes 589824 | tf_op jit(solution)/shard_map/all_to_all | solution.py:21
where the time goes:
time: 149 us; the launch traced here: 147 us
  waiting for transfers between devices  43.6 us (29%)
  blocking collectives  26.1 us (18%)
  starting transfers between devices  24.9 us (17%)
  matrix products  23.5 us (16%)
  other arithmetic  13.8 us (9%)
  local copies, waits for them, and re-layouts  13.8 us (9%)
  between operations  1.67 us (1%)
    all_to_all x4, waiting for transfers between devices, sent_to_all(): lax.all_to_all(jnp.broadcast_to(x[None], (length, *x.shape)), axis, 0, 0,...  43.6 us
    all_to_all x4, blocking collectives, sent_to_all(): lax.all_to_all(jnp.broadcast_to(x[None], (length, *x.shape)), axis, 0, 0,...  26.1 us
    all_to_all x4, starting transfers between devices, sent_to_all(): lax.all_to_all(jnp.broadcast_to(x[None], (length, *x.shape)), axis, 0, 0,...  24.9 us
    dot_general x22, matrix products, mat_mul(): jnp.dot(left, right, precision=highest, preferred_element_type=jnp.float32)  22.8 us
    another operation x2, local copies, waits for them, and re-layouts, laid_out(): blocks.reshape(*shape[:dim], shape[dim] * shape[dim + 1], *shape[dim + 2:])  5.64 us
    another operation x4, other arithmetic, ritz_update(): lower = jnp.linalg.cholesky(mass)  5.06 us
    another operation x2, other arithmetic, ritz_update(): jax.scipy.linalg.solve_triangular(lower, projector[:, :NEIG], trans=1, lo...  4.32 us
    broadcast_in_dim x8, local copies, waits for them, and re-layouts, sent_to_all(): jnp.broadcast_to(x[None], (length, *x.shape))  4.01 us
  transfers between devices with their start and end apart: 4, of which 4 were waited for; matrix products, arithmetic and copies ran while one was open for 2% of the time, Pallas kernels for 0%

commit v1 on v0

v1 whole, which is shorter than its diff:
```python
import math

import jax
import jax.numpy as jnp
from jax import lax
from jax.experimental import pallas as pl
from jax.experimental.pallas import tpu as pltpu
from jax.sharding import Mesh
from jax.sharding import PartitionSpec as P

NEIG = 16
SIGN_STEPS = 6
ORDER = 13824
DEVICES = 128
ROWS = ORDER // DEVICES
CHIPS = DEVICES // 2
LANES = 128
HALF = CHIPS * LANES
TALL = 112
CHUNKS = 4
EPS = 1e-06
ROWS_GRP = ("rows_0", "rows_1", "grp_0", "grp_1")
CHIP_AXES = ("rows_0", "rows_1", "grp_0")
F32, BF16 = jnp.float32, jnp.bfloat16
HIGHEST = lax.Precision.HIGHEST
VMEM = pl.BlockSpec(memory_space=pltpu.VMEM)
LIMIT = 24 << 20


def split3(x):
    high = x.astype(BF16)
    rest = x - high.astype(F32)
    mid = rest.astype(BF16)
    return high, mid, (rest - mid.astype(F32)).astype(BF16)


def nt(left, right):
    return lax.dot_general(left, right, (((1,), (1,)), ((), ())), preferred_element_type=F32)


def nt_exact(left, right):
    return lax.dot_general(left, right, (((1,), (1,)), ((), ())), precision=HIGHEST, preferred_element_type=F32)


def dot_exact(left, right):
    return jnp.dot(left, right, precision=HIGHEST, preferred_element_type=F32)


def fold(parts):
    rows = (parts[32:48] + parts[16:32]) + parts[0:16]
    return (rows[:, 32:48] + rows[:, 16:32]) + rows[:, 0:16]


def fold_rows(product):
    rows = (product[2 * TALL :] + product[TALL : 2 * TALL]) + product[:TALL]
    wide = jnp.concatenate([rows, jnp.zeros((TALL, LANES - 3 * NEIG), F32)], axis=1)
    turned = jnp.concatenate([wide, jnp.zeros((LANES - TALL, LANES), F32)], axis=0).T
    image = (turned[32:48] + turned[16:32]) + turned[0:16]
    lane = lax.broadcasted_iota(jnp.int32, (NEIG, LANES), 1)
    return jnp.where(lane < ROWS, image, 0.0)


def prepare_kernel(h_ref, parts_ref):
    core = lax.axis_index("grp_1")
    step = pl.program_id(0)
    for block in range(2 * CHIPS // CHUNKS):
        chip, owner = divmod(block, 2)
        half = jnp.where(core == owner, 0, 1)
        x = h_ref[:, ROWS * block : ROWS * block + ROWS]
        x = jnp.concatenate([x, jnp.zeros((ROWS, LANES - ROWS), F32)], axis=1)
        lanes = pl.ds(pl.multiple_of(step * (HALF // CHUNKS) + LANES * chip, LANES), LANES)
        for number, part in enumerate(split3(x)):
            parts_ref[half, TALL * number : TALL * number + ROWS, lanes] = part


def prepare(hamiltonian):
    width = ORDER // CHUNKS
    return pl.pallas_call(
        prepare_kernel,
        grid=(CHUNKS,),
        out_shape=jax.ShapeDtypeStruct((2, 3 * TALL, HALF), BF16),
        in_specs=[pl.BlockSpec((ROWS, width), lambda i: (0, i))],
        out_specs=VMEM,
        compiler_params=pltpu.CompilerParams(vmem_limit_bytes=LIMIT),
        cost_estimate=pl.CostEstimate(flops=20 * ROWS * ORDER, bytes_accessed=10 * ROWS * ORDER, transcendentals=0),
        name="prepare",
    )(hamiltonian)


def take_parts(block_ref, parts_ref, half):
    for chip in range(CHIPS):
        for number, part in enumerate(split3(block_ref[chip, 0:NEIG])):
            parts_ref[half, NEIG * number : NEIG * (number + 1), LANES * chip : LANES * (chip + 1)] = part


def image_kernel(h_ref, own_ref, other_ref, image_ref, sent_ref, parts_ref):
    take_parts(own_ref, parts_ref, 0)
    product = nt(h_ref[0], parts_ref[0])
    take_parts(other_ref, parts_ref, 1)
    image = fold_rows(product + nt(h_ref[1], parts_ref[1]))
    image_ref[...] = image
    for chip in range(CHIPS):
        sent_ref[chip] = image


def previous_kernel(h_ref, own_ref, other_ref, c_ref, image_ref, parts_ref, gram_ref):
    take_parts(own_ref, parts_ref, 0)
    take_parts(other_ref, parts_ref, 1)
    image_ref[...] = fold_rows(nt(h_ref[0], parts_ref[0]) + nt(h_ref[1], parts_ref[1]))
    gram_ref[0] = fold(nt(c_ref[0], c_ref[0]) + nt(c_ref[1], c_ref[1]))
    gram_ref[1] = fold(nt(parts_ref[0], c_ref[0]) + nt(parts_ref[1], c_ref[1]))
    gram_ref[2] = fold(nt(parts_ref[0], parts_ref[0]) + nt(parts_ref[1], parts_ref[1]))


def search_kernel(
    h_ref, own_ref, other_ref, p_own_ref, p_other_ref, c_ref, pvec_ref, pimage_ref,
    search_ref, rms_ref, cross_ref, sent_ref, i_ref, s_ref, resid_ref,
):
    chip_here = (lax.axis_index("rows_0") * 4 + lax.axis_index("rows_1")) * 4 + lax.axis_index("grp_0")
    take_parts(own_ref, i_ref, 0)
    take_parts(other_ref, i_ref, 1)
    cross_t = fold(nt(i_ref[0], c_ref[0]) + nt(i_ref[1], c_ref[1]))
    cross_ref[...] = cross_t
    ritz_t = cross_t / ORDER
    stacked = jnp.concatenate(split3(ritz_t), axis=0)
    stacked = jnp.concatenate([stacked, stacked, stacked], axis=1)
    square = jnp.zeros((NEIG, LANES), F32)
    for half, ref in ((0, own_ref), (1, other_ref)):
        moved = jnp.dot(stacked, c_ref[half], preferred_element_type=F32)
        moved = (moved[32:48] + moved[16:32]) + moved[0:16]
        part = jnp.zeros((NEIG, LANES), F32)
        for chip in range(CHIPS):
            lanes = slice(LANES * chip, LANES * (chip + 1))
            resid = ref[chip] - moved[:, lanes]
            resid_ref[half, :, lanes] = resid
            part = part + resid * resid
        square = square + part
    rms = jnp.sqrt(jnp.sum(square, axis=1, keepdims=True) / ORDER + EPS)
    rms_ref[...] = rms
    row = lax.broadcasted_iota(jnp.int32, (NEIG, NEIG), 0)
    column = lax.broadcasted_iota(jnp.int32, (NEIG, NEIG), 1)
    value = jnp.sum(jnp.where(row == column, ritz_t, 0.0), axis=1, keepdims=True)
    value = jnp.broadcast_to(value, (NEIG, LANES))
    rms = jnp.broadcast_to(rms, (NEIG, LANES))

    def scaled(resid, diag):
        diag = jnp.concatenate([diag, diag], axis=0)
        return resid / (jnp.maximum(jnp.abs(diag - value), 1.0) * rms)

    product = jnp.zeros((3 * TALL, 3 * NEIG), F32)
    for half, ref in ((0, p_own_ref), (1, p_other_ref)):
        for chip in range(CHIPS):
            lanes = slice(LANES * chip, LANES * (chip + 1))
            search = scaled(resid_ref[half, :, lanes], ref[chip, NEIG : NEIG + 8])
            for number, part in enumerate(split3(search)):
                s_ref[half, NEIG * number : NEIG * (number + 1), lanes] = part
        product = product + nt(h_ref[half], s_ref[half])
    simage = fold_rows(product)
    lanes = pl.ds(pl.multiple_of(chip_here * LANES, LANES), LANES)
    search = scaled(resid_ref[0, :, lanes], p_own_ref[chip_here, NEIG : NEIG + 8])
    search_ref[...] = search
    pvec = pvec_ref[...]
    terms = jnp.concatenate(
        [nt_exact(simage, search), nt_exact(simage, pvec), nt_exact(pimage_ref[...], pvec), jnp.zeros((NEIG, NEIG), F32)],
        axis=1,
    )
    packed = jnp.concatenate([terms[0:8], terms[8:16]], axis=1)
    for chip in range(CHIPS):
        sent_ref[chip] = packed


def factor_kernel(s_ref, c_ref, p_ref, i_ref, gram_ref, cross_ref, inverse_ref, stiff_ref):
    def gram(left, right):
        return fold(nt(left[0], right[0]) + nt(left[1], right[1]))

    empty = jnp.zeros((NEIG, NEIG), F32)
    cc, pc, pp = gram_ref[0], gram_ref[1], gram_ref[2]
    sc, ss, ps = gram(s_ref, c_ref), gram(s_ref, s_ref), gram(p_ref, s_ref)
    low = jnp.concatenate(
        [
            jnp.concatenate([0.5 * cc, empty, empty], axis=1),
            jnp.concatenate([sc, 0.5 * ss, empty], axis=1),
            jnp.concatenate([pc, ps, 0.5 * pp], axis=1),
        ],
        axis=0,
    )
    mass = low + low.T
    low = jnp.concatenate(
        [
            jnp.concatenate([0.5 * cross_ref[...], empty, empty], axis=1),
            jnp.concatenate([gram(s_ref, i_ref), empty, empty], axis=1),
            jnp.concatenate([gram(p_ref, i_ref), empty, empty], axis=1),
        ],
        axis=0,
    )
    stiff_ref[...] = low + low.T
    size = 3 * NEIG
    row = lax.broadcasted_iota(jnp.int32, (size, size), 0)
    column = lax.broadcasted_iota(jnp.int32, (size, size), 1)
    identity = jnp.where(row == column, 1.0, 0.0).astype(F32)
    work = jnp.concatenate([mass, identity], axis=1)
    below = lax.broadcasted_iota(jnp.int32, (size, 1), 0)
    for k in range(size):
        factor = jnp.where(below > k, work[:, k : k + 1] / work[k : k + 1, k : k + 1], 0.0)
        work = work - factor * work[k : k + 1, :]
    pivots = jnp.sum(work[:, :size] * identity, axis=1, keepdims=True)
    inverse_ref[...] = work[:, size:] / jnp.sqrt(pivots)


def finish_kernel(inverse_ref, stiff_ref, own_ref, other_ref, c_ref, s_ref, p_ref, current_ref, previous_ref):
    size = 3 * NEIG
    total = own_ref[0] + other_ref[0]
    for chip in range(1, CHIPS):
        total = total + (own_ref[chip] + other_ref[chip])
    terms = jnp.concatenate([total[:, 0 : 3 * NEIG], total[:, 4 * NEIG : 7 * NEIG]], axis=0)
    ss, sp, pp = terms[:, 0:16], terms[:, 16:32], terms[:, 32:48]
    empty = jnp.zeros((NEIG, NEIG), F32)
    up = jnp.concatenate(
        [
            jnp.zeros((NEIG, size), F32),
            jnp.concatenate([empty, 0.5 * ss, sp], axis=1),
            jnp.concatenate([empty, empty, 0.5 * pp], axis=1),
        ],
        axis=0,
    )
    stiff = stiff_ref[...] + (up + up.T)
    inverse = inverse_ref[...]
    reduced = nt_exact(dot_exact(inverse, stiff), inverse)
    row = lax.broadcasted_iota(jnp.int32, (size, size), 0)
    column = lax.broadcasted_iota(jnp.int32, (size, size), 1)
    identity = jnp.where(row == column, 1.0, 0.0).astype(F32)
    diagonal = jnp.sum(reduced * identity, axis=1, keepdims=True)
    level = jnp.max(diagonal[:NEIG], axis=0, keepdims=True)
    signed = level * identity - reduced
    norm = jnp.sqrt(jnp.sum(jnp.sum(signed * signed, axis=1, keepdims=True), axis=0, keepdims=True))
    signed = signed / norm
    for _ in range(SIGN_STEPS):
        signed = 1.5 * signed - 0.5 * dot_exact(signed, dot_exact(signed, signed))
    projector = 0.5 * (identity + signed)
    wanted = jnp.where(lax.broadcasted_iota(jnp.int32, (size, size), 1) < NEIG, projector, 0.0)
    tn = (((0,), (0,)), ((), ()))
    coeffs_t = lax.dot_general(wanted, inverse, tn, precision=HIGHEST, preferred_element_type=F32)[0:NEIG]
    coeffs_t = coeffs_t * math.sqrt(ORDER)
    basis = jnp.concatenate([c_ref[...], s_ref[...], p_ref[...]], axis=0)
    current_ref[...] = dot_exact(coeffs_t, basis)[:, :ROWS]
    lane = lax.broadcasted_iota(jnp.int32, (NEIG, size), 1)
    previous_ref[...] = dot_exact(jnp.where(lane < NEIG, 0.0, coeffs_t), basis)[:, :ROWS]


def kernel_call(body, outs, args, flops, name, scratch=()):
    return pl.pallas_call(
        body,
        out_shape=[jax.ShapeDtypeStruct(shape, kind) for shape, kind in outs],
        in_specs=[VMEM] * len(args),
        out_specs=[VMEM] * len(outs),
        scratch_shapes=scratch,
        compiler_params=pltpu.CompilerParams(vmem_limit_bytes=LIMIT),
        cost_estimate=pl.CostEstimate(flops=flops, bytes_accessed=4 << 20, transcendentals=0),
        name=name,
    )(*args)


def to_chips(x):
    return lax.all_to_all(x, CHIP_AXES, 0, 0, tiled=True)


def to_core(x):
    return lax.ppermute(x, "grp_1", [(0, 1), (1, 0)])


def body(hamiltonian, current, previous):
    device = lax.axis_index(ROWS_GRP)
    cvec = jnp.pad(current.T, ((0, 0), (0, LANES - ROWS)))
    c_own = to_chips(jnp.broadcast_to(cvec[None], (CHIPS, NEIG, LANES)))
    own_block = lax.dynamic_slice_in_dim(hamiltonian, device * ROWS, ROWS, 1)
    diag = jnp.sum(own_block * jnp.eye(ROWS, dtype=F32), axis=0)
    pvec = jnp.pad(previous.T, ((0, 0), (0, LANES - ROWS)))
    diag_rows = jnp.broadcast_to(jnp.pad(diag, (0, LANES - ROWS))[None], (8, LANES))
    with_diag = jnp.concatenate([pvec, diag_rows], axis=0)
    p_own = to_chips(jnp.broadcast_to(with_diag[None], (CHIPS, NEIG + 8, LANES)))
    h_parts = prepare(hamiltonian)
    c_other = to_core(c_own)
    block, parts = ((NEIG, LANES), F32), ((2, 3 * NEIG, HALF), BF16)
    image, sent, c_parts = kernel_call(
        image_kernel, [block, ((CHIPS, NEIG, LANES), F32), parts], (h_parts, c_own, c_other), 6 << 30, "image"
    )
    i_own = to_chips(sent)
    p_other = to_core(p_own)
    p_image, p_parts, grams = kernel_call(
        previous_kernel,
        [block, parts, ((3, NEIG, NEIG), F32)],
        (h_parts, p_own, p_other, c_parts),
        6 << 30,
        "previous",
    )
    i_other = to_core(i_own)
    search, rms, cross, sent, i_parts, s_parts = kernel_call(
        search_kernel,
        [block, ((NEIG, 1), F32), ((NEIG, NEIG), F32), ((CHIPS, 8, LANES), F32), parts, parts],
        (h_parts, i_own, i_other, p_own, p_other, c_parts, pvec, p_image),
        6 << 30,
        "search",
        scratch=[pltpu.VMEM((2, NEIG, HALF), F32)],
    )
    r_own = to_chips(sent)
    square = ((3 * NEIG, 3 * NEIG), F32)
    inverse, stiff = kernel_call(
        factor_kernel, [square, square], (s_parts, c_parts, p_parts, i_parts, grams, cross), 6 << 30, "factor"
    )
    r_other = to_core(r_own)
    new_current, new_previous = kernel_call(
        finish_kernel,
        [((NEIG, ROWS), F32)] * 2,
        (inverse, stiff, r_own, r_other, cvec, search, pvec),
        1 << 28,
        "finish",
    )
    return new_current.T, new_previous.T, rms.reshape(NEIG)


def solution(mesh):
    finer = Mesh(mesh.devices.reshape(4, 4, 4, 2), ROWS_GRP)
    return jax.shard_map(
        body,
        mesh=finer,
        in_specs=(P(ROWS_GRP, None), P(ROWS_GRP, None), P(ROWS_GRP, None)),
        out_specs=(P(ROWS_GRP, None), P(ROWS_GRP, None), P()),
        check_vma=False,
    )
```

time: 149 us -> 118 us (0.79)
  waiting for transfers between devices: 43.6 us -> 11.4 us
  Pallas kernels: 0 us -> 31.1 us
  matrix products: 23.5 us -> 0 us
  other arithmetic: 13.8 us -> 1.64 us
  blocking collectives: 26.1 us -> 33.2 us
    all_to_all x4 -> x2, waiting for transfers between devices: 43.6 us -> 11.4 us  [to_chips(): return lax.all_to_all(x, CHIP_AXES, 0, 0, tiled=True)]
    pallas_call x0 -> x6, Pallas kernels: none -> 31.1 us  [the longest x5 26.7 us: kernel_call(): pl.pallas_call(body, out_shape=[jax.ShapeDtypeStruct(shape, kind) for sha...]
    dot_general x22 -> x0, matrix products: 22.8 us -> none  [mat_mul(): jnp.dot(left, right, precision=highest, preferred_element_type=jnp.float32)]
    unnamed x6 -> x8, local copies, waits for them, and re-layouts: 0.03 us -> 11.1 us
    another operation x6 -> x0, other arithmetic: 9.39 us -> none  [the longest x4 5.06 us: ritz_update(): lower = jnp.linalg.cholesky(mass)]
    ppermute x0 -> x4, starting transfers between devices: none -> 8.83 us  [to_core(): return lax.ppermute(x, 'grp_1', [(0, 1), (1, 0)])]
    all_to_all x4 -> x2, starting transfers between devices: 24.9 us -> 16.6 us  [to_chips(): return lax.all_to_all(x, CHIP_AXES, 0, 0, tiled=True)]
    all_to_all x4 -> x2, blocking collectives: 26.1 us -> 33.2 us  [to_chips(): return lax.all_to_all(x, CHIP_AXES, 0, 0, tiled=True)]
  transfers between devices with their start and end apart: 4 -> 6, of which waited for: 4 -> 2; matrix products, arithmetic and copies ran while one was open for 2% -> 1% of each run, Pallas kernels for 0% -> 18%
where the time goes in v1:
time: 118 us; the launch traced here: 117 us
  blocking collectives  33.2 us (28%)
  Pallas kernels  31.1 us (26%)
  starting transfers between devices  25.4 us (22%)
  local copies, waits for them, and re-layouts  13.5 us (11%)
  waiting for transfers between devices  11.4 us (10%)
  other arithmetic  1.64 us (1%)
    all_to_all x2, blocking collectives, to_chips(): return lax.all_to_all(x, CHIP_AXES, 0, 0, tiled=True)  33.2 us
    pallas_call x5, Pallas kernels, kernel_call(): pl.pallas_call(body, out_shape=[jax.ShapeDtypeStruct(shape, kind) for sha...  26.7 us
    all_to_all x2, starting transfers between devices, to_chips(): return lax.all_to_all(x, CHIP_AXES, 0, 0, tiled=True)  16.6 us
    all_to_all x2, waiting for transfers between devices, to_chips(): return lax.all_to_all(x, CHIP_AXES, 0, 0, tiled=True)  11.4 us
    unnamed x8, local copies, waits for them, and re-layouts  11.1 us
    ppermute x4, starting transfers between devices, to_core(): return lax.ppermute(x, 'grp_1', [(0, 1), (1, 0)])  8.83 us
    pallas_call x1, Pallas kernels, prepare(): pl.pallas_call(prepare_kernel, grid=(CHUNKS,), out_shape=jax.ShapeDtypeSt...  4.43 us
  transfers between devices with their start and end apart: 6, of which 2 were waited for; matrix products, arithmetic and copies ran while one was open for 1% of the time, Pallas kernels for 18%

profile of v1, /device:TPU:1, one launch (start us, length us, event | category | flops | bytes accessed | tf_op | source)
XLA Modules:
  0.0 117.0 jit_solution(13447341004944014352)
XLA Ops:
  0.6 0.7 pad.11.c_ref
  1.3 0.8 broadcast_in_dim.6
  2.2 12.0 %all-to-all-start = ((f32[64,16,128]{2,1,0:T(8,128)}), f32[64,16,128]{2,1,0:T(8,128)S(1)}, u32[]{:S(2)}, u32[]{:S(2)}) async-start(f32[64,16,128]{2,1,0:T(8,128)} %broadcast_in_dim.6), calls=%async_computation | async-start | bytes 1048576 | tf_op jit(solution)/shard_map/all_to_all | solution.py:264
  14.2 1.0 select_reduce_fusion
  15.2 11.0 %all-to-all-done.own_ref = f32[64,16,128]{2,1,0:T(8,128)S(1)} async-done(((f32[64,16,128]{2,1,0:T(8,128)}), f32[64,16,128]{2,1,0:T(8,128)S(1)}, u32[]{:S(2)}, u32[]{:S(2)}) %all-to-all-start) | async-done | bytes 524320 | tf_op jit(solution)/shard_map/all_to_all | solution.py:264
  26.2 0.9 broadcast_in_dim.8
  27.1 4.6 %all-to-all-start.2 = ((f32[64,24,128]{2,1,0:T(8,128)}), f32[64,24,128]{2,1,0:T(8,128)S(1)}, u32[]{:S(2)}, u32[]{:S(2)}) async-start(f32[64,24,128]{2,1,0:T(8,128)} %broadcast_in_dim.8), calls=%async_computation.2 | async-start | bytes 1572864 | tf_op jit(solution)/shard_map/all_to_all | solution.py:264
  31.8 2.4 %collective-permute-start = (f32[64,16,128]{2,1,0:T(8,128)S(1)}, f32[64,16,128]{2,1,0:T(8,128)S(1)}, u32[]{:S(2)}, u32[]{:S(2)}) collective-permute-start(f32[64,16,128]{2,1,0:T(8,128)S(1)} %all-to-all-done.own_ref), channel_id=1, source_target_pairs={{0,1},{1,0},{2,3},{3,2},{4,5},{5,4},{6,7},{7,6},{8,9},{9,8},{10,11... | collective-permute-start | bytes 1572872 | tf_op jit(solution)/shard_map/ppermute | solution.py:268
  34.2 2.8 %copy-done.2 = f32[108,13824]{1,0:T(8,128)S(1)} copy-done((f32[108,13824]{1,0:T(8,128)S(1)}, f32[108,13824]{1,0:T(8,128)}, u32[]{:S(2)}) %copy-start.2) | copy-done | bytes 5971992
  37.0 4.4 %prepare.1.h_ref = bf16[2,336,8192]{2,1,0:T(8,128)(2,1)S(1)} custom-call(f32[108,13824]{1,0:T(8,128)S(1)} %copy-done.2), custom_call_target="tpu_custom_call" | custom-call | flops 29859840 | bytes 14929920 | tf_op jit(solution)/shard_map/prepare/pallas_call | solution.py:78
  41.4 4.2 %copy-done = bf16[2,336,8192]{2,1,0:T(8,128)(2,1)} copy-done((bf16[2,336,8192]{2,1,0:T(8,128)(2,1)}, bf16[2,336,8192]{2,1,0:T(8,128)(2,1)S(1)}, u32[]{:S(2)}) %copy-start) | copy-done | bytes 11010072
  45.6 0.4 all-to-all-done.2.own_ref.p_own_ref
  46.0 2.9 %collective-permute-start.2 = (f32[64,24,128]{2,1,0:T(8,128)S(1)}, f32[64,24,128]{2,1,0:T(8,128)S(1)}, u32[]{:S(2)}, u32[]{:S(2)}) collective-permute-start(f32[64,24,128]{2,1,0:T(8,128)S(1)} %all-to-all-done.2.own_ref.p_own_ref), channel_id=1, source_target_pairs={{0,1},{1,0},{2,3},{3,2},{4,5},{5,4},{6,7},{7,6},{8,9},{9,8},{10,11... | collective-permute-start | bytes 2359304 | tf_op jit(solution)/shard_map/ppermute | solution.py:268
  48.9 4.1 %copy-done.1 = bf16[2,336,8192]{2,1,0:T(8,128)(2,1)S(1)} copy-done((bf16[2,336,8192]{2,1,0:T(8,128)(2,1)S(1)}, bf16[2,336,8192]{2,1,0:T(8,128)(2,1)}, u32[]{:S(2)}) %copy-start.1) | copy-done | bytes 11010072
  53.1 3.9 %image.1 = (f32[16,128]{1,0:T(8,128)}, f32[64,16,128]{2,1,0:T(8,128)S(1)}, bf16[2,48,8192]{2,1,0:T(8,128)(2,1)S(1)}) custom-call(bf16[2,336,8192]{2,1,0:T(8,128)(2,1)S(1)} %copy-done.1, f32[64,16,128]{2,1,0:T(8,128)S(1)} %all-to-all-done.own_ref, f32[64,16,128]{2,1,0:T(8,128)S(1)} %collective-permute-done.other_ref), custom_call_target="tpu_custom_call" | custom-call | flops 6442450944 | bytes 4194304 | tf_op jit(solution)/shard_map/image/pallas_call | solution.py:251
  56.9 18.9 %all_to_all.20.own_ref = f32[64,16,128]{2,1,0:T(8,128)S(1)} all-to-all(f32[64,16,128]{2,1,0:T(8,128)S(1)} %get-tuple-element.18), channel_id=1, replica_groups=mesh['rows_0'=4,'rows_1'=4,'grp_0'=4,'grp_1'=2] {'rows_0','rows_1','grp_0'}, dimensions={0} | all-to-all | bytes 1048576 | tf_op jit(solution)/shard_map/all_to_all | solution.py:264
  75.8 2.0 %collective-permute-start.1 = (f32[64,16,128]{2,1,0:T(8,128)S(1)}, f32[64,16,128]{2,1,0:T(8,128)S(1)}, u32[]{:S(2)}, u32[]{:S(2)}) collective-permute-start(f32[64,16,128]{2,1,0:T(8,128)S(1)} %all_to_all.20.own_ref), channel_id=1, source_target_pairs={{0,1},{1,0},{2,3},{3,2},{4,5},{5,4},{6,7},{7,6},{8,9},{9,8},{10,11... | collective-permute-start | bytes 1572872 | tf_op jit(solution)/shard_map/ppermute | solution.py:268
  77.8 6.1 %previous.1 = (f32[16,128]{1,0:T(8,128)S(1)}, bf16[2,48,8192]{2,1,0:T(8,128)(2,1)S(1)}, f32[3,16,16]{2,1,0:T(8,128)S(1)}) custom-call(bf16[2,336,8192]{2,1,0:T(8,128)(2,1)S(1)} %copy-done.1, f32[64,24,128]{2,1,0:T(8,128)S(1)} %all-to-all-done.2.own_ref.p_own_ref, f32[64,24,128]{2,1,0:T(8,128)S(1)} %collective-permute-done.2.other_ref.p_other_ref, ...), custom_call_target="tpu_custom_call" | custom-call | flops 6442450944 | bytes 4194304 | tf_op jit(solution)/shard_map/previous/pallas_call | solution.py:251
  84.0 6.4 %search.1 = (f32[16,128]{1,0:T(8,128)S(1)}, f32[16,1]{1,0:T(8,128)S(1)}, f32[16,16]{1,0:T(8,128)S(1)}, f32[64,8,128]{2,1,0:T(8,128)S(1)}, bf16[2,48,8192]{2,1,0:...) custom-call(bf16[2,336,8192]{2,1,0:T(8,128)(2,1)S(1)} %copy-done.1, f32[64,16,128]{2,1,0:T(8,128)S(1)} %all_to_all.20.own_ref, ...), custom_call_target="tpu_custom_call" | custom-call | flops 6442450944 | bytes 4194304 | tf_op jit(solution)/shard_map/search/pallas_call | solution.py:251
  90.4 14.3 %all_to_all.21.own_ref = f32[64,8,128]{2,1,0:T(8,128)S(1)} all-to-all(f32[64,8,128]{2,1,0:T(8,128)S(1)} %get-tuple-element.28), channel_id=1, replica_groups=mesh['rows_0'=4,'rows_1'=4,'grp_0'=4,'grp_1'=2] {'rows_0','rows_1','grp_0'}, dimensions={0} | all-to-all | bytes 524288 | tf_op jit(solution)/shard_map/all_to_all | solution.py:264
  104.7 1.4 %collective-permute-start.3 = (f32[64,8,128]{2,1,0:T(8,128)S(1)}, f32[64,8,128]{2,1,0:T(8,128)S(1)}, u32[]{:S(2)}, u32[]{:S(2)}) collective-permute-start(f32[64,8,128]{2,1,0:T(8,128)S(1)} %all_to_all.21.own_ref), channel_id=1, source_target_pairs={{0,1},{1,0},{2,3},{3,2},{4,5},{5,4},{6,7},{7,6},{8,9},{9,8},{10,11... | collective-permute-start | bytes 786440 | tf_op jit(solution)/shard_map/ppermute | solution.py:268
  106.1 6.5 %factor.1 = (f32[48,48]{1,0:T(8,128)S(1)}, f32[48,48]{1,0:T(8,128)S(1)}) custom-call(bf16[2,48,8192]{2,1,0:T(8,128)(2,1)S(1)} %get-tuple-element.21.s_ref, bf16[2,48,8192]{2,1,0:T(8,128)(2,1)S(1)} %get-tuple-element.19.c_ref, bf16[2,48,8192]{2,1,0:T(8,128)(2,1)S(1)} %get-tuple-element.22.p_ref, bf16[2,48,8192]{2,1,0:T(8,128)(2,1)S(1)} %get-tuple-element.23.i_ref, ...), custom_call_target="tpu_custom_call" | custom-call | flops 6442450944 | bytes 4194304 | tf_op jit(solution)/shard_map/factor/pallas_call | solution.py:251
  112.6 0.6 reduce
  113.2 3.8 %finish.1 = (f32[16,108]{1,0:T(8,128)}, f32[16,108]{1,0:T(8,128)}) custom-call(f32[48,48]{1,0:T(8,128)S(1)} %get-tuple-element.26.inverse_ref, f32[48,48]{1,0:T(8,128)S(1)} %get-tuple-element.27.stiff_ref, f32[64,8,128]{2,1,0:T(8,128)S(1)} %all_to_all.21.own_ref, f32[64,8,128]{2,1,0:T(8,128)S(1)} %collective-permute-done.3.other_ref, ...), custom_call_target="tpu_custom_call" | custom-call | flops 268435456 | bytes 4194304 | tf_op jit(solution)/shard_map/finish/pallas_call | solution.py:251
  (13 shorter events, 0.1 us)
Async XLA Ops:
  0.6 14.5 %copy-start.3 = (f32[108,16]{0,1:T(8,128)S(1)}, f32[108,16]{0,1:T(8,128)}, u32[]{:S(2)}) copy-start(f32[108,16]{0,1:T(8,128)} %param.5) | copy-start | bytes 20740
  2.2 24.0 %all-to-all-start = ((f32[64,16,128]{2,1,0:T(8,128)}), f32[64,16,128]{2,1,0:T(8,128)S(1)}, u32[]{:S(2)}, u32[]{:S(2)}) async-start(f32[64,16,128]{2,1,0:T(8,128)} %broadcast_in_dim.6), calls=%async_computation | async-start | bytes 1048576 | tf_op jit(solution)/shard_map/all_to_all | solution.py:264
  27.1 18.8 %all-to-all-start.2 = ((f32[64,24,128]{2,1,0:T(8,128)}), f32[64,24,128]{2,1,0:T(8,128)S(1)}, u32[]{:S(2)}, u32[]{:S(2)}) async-start(f32[64,24,128]{2,1,0:T(8,128)} %broadcast_in_dim.8), calls=%async_computation.2 | async-start | bytes 1572864 | tf_op jit(solution)/shard_map/all_to_all | solution.py:264
  31.8 17.1 %collective-permute-start = (f32[64,16,128]{2,1,0:T(8,128)S(1)}, f32[64,16,128]{2,1,0:T(8,128)S(1)}, u32[]{:S(2)}, u32[]{:S(2)}) collective-permute-start(f32[64,16,128]{2,1,0:T(8,128)S(1)} %all-to-all-done.own_ref), channel_id=1, source_target_pairs={{0,1},{1,0},{2,3},{3,2},{4,5},{5,4},{6,7},{7,6},{8,9},{9,8},{10,11... | collective-permute-start | bytes 1572872 | tf_op jit(solution)/shard_map/ppermute | solution.py:268
  34.2 2.8 %copy-start.2 = (f32[108,13824]{1,0:T(8,128)S(1)}, f32[108,13824]{1,0:T(8,128)}, u32[]{:S(2)}) copy-start(f32[108,13824]{1,0:T(8,128)} %h_ref.1) | copy-start | bytes 17915908
  41.4 4.2 %copy-start = (bf16[2,336,8192]{2,1,0:T(8,128)(2,1)}, bf16[2,336,8192]{2,1,0:T(8,128)(2,1)S(1)}, u32[]{:S(2)}) copy-start(bf16[2,336,8192]{2,1,0:T(8,128)(2,1)S(1)} %prepare.1.h_ref) | copy-start | bytes 33030148
  46.0 31.9 %collective-permute-start.2 = (f32[64,24,128]{2,1,0:T(8,128)S(1)}, f32[64,24,128]{2,1,0:T(8,128)S(1)}, u32[]{:S(2)}, u32[]{:S(2)}) collective-permute-start(f32[64,24,128]{2,1,0:T(8,128)S(1)} %all-to-all-done.2.own_ref.p_own_ref), channel_id=1, source_target_pairs={{0,1},{1,0},{2,3},{3,2},{4,5},{5,4},{6,7},{7,6},{8,9},{9,8},{10,11... | collective-permute-start | bytes 2359304 | tf_op jit(solution)/shard_map/ppermute | solution.py:268
  48.9 4.1 %copy-start.1 = (bf16[2,336,8192]{2,1,0:T(8,128)(2,1)S(1)}, bf16[2,336,8192]{2,1,0:T(8,128)(2,1)}, u32[]{:S(2)}) copy-start(bf16[2,336,8192]{2,1,0:T(8,128)(2,1)} %copy-done) | copy-start | bytes 33030148
  75.8 8.1 %collective-permute-start.1 = (f32[64,16,128]{2,1,0:T(8,128)S(1)}, f32[64,16,128]{2,1,0:T(8,128)S(1)}, u32[]{:S(2)}, u32[]{:S(2)}) collective-permute-start(f32[64,16,128]{2,1,0:T(8,128)S(1)} %all_to_all.20.own_ref), channel_id=1, source_target_pairs={{0,1},{1,0},{2,3},{3,2},{4,5},{5,4},{6,7},{7,6},{8,9},{9,8},{10,11... | collective-permute-start | bytes 1572872 | tf_op jit(solution)/shard_map/ppermute | solution.py:268
  104.7 8.6 %collective-permute-start.3 = (f32[64,8,128]{2,1,0:T(8,128)S(1)}, f32[64,8,128]{2,1,0:T(8,128)S(1)}, u32[]{:S(2)}, u32[]{:S(2)}) collective-permute-start(f32[64,8,128]{2,1,0:T(8,128)S(1)} %all_to_all.21.own_ref), channel_id=1, source_target_pairs={{0,1},{1,0},{2,3},{3,2},{4,5},{5,4},{6,7},{7,6},{8,9},{9,8},{10,11... | collective-permute-start | bytes 786440 | tf_op jit(solution)/shard_map/ppermute | solution.py:268

commit v2 on v1

v2 whole, which is shorter than its diff:
```python
import math

import jax
import jax.numpy as jnp
from jax import lax
from jax.experimental import pallas as pl
from jax.experimental.pallas import tpu as pltpu
from jax.sharding import Mesh
from jax.sharding import PartitionSpec as P

NEIG = 16
SIGN_STEPS = 6
ORDER = 13824
DEVICES = 128
ROWS = ORDER // DEVICES
CHIPS = DEVICES // 2
LANES = 128
HALF = CHIPS * LANES
TALL = 112
CHUNKS = 4
EPS = 1e-06
ROWS_GRP = ("rows_0", "rows_1", "grp_0", "grp_1")
CHIP_AXES = ("rows_0", "rows_1", "grp_0")
F32, BF16 = jnp.float32, jnp.bfloat16
HIGHEST = lax.Precision.HIGHEST
VMEM = pl.BlockSpec(memory_space=pltpu.VMEM)
HBM = pl.BlockSpec(memory_space=pltpu.HBM)
LIMIT = 48 << 20
PARTS = 2
STACK = PARTS * NEIG
SPARE = ROWS


def split(x):
    high = x.astype(BF16)
    return high, (x - high.astype(F32)).astype(BF16)


def split3(x):
    high = x.astype(BF16)
    rest = x - high.astype(F32)
    mid = rest.astype(BF16)
    return high, mid, (rest - mid.astype(F32)).astype(BF16)


def nt(left, right):
    return lax.dot_general(left, right, (((1,), (1,)), ((), ())), preferred_element_type=F32)


def nt_exact(left, right):
    return lax.dot_general(left, right, (((1,), (1,)), ((), ())), precision=HIGHEST, preferred_element_type=F32)


def dot_exact(left, right):
    return jnp.dot(left, right, precision=HIGHEST, preferred_element_type=F32)


def fold(parts):
    rows = parts[16:32] + parts[0:16]
    return rows[:, 16:32] + rows[:, 0:16]


def fold_rows(product):
    rows = product[TALL:] + product[:TALL]
    wide = jnp.concatenate([rows, jnp.zeros((TALL, LANES - STACK), F32)], axis=1)
    turned = jnp.concatenate([wide, jnp.zeros((LANES - TALL, LANES), F32)], axis=0).T
    return real_lanes(turned[16:32] + turned[0:16])


def real_lanes(tile):
    lane = lax.broadcasted_iota(jnp.int32, tile.shape, 1)
    return jnp.where(lane < ROWS, tile, 0.0)


def padded(tile):
    return jnp.concatenate([tile, jnp.zeros((tile.shape[0], LANES - ROWS), F32)], axis=1)


def prepare_kernel(h_ref, parts_ref):
    core = lax.axis_index("grp_1")
    for block in range(2 * CHIPS // CHUNKS):
        chip, owner = divmod(block, 2)
        half = jnp.where(core == owner, 0, 1)
        x = padded(h_ref[:, ROWS * block : ROWS * block + ROWS])
        for number, part in enumerate(split(x)):
            parts_ref[half, TALL * number : TALL * number + ROWS, LANES * chip : LANES * (chip + 1)] = part


def prepare(hamiltonian):
    width, out = ORDER // CHUNKS, HALF // CHUNKS
    return pl.pallas_call(
        prepare_kernel,
        grid=(CHUNKS,),
        out_shape=jax.ShapeDtypeStruct((2, PARTS * TALL, HALF), BF16),
        in_specs=[pl.BlockSpec((ROWS, width), lambda i: (0, i))],
        out_specs=pl.BlockSpec((2, PARTS * TALL, out), lambda i: (0, 0, i)),
        compiler_params=pltpu.CompilerParams(vmem_limit_bytes=58 << 20),
        cost_estimate=pl.CostEstimate(flops=20 * ROWS * ORDER, bytes_accessed=10 * ROWS * ORDER, transcendentals=0),
        name="prepare",
    )(hamiltonian)


def take_parts(tile_of, parts_ref):
    for chip in range(CHIPS):
        for number, part in enumerate(split(tile_of(chip))):
            parts_ref[NEIG * number : NEIG * (number + 1), LANES * chip : LANES * (chip + 1)] = part


def image_own_kernel(h_ref, own_ref, product_ref, own_out, h_vmem, parts, sems):
    copy = pltpu.make_async_copy(h_ref.at[0], h_vmem, sems.at[0])
    copy.start()
    keep = pltpu.make_async_copy(own_ref, own_out, sems.at[1])
    keep.start()
    take_parts(lambda chip: padded(own_ref[chip, 0:NEIG]), parts)
    copy.wait()
    product_ref[...] = nt(h_vmem[...], parts[...])
    keep.wait()


def image_other_kernel(h_ref, other_ref, product_ref, tile_ref, image_ref, sent_ref, other_out, h_vmem, parts, sems):
    copy = pltpu.make_async_copy(h_ref.at[1], h_vmem, sems.at[0])
    copy.start()
    keep = pltpu.make_async_copy(other_ref, other_out, sems.at[1])
    keep.start()
    take_parts(lambda chip: padded(other_ref[chip, 0:NEIG]), parts)
    copy.wait()
    image = fold_rows(product_ref[...] + nt(h_vmem[...], parts[...]))
    image_ref[...] = image
    sent = image + tile_ref[...]
    for chip in range(CHIPS):
        sent_ref[chip] = sent
    keep.wait()


def previous_kernel(h_ref, own_ref, other_ref, image_ref, c_out, p_out, gram_ref, h_vmem, c_ref, p_ref, sems):
    copy = pltpu.make_async_copy(h_ref, h_vmem, sems.at[0])
    copy.start()
    for half, ref in ((0, own_ref), (1, other_ref)):
        take_parts(lambda chip: padded(ref[chip, 0:NEIG]), c_ref.at[half])
        take_parts(lambda chip: padded(ref[chip, NEIG : 2 * NEIG]), p_ref.at[half])
    out_c = pltpu.make_async_copy(c_ref, c_out, sems.at[1])
    out_p = pltpu.make_async_copy(p_ref, p_out, sems.at[2])
    out_c.start()
    out_p.start()
    gram_ref[0] = fold(nt(c_ref[0], c_ref[0]) + nt(c_ref[1], c_ref[1]))
    gram_ref[1] = fold(nt(p_ref[0], c_ref[0]) + nt(p_ref[1], c_ref[1]))
    gram_ref[2] = fold(nt(p_ref[0], p_ref[0]) + nt(p_ref[1], p_ref[1]))
    copy.wait()
    image_ref[...] = fold_rows(nt(h_vmem[0], p_ref[0]) + nt(h_vmem[1], p_ref[1]))
    out_c.wait()
    out_p.wait()


def diagonal_of(tile):
    row = lax.broadcasted_iota(jnp.int32, (NEIG, LANES), 0)
    lane = lax.broadcasted_iota(jnp.int32, (NEIG, LANES), 1)
    spread = jnp.take_along_axis(tile, SPARE + lane // NEIG, axis=1)
    return jnp.sum(jnp.where(lane % NEIG == row, spread, 0.0), axis=0, keepdims=True)


def search_kernel(
    h_ref, own_ref, other_ref, c_hbm, cvec_ref, pvec_ref, pimage_ref, image_ref, tile_ref,
    search_ref, rms_ref, cross_ref, sent_ref, s_out, i_out,
    h_vmem, c_ref, i_ref, s_ref, resid_ref, sems,
):
    copy_c = pltpu.make_async_copy(c_hbm, c_ref, sems.at[0])
    copy_c.start()
    copy_h = pltpu.make_async_copy(h_ref, h_vmem, sems.at[1])
    copy_h.start()
    take_parts(lambda chip: real_lanes(own_ref[chip]), i_ref.at[0])
    take_parts(lambda chip: real_lanes(other_ref[chip]), i_ref.at[1])
    out_i = pltpu.make_async_copy(i_ref, i_out, sems.at[3])
    out_i.start()
    copy_c.wait()
    cross_t = fold(nt(i_ref[0], c_ref[0]) + nt(i_ref[1], c_ref[1]))
    cross_ref[...] = cross_t
    ritz_t = cross_t / ORDER
    stacked = jnp.concatenate(split3(ritz_t), axis=0)
    stacked = jnp.concatenate([stacked] * PARTS, axis=1)
    square = jnp.zeros((NEIG, LANES), F32)
    for half, ref in ((0, own_ref), (1, other_ref)):
        moved = jnp.dot(stacked, c_ref[half], preferred_element_type=F32)
        moved = (moved[32:48] + moved[16:32]) + moved[0:16]
        part = jnp.zeros((NEIG, LANES), F32)
        for chip in range(CHIPS):
            lanes = slice(LANES * chip, LANES * (chip + 1))
            resid = real_lanes(ref[chip]) - moved[:, lanes]
            resid_ref[half, :, lanes] = resid
            part = part + resid * resid
        square = square + part
    rms = jnp.sqrt(jnp.sum(square, axis=1, keepdims=True) / ORDER + EPS)
    rms_ref[...] = rms
    row = lax.broadcasted_iota(jnp.int32, (NEIG, NEIG), 0)
    column = lax.broadcasted_iota(jnp.int32, (NEIG, NEIG), 1)
    value = jnp.sum(jnp.where(row == column, ritz_t, 0.0), axis=1, keepdims=True)
    value = jnp.broadcast_to(value, (NEIG, LANES))
    rms = jnp.broadcast_to(rms, (NEIG, LANES))

    def scaled(resid, tile):
        return resid / (jnp.maximum(jnp.abs(diagonal_of(tile) - value), 1.0) * rms)

    resid = image_ref[...] - dot_exact(ritz_t, cvec_ref[...])
    search = scaled(resid, tile_ref[...])
    search_ref[...] = search
    for half, ref in ((0, own_ref), (1, other_ref)):
        take_parts(lambda chip: scaled(resid_ref[half, :, LANES * chip : LANES * (chip + 1)], ref[chip]), s_ref.at[half])
    out_s = pltpu.make_async_copy(s_ref, s_out, sems.at[2])
    out_s.start()
    copy_h.wait()
    simage = fold_rows(nt(h_vmem[0], s_ref[0]) + nt(h_vmem[1], s_ref[1]))
    pvec = pvec_ref[...]
    terms = jnp.concatenate(
        [nt_exact(simage, search), nt_exact(simage, pvec), nt_exact(pimage_ref[...], pvec), jnp.zeros((NEIG, NEIG), F32)],
        axis=1,
    )
    packed = jnp.concatenate([terms[0:8], terms[8:16]], axis=1)
    for chip in range(CHIPS):
        sent_ref[chip] = packed
    out_s.wait()
    out_i.wait()


def factor_kernel(
    s_hbm, c_hbm, p_hbm, i_hbm, gram_ref, cross_ref, inverse_ref, stiff_ref,
    s_ref, c_ref, p_ref, i_ref, sems,
):
    pairs = ((s_hbm, s_ref), (c_hbm, c_ref), (p_hbm, p_ref), (i_hbm, i_ref))
    copies = [pltpu.make_async_copy(a, b, sems.at[n]) for n, (a, b) in enumerate(pairs)]
    for copy in copies:
        copy.start()
    for copy in copies:
        copy.wait()

    def gram(left, right):
        return fold(nt(left[0], right[0]) + nt(left[1], right[1]))

    empty = jnp.zeros((NEIG, NEIG), F32)
    cc, pc, pp = gram_ref[0], gram_ref[1], gram_ref[2]
    sc, ss, ps = gram(s_ref, c_ref), gram(s_ref, s_ref), gram(p_ref, s_ref)
    low = jnp.concatenate(
        [
            jnp.concatenate([0.5 * cc, empty, empty], axis=1),
            jnp.concatenate([sc, 0.5 * ss, empty], axis=1),
            jnp.concatenate([pc, ps, 0.5 * pp], axis=1),
        ],
        axis=0,
    )
    mass = low + low.T
    low = jnp.concatenate(
        [
            jnp.concatenate([0.5 * cross_ref[...], empty, empty], axis=1),
            jnp.concatenate([gram(s_ref, i_ref), empty, empty], axis=1),
            jnp.concatenate([gram(p_ref, i_ref), empty, empty], axis=1),
        ],
        axis=0,
    )
    stiff_ref[...] = low + low.T
    size = 3 * NEIG
    row = lax.broadcasted_iota(jnp.int32, (size, size), 0)
    column = lax.broadcasted_iota(jnp.int32, (size, size), 1)
    identity = jnp.where(row == column, 1.0, 0.0).astype(F32)
    work = jnp.concatenate([mass, identity], axis=1)
    below = lax.broadcasted_iota(jnp.int32, (size, 1), 0)
    for k in range(size):
        factor = jnp.where(below > k, work[:, k : k + 1] / work[k : k + 1, k : k + 1], 0.0)
        work = work - factor * work[k : k + 1, :]
    pivots = jnp.sum(work[:, :size] * identity, axis=1, keepdims=True)
    inverse_ref[...] = work[:, size:] / jnp.sqrt(pivots)


def finish_kernel(inverse_ref, stiff_ref, own_ref, other_ref, c_ref, s_ref, p_ref, current_ref, previous_ref):
    size = 3 * NEIG
    total = own_ref[0] + other_ref[0]
    for chip in range(1, CHIPS):
        total = total + (own_ref[chip] + other_ref[chip])
    terms = jnp.concatenate([total[:, 0 : 3 * NEIG], total[:, 4 * NEIG : 7 * NEIG]], axis=0)
    ss, sp, pp = terms[:, 0:16], terms[:, 16:32], terms[:, 32:48]
    empty = jnp.zeros((NEIG, NEIG), F32)
    up = jnp.concatenate(
        [
            jnp.zeros((NEIG, size), F32),
            jnp.concatenate([empty, 0.5 * ss, sp], axis=1),
            jnp.concatenate([empty, empty, 0.5 * pp], axis=1),
        ],
        axis=0,
    )
    stiff = stiff_ref[...] + (up + up.T)
    inverse = inverse_ref[...]
    reduced = nt_exact(dot_exact(inverse, stiff), inverse)
    row = lax.broadcasted_iota(jnp.int32, (size, size), 0)
    column = lax.broadcasted_iota(jnp.int32, (size, size), 1)
    identity = jnp.where(row == column, 1.0, 0.0).astype(F32)
    diagonal = jnp.sum(reduced * identity, axis=1, keepdims=True)
    level = jnp.max(diagonal[:NEIG], axis=0, keepdims=True)
    signed = level * identity - reduced
    norm = jnp.sqrt(jnp.sum(jnp.sum(signed * signed, axis=1, keepdims=True), axis=0, keepdims=True))
    signed = signed / norm
    for _ in range(SIGN_STEPS):
        signed = 1.5 * signed - 0.5 * dot_exact(signed, dot_exact(signed, signed))
    projector = 0.5 * (identity + signed)
    wanted = jnp.where(lax.broadcasted_iota(jnp.int32, (size, size), 1) < NEIG, projector, 0.0)
    tn = (((0,), (0,)), ((), ()))
    coeffs_t = lax.dot_general(wanted, inverse, tn, precision=HIGHEST, preferred_element_type=F32)[0:NEIG]
    coeffs_t = coeffs_t * math.sqrt(ORDER)
    basis = jnp.concatenate([c_ref[...], s_ref[...], p_ref[...]], axis=0)
    current_ref[...] = dot_exact(coeffs_t, basis)[:, :ROWS]
    lane = lax.broadcasted_iota(jnp.int32, (NEIG, size), 1)
    previous_ref[...] = dot_exact(jnp.where(lane < NEIG, 0.0, coeffs_t), basis)[:, :ROWS]


def kernel_call(body, outs, args, flops, name, scratch=(), in_hbm=(), out_hbm=(), limit=LIMIT):
    return pl.pallas_call(
        body,
        out_shape=[jax.ShapeDtypeStruct(shape, kind) for shape, kind in outs],
        in_specs=[HBM if n in in_hbm else VMEM for n in range(len(args))],
        out_specs=[HBM if n in out_hbm else VMEM for n in range(len(outs))],
        scratch_shapes=scratch,
        compiler_params=pltpu.CompilerParams(vmem_limit_bytes=limit),
        cost_estimate=pl.CostEstimate(flops=flops, bytes_accessed=4 << 20, transcendentals=0),
        name=name,
    )(*args)


def to_chips(x):
    return lax.all_to_all(x, CHIP_AXES, 0, 0, tiled=True)


def to_core(x):
    return lax.ppermute(x, "grp_1", [(0, 1), (1, 0)])


def diagonal_tile(hamiltonian):
    device = lax.axis_index(ROWS_GRP)
    own_block = lax.dynamic_slice_in_dim(hamiltonian, device * ROWS, ROWS, 1)
    index = jnp.arange(ROWS)
    diag = jnp.sum(jnp.where(index[:, None] == index[None, :], own_block, 0.0), axis=0)
    rows = jnp.where(index[None, :] % NEIG == jnp.arange(NEIG)[:, None], diag[None, :], 0.0)
    lanes = (jnp.arange(LANES)[None, :] == SPARE + index[:, None] // NEIG).astype(F32)
    return dot_exact(rows, lanes)


def body(hamiltonian, current, previous):
    both = jnp.concatenate([current.T, previous.T], axis=0)
    v_own = to_chips(jnp.broadcast_to(both[None], (CHIPS, 2 * NEIG, ROWS)))
    tile = diagonal_tile(hamiltonian)
    cvec = jnp.pad(current.T, ((0, 0), (0, LANES - ROWS)))
    pvec = jnp.pad(previous.T, ((0, 0), (0, LANES - ROWS)))
    h_parts = prepare(hamiltonian)
    v_own, h_parts, tile = lax.optimization_barrier((v_own, h_parts, tile))
    v_other = to_core(v_own)
    block, parts = ((NEIG, LANES), F32), ((2, STACK, HALF), BF16)
    parts_vmem, h_half = pltpu.VMEM(*parts), pltpu.VMEM((PARTS * TALL, HALF), BF16)
    h_vmem = pltpu.VMEM((2, PARTS * TALL, HALF), BF16)
    half_vmem = pltpu.VMEM((STACK, HALF), BF16)
    whole = ((CHIPS, 2 * NEIG, ROWS), F32)
    product, v_own = kernel_call(
        image_own_kernel, [((PARTS * TALL, STACK), F32), whole], (h_parts, v_own), 1 << 30, "image_own",
        [h_half, half_vmem, pltpu.SemaphoreType.DMA((2,))], (0,), (1,),
    )
    image, sent, v_other = kernel_call(
        image_other_kernel, [block, ((CHIPS, NEIG, LANES), F32), whole], (h_parts, v_other, product, tile), 1 << 30, "image_other",
        [h_half, half_vmem, pltpu.SemaphoreType.DMA((2,))], (0,), (2,),
    )
    i_own = to_chips(sent)
    p_image, c_parts, p_parts, grams = kernel_call(
        previous_kernel,
        [block, parts, parts, ((3, NEIG, NEIG), F32)],
        (h_parts, v_own, v_other),
        6 << 30,
        "previous",
        [h_vmem, parts_vmem, parts_vmem, pltpu.SemaphoreType.DMA((3,))], (0,), (1, 2),
    )
    i_own, p_image, c_parts = lax.optimization_barrier((i_own, p_image, c_parts))
    i_other = to_core(i_own)
    search, rms, cross, sent, s_parts, i_parts = kernel_call(
        search_kernel,
        [block, ((NEIG, 1), F32), ((NEIG, NEIG), F32), ((CHIPS, 8, LANES), F32), parts, parts],
        (h_parts, i_own, i_other, c_parts, cvec, pvec, p_image, image, tile),
        6 << 30,
        "search",
        [h_vmem, parts_vmem, parts_vmem, parts_vmem, pltpu.VMEM((2, NEIG, HALF), F32), pltpu.SemaphoreType.DMA((4,))],
        (0, 3), (4, 5),
    )
    r_own = to_chips(sent)
    square = ((3 * NEIG, 3 * NEIG), F32)
    inverse, stiff = kernel_call(
        factor_kernel, [square, square], (s_parts, c_parts, p_parts, i_parts, grams, cross), 6 << 30, "factor",
        [parts_vmem] * 4 + [pltpu.SemaphoreType.DMA((4,))], (0, 1, 2, 3),
    )
    r_own, inverse = lax.optimization_barrier((r_own, inverse))
    r_other = to_core(r_own)
    new_current, new_previous = kernel_call(
        finish_kernel,
        [((NEIG, ROWS), F32)] * 2,
        (inverse, stiff, r_own, r_other, cvec, search, pvec),
        1 << 28,
        "finish",
        limit=8 << 20,
    )
    return new_current.T, new_previous.T, rms[:, 0]


def solution(mesh):
    finer = Mesh(mesh.devices.reshape(4, 4, 4, 2), ROWS_GRP)
    return jax.shard_map(
        body,
        mesh=finer,
        in_specs=(P(ROWS_GRP, None), P(ROWS_GRP, None), P(ROWS_GRP, None)),
        out_specs=(P(ROWS_GRP, None), P(ROWS_GRP, None), P()),
        check_vma=False,
    )
```

time: 118 us -> 92.6 us (0.78)
  blocking collectives: 33.2 us -> 0 us
  Pallas kernels: 31.1 us -> 37 us
  waiting for transfers between devices: 11.4 us -> 17.2 us
  local copies, waits for them, and re-layouts: 13.5 us -> 7.93 us
    all_to_all x2 -> x0, blocking collectives: 33.2 us -> none  [to_chips(): return lax.all_to_all(x, CHIP_AXES, 0, 0, tiled=True)]
    all_to_all x2 -> x3, starting transfers between devices: 16.6 us -> 21.4 us  [to_chips(): return lax.all_to_all(x, CHIP_AXES, 0, 0, tiled=True)]
    unnamed x8 -> x18, local copies, waits for them, and re-layouts: 11.1 us -> 6.75 us
    ppermute x4 -> x3, starting transfers between devices: 8.83 us -> 5.02 us  [to_core(): return lax.ppermute(x, 'grp_1', [(0, 1), (1, 0)])]
    all_to_all x2 -> x3, waiting for transfers between devices: 11.4 us -> 15.2 us  [to_chips(): return lax.all_to_all(x, CHIP_AXES, 0, 0, tiled=True)]
    pallas_call x1, Pallas kernels: 4.43 us -> 7.93 us  [prepare(): pl.pallas_call(prepare_kernel, grid=(CHUNKS,), out_shape=jax.ShapeDtypeSt...]
    pallas_call x5 -> x6, Pallas kernels: 26.7 us -> 29.1 us  [kernel_call(): pl.pallas_call(body, out_shape=[jax.ShapeDtypeStruct(shape, kind) for sha...]
    ppermute x4 -> x3, waiting for transfers between devices: 0.04 us -> 2.05 us  [to_core(): return lax.ppermute(x, 'grp_1', [(0, 1), (1, 0)])]
  transfers between devices with their start and end apart: 6 -> 6, of which waited for: 2 -> 5; matrix products, arithmetic and copies ran while one was open for 1% -> 2% of each run, Pallas kernels for 18% -> 25%
where the time goes in v2:
time: 92.6 us; the launch traced here: 91.9 us
  Pallas kernels  37 us (40%)
  starting transfers between devices  26.4 us (29%)
  waiting for transfers between devices  17.2 us (19%)
  local copies, waits for them, and re-layouts  7.93 us (9%)
  other arithmetic  2.35 us (3%)
    pallas_call x6, Pallas kernels, kernel_call(): pl.pallas_call(body, out_shape=[jax.ShapeDtypeStruct(shape, kind) for sha...  29.1 us
    all_to_all x3, starting transfers between devices, to_chips(): return lax.all_to_all(x, CHIP_AXES, 0, 0, tiled=True)  21.4 us
    all_to_all x3, waiting for transfers between devices, to_chips(): return lax.all_to_all(x, CHIP_AXES, 0, 0, tiled=True)  15.2 us
    pallas_call x1, Pallas kernels, prepare(): pl.pallas_call(prepare_kernel, grid=(CHUNKS,), out_shape=jax.ShapeDtypeSt...  7.93 us
    unnamed x18, local copies, waits for them, and re-layouts  6.75 us
    ppermute x3, starting transfers between devices, to_core(): return lax.ppermute(x, 'grp_1', [(0, 1), (1, 0)])  5.02 us
    ppermute x3, waiting for transfers between devices, to_core(): return lax.ppermute(x, 'grp_1', [(0, 1), (1, 0)])  2.05 us
  transfers between devices with their start and end apart: 6, of which 5 were waited for; matrix products, arithmetic and copies ran while one was open for 2% of the time, Pallas kernels for 25%

profile of v2, /device:TPU:1, one launch (start us, length us, event | category | flops | bytes accessed | tf_op | source)
XLA Modules:
  0.0 91.9 jit_solution(1919571025683250)
XLA Ops:
  1.4 1.2 %broadcast_in_dim.14 = f32[64,32,108]{2,1,0:T(8,128)} broadcast(f32[32,108]{1,0:T(8,128)S(1)} %pad_maximum_fusion), dimensions={1,2} | broadcast | bytes 898560 | tf_op jit(solution)/shard_map/broadcast_in_dim | solution.py:344
  2.5 12.0 %all-to-all-start = ((f32[64,32,108]{2,1,0:T(8,128)}), f32[64,32,108]{2,1,0:T(8,128)S(1)}, u32[]{:S(2)}, u32[]{:S(2)}) async-start(f32[64,32,108]{2,1,0:T(8,128)} %broadcast_in_dim.14), calls=%async_computation | async-start | bytes 2097152 | tf_op jit(solution)/shard_map/all_to_all | solution.py:325
  14.5 1.0 %select_reduce_fusion = f32[108]{0:T(128)S(1)} fusion(f32[108,13824]{1,0:T(8,128)} %h_ref.1, s32[]{:T(128)S(6)} %select_n.34), kind=kLoop, calls=%fused_computation.1 | loop fusion | flops 34884 | bytes 47092 | tf_op jit(solution)/shard_map/reduce_sum | solution.py:336
  15.5 7.9 %prepare.1.h_ref = bf16[2,224,8192]{2,1,0:T(8,128)(2,1)} custom-call(f32[108,13824]{1,0:T(8,128)} %h_ref.1), custom_call_target="tpu_custom_call" | custom-call | flops 29859840 | bytes 14929920 | tf_op jit(solution)/shard_map/prepare/pallas_call | solution.py:91
  23.6 8.4 %all-to-all-done.own_ref = f32[64,32,108]{2,1,0:T(8,128)S(1)} async-done(((f32[64,32,108]{2,1,0:T(8,128)}), f32[64,32,108]{2,1,0:T(8,128)S(1)}, u32[]{:S(2)}, u32[]{:S(2)}) %all-to-all-start) | async-done | bytes 884768 | tf_op jit(solution)/shard_map/all_to_all | solution.py:325
  32.0 2.4 %collective-permute-start = (f32[64,32,108]{2,1,0:T(8,128)S(1)}, f32[64,32,108]{2,1,0:T(8,128)S(1)}, u32[]{:S(2)}, u32[]{:S(2)}) collective-permute-start(f32[64,32,108]{2,1,0:T(8,128)S(1)} %all-to-all-done.own_ref), channel_id=1, source_target_pairs={{0,1},{1,0},{2,3},{3,2},{4,5},{5,4},{6,7},{7,6},{8,9},{9,8},{10,11... | collective-permute-start | bytes 2654216 | tf_op jit(solution)/shard_map/ppermute | solution.py:329
  34.4 3.1 %image_own.1 = (f32[224,32]{1,0:T(8,128)S(1)}, f32[64,32,108]{2,1,0:T(8,128)S(1)}) custom-call(bf16[2,224,8192]{2,1,0:T(8,128)(2,1)} %prepare.1.h_ref, f32[64,32,108]{2,1,0:T(8,128)S(1)} %all-to-all-done.own_ref), custom_call_target="tpu_custom_call" | custom-call | flops 1073741824 | bytes 4194304 | tf_op jit(solution)/shard_map/image_own/pallas_call | solution.py:312
  37.6 4.0 %image_other.1 = (f32[16,128]{1,0:T(8,128)S(1)}, f32[64,16,128]{2,1,0:T(8,128)}, f32[64,32,108]{2,1,0:T(8,128)S(1)}) custom-call(bf16[2,224,8192]{2,1,0:T(8,128)(2,1)} %prepare.1.h_ref, f32[64,32,108]{2,1,0:T(8,128)S(1)} %collective-permute-done.other_ref, f32[224,32]{1,0:T(8,128)S(1)} %get-tuple-element.32.product_ref, f32[16,128]{1,0:T(8,128)S(1)} %fusion.tile_ref), custom_call_target="tpu_custom_call" | custom-call | flops 1073741824 | bytes 4194304 | tf_op jit(solution)/shard_map/image_other/pallas_call | solution.py:312
  41.6 4.6 %all-to-all-start.1 = ((f32[64,16,128]{2,1,0:T(8,128)}), f32[64,16,128]{2,1,0:T(8,128)S(1)}, u32[]{:S(2)}, u32[]{:S(2)}) async-start(f32[64,16,128]{2,1,0:T(8,128)} %get-tuple-element.34), calls=%async_computation.1 | async-start | bytes 1048576 | tf_op jit(solution)/shard_map/all_to_all | solution.py:325
  46.3 5.5 %previous.1 = (f32[16,128]{1,0:T(8,128)S(1)}, bf16[2,32,8192]{2,1,0:T(8,128)(2,1)S(1)}, bf16[2,32,8192]{2,1,0:T(8,128)(2,1)S(1)}, f32[3,16,16]{2,1,0:T(8,128)S(1)}) custom-call(bf16[2,224,8192]{2,1,0:T(8,128)(2,1)} %prepare.1.h_ref, f32[64,32,108]{2,1,0:T(8,128)S(1)} %get-tuple-element.35.own_ref, f32[64,32,108]{2,1,0:T(8,128)S(1)} %get-tuple-element.36.other_ref), custom_call_target="tpu_custom_call" | custom-call | flops 6442450944 | bytes 4194304 | tf_op jit(solution)/shard_map/previous/pallas_call | solution.py:312
  51.8 1.1 %copy-done = bf16[2,32,8192]{2,1,0:T(8,128)(2,1)} copy-done((bf16[2,32,8192]{2,1,0:T(8,128)(2,1)}, bf16[2,32,8192]{2,1,0:T(8,128)(2,1)S(1)}, u32[]{:S(2)}) %copy-start) | copy-done | bytes 1048600
  52.8 1.0 %copy-done.5 = bf16[2,32,8192]{2,1,0:T(8,128)(2,1)} copy-done((bf16[2,32,8192]{2,1,0:T(8,128)(2,1)}, bf16[2,32,8192]{2,1,0:T(8,128)(2,1)S(1)}, u32[]{:S(2)}) %copy-start.5) | copy-done | bytes 1048600
  53.9 5.5 %all-to-all-done.1.own_ref = f32[64,16,128]{2,1,0:T(8,128)S(1)} async-done(((f32[64,16,128]{2,1,0:T(8,128)}), f32[64,16,128]{2,1,0:T(8,128)S(1)}, u32[]{:S(2)}, u32[]{:S(2)}) %all-to-all-start.1) | async-done | bytes 524320 | tf_op jit(solution)/shard_map/all_to_all | solution.py:325
  59.4 1.2 %collective-permute-start.1 = (f32[64,16,128]{2,1,0:T(8,128)S(1)}, f32[64,16,128]{2,1,0:T(8,128)S(1)}, u32[]{:S(2)}, u32[]{:S(2)}) collective-permute-start(f32[64,16,128]{2,1,0:T(8,128)S(1)} %all-to-all-done.1.own_ref), channel_id=1, source_target_pairs={{0,1},{1,0},{2,3},{3,2},{4,5},{5,4},{6,7},{7,6},{8,9},{9,8},{10,11... | collective-permute-start | bytes 1572872 | tf_op jit(solution)/shard_map/ppermute | solution.py:329
  60.7 1.5 %collective-permute-done.1.other_ref = f32[64,16,128]{2,1,0:T(8,128)S(1)} collective-permute-done((f32[64,16,128]{2,1,0:T(8,128)S(1)}, f32[64,16,128]{2,1,0:T(8,128)S(1)}, u32[]{:S(2)}, u32[]{:S(2)}) %collective-permute-start.1) | collective-permute-done | bytes 524320 | tf_op jit(solution)/shard_map/ppermute | solution.py:329
  62.2 1.2 %copy-done.1 = bf16[2,32,8192]{2,1,0:T(8,128)(2,1)S(1)} copy-done((bf16[2,32,8192]{2,1,0:T(8,128)(2,1)S(1)}, bf16[2,32,8192]{2,1,0:T(8,128)(2,1)}, u32[]{:S(2)}) %copy-start.1) | copy-done | bytes 1048600
  63.4 6.4 %search.1 = (f32[16,128]{1,0:T(8,128)S(1)}, f32[16,1]{1,0:T(8,128)S(1)}, f32[16,16]{1,0:T(8,128)S(1)}, f32[64,8,128]{2,1,0:T(8,128)}, bf16[2,32,8192]{2,1,0:T(8,...) custom-call(bf16[2,224,8192]{2,1,0:T(8,128)(2,1)} %prepare.1.h_ref, f32[64,16,128]{2,1,0:T(8,128)S(1)} %all-to-all-done.1.own_ref, ...), custom_call_target="tpu_custom_call" | custom-call | flops 6442450944 | bytes 4194304 | tf_op jit(solution)/shard_map/search/pallas_call | solution.py:312
  70.8 4.8 %all-to-all-start.2 = ((f32[64,8,128]{2,1,0:T(8,128)}), f32[64,8,128]{2,1,0:T(8,128)S(1)}, u32[]{:S(2)}, u32[]{:S(2)}) async-start(f32[64,8,128]{2,1,0:T(8,128)} %get-tuple-element.43), calls=%async_computation.2 | async-start | bytes 524288 | tf_op jit(solution)/shard_map/all_to_all | solution.py:325
  75.6 1.2 %copy-done.4 = bf16[2,32,8192]{2,1,0:T(8,128)(2,1)S(1)} copy-done((bf16[2,32,8192]{2,1,0:T(8,128)(2,1)S(1)}, bf16[2,32,8192]{2,1,0:T(8,128)(2,1)}, u32[]{:S(2)}) %copy-start.4) | copy-done | bytes 1048600
  76.8 1.2 %copy-done.6 = bf16[2,32,8192]{2,1,0:T(8,128)(2,1)S(1)} copy-done((bf16[2,32,8192]{2,1,0:T(8,128)(2,1)S(1)}, bf16[2,32,8192]{2,1,0:T(8,128)(2,1)}, u32[]{:S(2)}) %copy-start.6) | copy-done | bytes 1048600
  78.1 6.2 %factor.1 = (f32[48,48]{1,0:T(8,128)S(1)}, f32[48,48]{1,0:T(8,128)S(1)}) custom-call(bf16[2,32,8192]{2,1,0:T(8,128)(2,1)S(1)} %get-tuple-element.44.s_hbm, bf16[2,32,8192]{2,1,0:T(8,128)(2,1)S(1)} %copy-done.2, bf16[2,32,8192]{2,1,0:T(8,128)(2,1)S(1)} %copy-done.6, bf16[2,32,8192]{2,1,0:T(8,128)(2,1)S(1)} %copy-done.4, ...), custom_call_target="tpu_custom_call" | custom-call | flops 6442450944 | bytes 4194304 | tf_op jit(solution)/shard_map/factor/pallas_call | solution.py:312
  84.3 1.3 %all-to-all-done.2.own_ref = f32[64,8,128]{2,1,0:T(8,128)S(1)} async-done(((f32[64,8,128]{2,1,0:T(8,128)}), f32[64,8,128]{2,1,0:T(8,128)S(1)}, u32[]{:S(2)}, u32[]{:S(2)}) %all-to-all-start.2) | async-done | bytes 262176 | tf_op jit(solution)/shard_map/all_to_all | solution.py:325
  85.6 1.4 %collective-permute-start.2 = (f32[64,8,128]{2,1,0:T(8,128)S(1)}, f32[64,8,128]{2,1,0:T(8,128)S(1)}, u32[]{:S(2)}, u32[]{:S(2)}) collective-permute-start(f32[64,8,128]{2,1,0:T(8,128)S(1)} %all-to-all-done.2.own_ref), channel_id=1, source_target_pairs={{0,1},{1,0},{2,3},{3,2},{4,5},{5,4},{6,7},{7,6},{8,9},{9,8},{10,11... | collective-permute-start | bytes 786440 | tf_op jit(solution)/shard_map/ppermute | solution.py:329
  88.1 3.8 %finish.1 = (f32[16,108]{1,0:T(8,128)}, f32[16,108]{1,0:T(8,128)}) custom-call(f32[48,48]{1,0:T(8,128)S(1)} %get-tuple-element.50.inverse_ref, f32[48,48]{1,0:T(8,128)S(1)} %get-tuple-element.51.stiff_ref, f32[64,8,128]{2,1,0:T(8,128)S(1)} %all-to-all-done.2.own_ref, f32[64,8,128]{2,1,0:T(8,128)S(1)} %collective-permute-done.2.other_ref, ...), custom_call_target="tpu_custom_call" | custom-call | flops 268435456 | bytes 4194304 | tf_op jit(solution)/shard_map/finish/pallas_call | solution.py:312
  (21 shorter events, 3.1 us)
Async XLA Ops:
  2.5 29.5 %all-to-all-start = ((f32[64,32,108]{2,1,0:T(8,128)}), f32[64,32,108]{2,1,0:T(8,128)S(1)}, u32[]{:S(2)}, u32[]{:S(2)}) async-start(f32[64,32,108]{2,1,0:T(8,128)} %broadcast_in_dim.14), calls=%async_computation | async-start | bytes 2097152 | tf_op jit(solution)/shard_map/all_to_all | solution.py:325
  32.0 5.5 %collective-permute-start = (f32[64,32,108]{2,1,0:T(8,128)S(1)}, f32[64,32,108]{2,1,0:T(8,128)S(1)}, u32[]{:S(2)}, u32[]{:S(2)}) collective-permute-start(f32[64,32,108]{2,1,0:T(8,128)S(1)} %all-to-all-done.own_ref), channel_id=1, source_target_pairs={{0,1},{1,0},{2,3},{3,2},{4,5},{5,4},{6,7},{7,6},{8,9},{9,8},{10,11... | collective-permute-start | bytes 2654216 | tf_op jit(solution)/shard_map/ppermute | solution.py:329
  41.6 17.8 %all-to-all-start.1 = ((f32[64,16,128]{2,1,0:T(8,128)}), f32[64,16,128]{2,1,0:T(8,128)S(1)}, u32[]{:S(2)}, u32[]{:S(2)}) async-start(f32[64,16,128]{2,1,0:T(8,128)} %get-tuple-element.34), calls=%async_computation.1 | async-start | bytes 1048576 | tf_op jit(solution)/shard_map/all_to_all | solution.py:325
  46.2 14.4 %copy-start.7 = (f32[108,16]{0,1:T(8,128)S(1)}, f32[108,16]{0,1:T(8,128)}, u32[]{:S(2)}) copy-start(f32[108,16]{0,1:T(8,128)} %param.4) | copy-start | bytes 20740
  46.3 14.4 %copy-start.8 = (f32[108,16]{0,1:T(8,128)S(1)}, f32[108,16]{0,1:T(8,128)}, u32[]{:S(2)}) copy-start(f32[108,16]{0,1:T(8,128)} %param.5) | copy-start | bytes 20740
  51.7 1.1 %copy-start = (bf16[2,32,8192]{2,1,0:T(8,128)(2,1)}, bf16[2,32,8192]{2,1,0:T(8,128)(2,1)S(1)}, u32[]{:S(2)}) copy-start(bf16[2,32,8192]{2,1,0:T(8,128)(2,1)S(1)} %get-tuple-element.40.c_hbm) | copy-start | bytes 3145732
  52.8 1.0 %copy-start.5 = (bf16[2,32,8192]{2,1,0:T(8,128)(2,1)}, bf16[2,32,8192]{2,1,0:T(8,128)(2,1)S(1)}, u32[]{:S(2)}) copy-start(bf16[2,32,8192]{2,1,0:T(8,128)(2,1)S(1)} %get-tuple-element.45.p_hbm) | copy-start | bytes 3145732
  59.4 2.8 %collective-permute-start.1 = (f32[64,16,128]{2,1,0:T(8,128)S(1)}, f32[64,16,128]{2,1,0:T(8,128)S(1)}, u32[]{:S(2)}, u32[]{:S(2)}) collective-permute-start(f32[64,16,128]{2,1,0:T(8,128)S(1)} %all-to-all-done.1.own_ref), channel_id=1, source_target_pairs={{0,1},{1,0},{2,3},{3,2},{4,5},{5,4},{6,7},{7,6},{8,9},{9,8},{10,11... | collective-permute-start | bytes 1572872 | tf_op jit(solution)/shard_map/ppermute | solution.py:329
  62.2 1.2 %copy-start.1 = (bf16[2,32,8192]{2,1,0:T(8,128)(2,1)S(1)}, bf16[2,32,8192]{2,1,0:T(8,128)(2,1)}, u32[]{:S(2)}) copy-start(bf16[2,32,8192]{2,1,0:T(8,128)(2,1)} %copy-done) | copy-start | bytes 3145732
  63.4 12.2 %copy-start.2 = (bf16[2,32,8192]{2,1,0:T(8,128)(2,1)S(1)}, bf16[2,32,8192]{2,1,0:T(8,128)(2,1)}, u32[]{:S(2)}) copy-start(bf16[2,32,8192]{2,1,0:T(8,128)(2,1)} %copy-done) | copy-start | bytes 3145732
  69.8 1.0 %copy-start.3 = (bf16[2,32,8192]{2,1,0:T(8,128)(2,1)}, bf16[2,32,8192]{2,1,0:T(8,128)(2,1)S(1)}, u32[]{:S(2)}) copy-start(bf16[2,32,8192]{2,1,0:T(8,128)(2,1)S(1)} %get-tuple-element.46.i_hbm) | copy-start | bytes 3145732
  70.8 14.8 %all-to-all-start.2 = ((f32[64,8,128]{2,1,0:T(8,128)}), f32[64,8,128]{2,1,0:T(8,128)S(1)}, u32[]{:S(2)}, u32[]{:S(2)}) async-start(f32[64,8,128]{2,1,0:T(8,128)} %get-tuple-element.43), calls=%async_computation.2 | async-start | bytes 524288 | tf_op jit(solution)/shard_map/all_to_all | solution.py:325
  75.6 1.2 %copy-start.4 = (bf16[2,32,8192]{2,1,0:T(8,128)(2,1)S(1)}, bf16[2,32,8192]{2,1,0:T(8,128)(2,1)}, u32[]{:S(2)}) copy-start(bf16[2,32,8192]{2,1,0:T(8,128)(2,1)} %copy-done.3) | copy-start | bytes 3145732
  76.8 1.2 %copy-start.6 = (bf16[2,32,8192]{2,1,0:T(8,128)(2,1)S(1)}, bf16[2,32,8192]{2,1,0:T(8,128)(2,1)}, u32[]{:S(2)}) copy-start(bf16[2,32,8192]{2,1,0:T(8,128)(2,1)} %copy-done.5) | copy-start | bytes 3145732
  85.6 2.6 %collective-permute-start.2 = (f32[64,8,128]{2,1,0:T(8,128)S(1)}, f32[64,8,128]{2,1,0:T(8,128)S(1)}, u32[]{:S(2)}, u32[]{:S(2)}) collective-permute-start(f32[64,8,128]{2,1,0:T(8,128)S(1)} %all-to-all-done.2.own_ref), channel_id=1, source_target_pairs={{0,1},{1,0},{2,3},{3,2},{4,5},{5,4},{6,7},{7,6},{8,9},{9,8},{10,11... | collective-permute-start | bytes 786440 | tf_op jit(solution)/shard_map/ppermute | solution.py:329

commit v3 on v2

--- a/solution.py
+++ b/solution.py
@@ -18,14 +18,17 @@
 HALF = CHIPS * LANES
 TALL = 112
 CHUNKS = 4
+CHUNK = HALF // CHUNKS
 EPS = 1e-06
-ROWS_GRP = ("rows_0", "rows_1", "grp_0", "grp_1")
-CHIP_AXES = ("rows_0", "rows_1", "grp_0")
+AXIS = "device"
+CHIP_ORDER = [[2 * chip + core for chip in reversed(range(CHIPS))] for core in range(2)]
 F32, BF16 = jnp.float32, jnp.bfloat16
 HIGHEST = lax.Precision.HIGHEST
 VMEM = pl.BlockSpec(memory_space=pltpu.VMEM)
 HBM = pl.BlockSpec(memory_space=pltpu.HBM)
-LIMIT = 48 << 20
+LIMIT = 53 << 20
+LIMIT_IMAGE = 48 << 20
+LIMIT_SEARCH = 52 << 20
 PARTS = 2
 STACK = PARTS * NEIG
 SPARE = ROWS
@@ -77,76 +80,80 @@
 
 
 def prepare_kernel(h_ref, parts_ref):
-    core = lax.axis_index("grp_1")
+    core = lax.rem(lax.axis_index(AXIS), 2)
     for block in range(2 * CHIPS // CHUNKS):
         chip, owner = divmod(block, 2)
+        place = CHIPS // CHUNKS - 1 - chip
         half = jnp.where(core == owner, 0, 1)
         x = padded(h_ref[:, ROWS * block : ROWS * block + ROWS])
         for number, part in enumerate(split(x)):
-            parts_ref[half, TALL * number : TALL * number + ROWS, LANES * chip : LANES * (chip + 1)] = part
+            parts_ref[half, 0, TALL * number : TALL * number + ROWS, LANES * place : LANES * (place + 1)] = part
 
 
 def prepare(hamiltonian):
-    width, out = ORDER // CHUNKS, HALF // CHUNKS
     return pl.pallas_call(
         prepare_kernel,
         grid=(CHUNKS,),
-        out_shape=jax.ShapeDtypeStruct((2, PARTS * TALL, HALF), BF16),
-        in_specs=[pl.BlockSpec((ROWS, width), lambda i: (0, i))],
-        out_specs=pl.BlockSpec((2, PARTS * TALL, out), lambda i: (0, 0, i)),
+        out_shape=jax.ShapeDtypeStruct((2, CHUNKS, PARTS * TALL, CHUNK), BF16),
+        in_specs=[pl.BlockSpec((ROWS, ORDER // CHUNKS), lambda i: (0, i))],
+        out_specs=pl.BlockSpec((2, 1, PARTS * TALL, CHUNK), lambda i: (0, CHUNKS - 1 - i, 0, 0)),
         compiler_params=pltpu.CompilerParams(vmem_limit_bytes=58 << 20),
         cost_estimate=pl.CostEstimate(flops=20 * ROWS * ORDER, bytes_accessed=10 * ROWS * ORDER, transcendentals=0),
         name="prepare",
     )(hamiltonian)
 
 
+def half_copies(h_ref, h_vmem, half, sems):
+    copies = [pltpu.make_async_copy(h_ref.at[half, n], h_vmem.at[n], sems.at[n]) for n in range(CHUNKS)]
+    for copy in copies:
+        copy.start()
+    return copies
+
+
+def times(h_vmem, parts, copies):
+    product = None
+    for n, copy in enumerate(copies):
+        copy.wait()
+        term = nt(h_vmem[n], parts[:, CHUNK * n : CHUNK * (n + 1)])
+        product = term if product is None else product + term
+    return product
+
+
 def take_parts(tile_of, parts_ref):
     for chip in range(CHIPS):
         for number, part in enumerate(split(tile_of(chip))):
             parts_ref[NEIG * number : NEIG * (number + 1), LANES * chip : LANES * (chip + 1)] = part
 
 
-def image_own_kernel(h_ref, own_ref, product_ref, own_out, h_vmem, parts, sems):
-    copy = pltpu.make_async_copy(h_ref.at[0], h_vmem, sems.at[0])
-    copy.start()
-    keep = pltpu.make_async_copy(own_ref, own_out, sems.at[1])
-    keep.start()
+def image_own_kernel(h_ref, own_ref, product_ref, h_vmem, parts, sems):
+    copies = half_copies(h_ref, h_vmem, 0, sems)
     take_parts(lambda chip: padded(own_ref[chip, 0:NEIG]), parts)
-    copy.wait()
-    product_ref[...] = nt(h_vmem[...], parts[...])
-    keep.wait()
-
-
-def image_other_kernel(h_ref, other_ref, product_ref, tile_ref, image_ref, sent_ref, other_out, h_vmem, parts, sems):
-    copy = pltpu.make_async_copy(h_ref.at[1], h_vmem, sems.at[0])
-    copy.start()
-    keep = pltpu.make_async_copy(other_ref, other_out, sems.at[1])
-    keep.start()
+    product_ref[...] = times(h_vmem, parts, copies)
+
+
+def image_other_kernel(h_ref, other_ref, product_ref, tile_ref, image_ref, sent_ref, h_vmem, parts, sems):
+    copies = half_copies(h_ref, h_vmem, 1, sems)
     take_parts(lambda chip: padded(other_ref[chip, 0:NEIG]), parts)
-    copy.wait()
-    image = fold_rows(product_ref[...] + nt(h_vmem[...], parts[...]))
+    image = fold_rows(product_ref[...] + times(h_vmem, parts, copies))
     image_ref[...] = image
     sent = image + tile_ref[...]
     for chip in range(CHIPS):
         sent_ref[chip] = sent
-    keep.wait()
-
-
-def previous_kernel(h_ref, own_ref, other_ref, image_ref, c_out, p_out, gram_ref, h_vmem, c_ref, p_ref, sems):
-    copy = pltpu.make_async_copy(h_ref, h_vmem, sems.at[0])
-    copy.start()
+
+
+def previous_kernel(h_ref, own_ref, other_ref, image_ref, c_out, p_out, gram_ref, h_vmem, c_ref, p_ref, sems, h_sems):
+    copies = [half_copies(h_ref, h_vmem.at[half], half, h_sems.at[half]) for half in range(2)]
     for half, ref in ((0, own_ref), (1, other_ref)):
         take_parts(lambda chip: padded(ref[chip, 0:NEIG]), c_ref.at[half])
         take_parts(lambda chip: padded(ref[chip, NEIG : 2 * NEIG]), p_ref.at[half])
-    out_c = pltpu.make_async_copy(c_ref, c_out, sems.at[1])
-    out_p = pltpu.make_async_copy(p_ref, p_out, sems.at[2])
+    out_c = pltpu.make_async_copy(c_ref, c_out, sems.at[0])
+    out_p = pltpu.make_async_copy(p_ref, p_out, sems.at[1])
     out_c.start()
     out_p.start()
     gram_ref[0] = fold(nt(c_ref[0], c_ref[0]) + nt(c_ref[1], c_ref[1]))
     gram_ref[1] = fold(nt(p_ref[0], c_ref[0]) + nt(p_ref[1], c_ref[1]))
     gram_ref[2] = fold(nt(p_ref[0], p_ref[0]) + nt(p_ref[1], p_ref[1]))
-    copy.wait()
-    image_ref[...] = fold_rows(nt(h_vmem[0], p_ref[0]) + nt(h_vmem[1], p_ref[1]))
+    image_ref[...] = fold_rows(times(h_vmem.at[0], p_ref[0], copies[0]) + times(h_vmem.at[1], p_ref[1], copies[1]))
     out_c.wait()
     out_p.wait()
 
@@ -161,15 +168,14 @@
 def search_kernel(
     h_ref, own_ref, other_ref, c_hbm, cvec_ref, pvec_ref, pimage_ref, image_ref, tile_ref,
     search_ref, rms_ref, cross_ref, sent_ref, s_out, i_out,
-    h_vmem, c_ref, i_ref, s_ref, resid_ref, sems,
+    h_vmem, c_ref, i_ref, s_ref, resid_ref, sems, h_sems,
 ):
     copy_c = pltpu.make_async_copy(c_hbm, c_ref, sems.at[0])
     copy_c.start()
-    copy_h = pltpu.make_async_copy(h_ref, h_vmem, sems.at[1])
-    copy_h.start()
+    copies = [half_copies(h_ref, h_vmem.at[half], half, h_sems.at[half]) for half in range(2)]
     take_parts(lambda chip: real_lanes(own_ref[chip]), i_ref.at[0])
     take_parts(lambda chip: real_lanes(other_ref[chip]), i_ref.at[1])
-    out_i = pltpu.make_async_copy(i_ref, i_out, sems.at[3])
+    out_i = pltpu.make_async_copy(i_ref, i_out, sems.at[1])
     out_i.start()
     copy_c.wait()
     cross_t = fold(nt(i_ref[0], c_ref[0]) + nt(i_ref[1], c_ref[1]))
@@ -206,8 +212,7 @@
         take_parts(lambda chip: scaled(resid_ref[half, :, LANES * chip : LANES * (chip + 1)], ref[chip]), s_ref.at[half])
     out_s = pltpu.make_async_copy(s_ref, s_out, sems.at[2])
     out_s.start()
-    copy_h.wait()
-    simage = fold_rows(nt(h_vmem[0], s_ref[0]) + nt(h_vmem[1], s_ref[1]))
+    simage = fold_rows(times(h_vmem.at[0], s_ref[0], copies[0]) + times(h_vmem.at[1], s_ref[1], copies[1]))
     pvec = pvec_ref[...]
     terms = jnp.concatenate(
         [nt_exact(simage, search), nt_exact(simage, pvec), nt_exact(pimage_ref[...], pvec), jnp.zeros((NEIG, NEIG), F32)],
@@ -293,10 +298,14 @@
     diagonal = jnp.sum(reduced * identity, axis=1, keepdims=True)
     level = jnp.max(diagonal[:NEIG], axis=0, keepdims=True)
     signed = level * identity - reduced
-    norm = jnp.sqrt(jnp.sum(jnp.sum(signed * signed, axis=1, keepdims=True), axis=0, keepdims=True))
-    signed = signed / norm
-    for _ in range(SIGN_STEPS):
-        signed = 1.5 * signed - 0.5 * dot_exact(signed, dot_exact(signed, signed))
+    square = dot_exact(signed, signed)
+    total = jnp.sum(jnp.sum(signed * signed, axis=1, keepdims=True), axis=0, keepdims=True)
+    square = square / total
+    signed = signed / jnp.sqrt(total)
+    for step in range(SIGN_STEPS):
+        if step > 0:
+            square = dot_exact(signed, signed)
+        signed = dot_exact(signed, 1.5 * identity - 0.5 * square)
     projector = 0.5 * (identity + signed)
     wanted = jnp.where(lax.broadcasted_iota(jnp.int32, (size, size), 1) < NEIG, projector, 0.0)
     tn = (((0,), (0,)), ((), ()))
@@ -322,15 +331,15 @@
 
 
 def to_chips(x):
-    return lax.all_to_all(x, CHIP_AXES, 0, 0, tiled=True)
+    return lax.all_to_all(x, AXIS, 0, 0, axis_index_groups=CHIP_ORDER, tiled=True)
 
 
 def to_core(x):
-    return lax.ppermute(x, "grp_1", [(0, 1), (1, 0)])
+    return lax.ppermute(x, AXIS, [(device, device ^ 1) for device in range(DEVICES)])
 
 
 def diagonal_tile(hamiltonian):
-    device = lax.axis_index(ROWS_GRP)
+    device = lax.axis_index(AXIS)
     own_block = lax.dynamic_slice_in_dim(hamiltonian, device * ROWS, ROWS, 1)
     index = jnp.arange(ROWS)
     diag = jnp.sum(jnp.where(index[:, None] == index[None, :], own_block, 0.0), axis=0)
@@ -349,17 +358,17 @@
     v_own, h_parts, tile = lax.optimization_barrier((v_own, h_parts, tile))
     v_other = to_core(v_own)
     block, parts = ((NEIG, LANES), F32), ((2, STACK, HALF), BF16)
-    parts_vmem, h_half = pltpu.VMEM(*parts), pltpu.VMEM((PARTS * TALL, HALF), BF16)
-    h_vmem = pltpu.VMEM((2, PARTS * TALL, HALF), BF16)
-    half_vmem = pltpu.VMEM((STACK, HALF), BF16)
-    whole = ((CHIPS, 2 * NEIG, ROWS), F32)
-    product, v_own = kernel_call(
-        image_own_kernel, [((PARTS * TALL, STACK), F32), whole], (h_parts, v_own), 1 << 30, "image_own",
-        [h_half, half_vmem, pltpu.SemaphoreType.DMA((2,))], (0,), (1,),
-    )
-    image, sent, v_other = kernel_call(
-        image_other_kernel, [block, ((CHIPS, NEIG, LANES), F32), whole], (h_parts, v_other, product, tile), 1 << 30, "image_other",
-        [h_half, half_vmem, pltpu.SemaphoreType.DMA((2,))], (0,), (2,),
+    parts_vmem, half_vmem = pltpu.VMEM(*parts), pltpu.VMEM((STACK, HALF), BF16)
+    h_vmem = pltpu.VMEM((2, CHUNKS, PARTS * TALL, CHUNK), BF16)
+    h_half = pltpu.VMEM((CHUNKS, PARTS * TALL, CHUNK), BF16)
+    dma = pltpu.SemaphoreType.DMA
+    (product,) = kernel_call(
+        image_own_kernel, [((PARTS * TALL, STACK), F32)], (h_parts, v_own), 1 << 30, "image_own",
+        [h_half, half_vmem, dma((CHUNKS,))], (0,), limit=LIMIT_IMAGE,
+    )
+    image, sent = kernel_call(
+        image_other_kernel, [block, ((CHIPS, NEIG, LANES), F32)], (h_parts, v_other, product, tile), 1 << 30, "image_other",
+        [h_half, half_vmem, dma((CHUNKS,))], (0,), limit=LIMIT_IMAGE,
     )
     i_own = to_chips(sent)
     p_image, c_parts, p_parts, grams = kernel_call(
@@ -368,7 +377,7 @@
         (h_parts, v_own, v_other),
         6 << 30,
         "previous",
-        [h_vmem, parts_vmem, parts_vmem, pltpu.SemaphoreType.DMA((3,))], (0,), (1, 2),
+        [h_vmem, parts_vmem, parts_vmem, dma((2,)), dma((2, CHUNKS))], (0,), (1, 2),
     )
     i_own, p_image, c_parts = lax.optimization_barrier((i_own, p_image, c_parts))
     i_other = to_core(i_own)
@@ -378,16 +387,16 @@
         (h_parts, i_own, i_other, c_parts, cvec, pvec, p_image, image, tile),
         6 << 30,
         "search",
-        [h_vmem, parts_vmem, parts_vmem, parts_vmem, pltpu.VMEM((2, NEIG, HALF), F32), pltpu.SemaphoreType.DMA((4,))],
-        (0, 3), (4, 5),
+        [h_vmem, parts_vmem, parts_vmem, parts_vmem, pltpu.VMEM((2, NEIG, HALF), F32), dma((3,)), dma((2, CHUNKS))],
+        (0, 3), (4, 5), limit=LIMIT_SEARCH,
     )
     r_own = to_chips(sent)
     square = ((3 * NEIG, 3 * NEIG), F32)
     inverse, stiff = kernel_call(
         factor_kernel, [square, square], (s_parts, c_parts, p_parts, i_parts, grams, cross), 6 << 30, "factor",
-        [parts_vmem] * 4 + [pltpu.SemaphoreType.DMA((4,))], (0, 1, 2, 3),
-    )
-    r_own, inverse = lax.optimization_barrier((r_own, inverse))
+        [parts_vmem] * 4 + [dma((4,))], (0, 1, 2, 3),
+    )
+    r_own, inverse, rms = lax.optimization_barrier((r_own, inverse, rms[:, 0]))
     r_other = to_core(r_own)
     new_current, new_previous = kernel_call(
         finish_kernel,
@@ -397,15 +406,15 @@
         "finish",
         limit=8 << 20,
     )
-    return new_current.T, new_previous.T, rms[:, 0]
+    return new_current.T, new_previous.T, rms
 
 
 def solution(mesh):
-    finer = Mesh(mesh.devices.reshape(4, 4, 4, 2), ROWS_GRP)
+    line = Mesh(mesh.devices.reshape(DEVICES), (AXIS,))
     return jax.shard_map(
         body,
-        mesh=finer,
-        in_specs=(P(ROWS_GRP, None), P(ROWS_GRP, None), P(ROWS_GRP, None)),
-        out_specs=(P(ROWS_GRP, None), P(ROWS_GRP, None), P()),
+        mesh=line,
+        in_specs=(P(AXIS, None), P(AXIS, None), P(AXIS, None)),
+        out_specs=(P(AXIS, None), P(AXIS, None), P()),
         check_vma=False,
     )

time: 92.6 us -> 96.2 us (1.039)
  starting transfers between devices: 26.4 us -> 37.9 us
  waiting for transfers between devices: 17.2 us -> 6.04 us
  Pallas kernels: 37 us -> 47.2 us
  local copies, waits for them, and re-layouts: 7.93 us -> 1.17 us
    all_to_all x3, starting transfers between devices: 21.4 us -> 34.1 us  [to_chips(): lax.all_to_all(x, AXIS, 0, 0, axis_index_groups=CHIP_ORDER, tiled=True)]
    all_to_all x3, waiting for transfers between devices: 15.2 us -> 3.36 us  [to_chips(): lax.all_to_all(x, AXIS, 0, 0, axis_index_groups=CHIP_ORDER, tiled=True)]
    pallas_call x6, Pallas kernels: 29.1 us -> 39.2 us  [kernel_call(): pl.pallas_call(body, out_shape=[jax.ShapeDtypeStruct(shape, kind) for sha...]
    unnamed x18 -> x8, local copies, waits for them, and re-layouts: 6.75 us -> 0.02 us
    ppermute x3, starting transfers between devices: 5.02 us -> 3.8 us  [to_core(): lax.ppermute(x, AXIS, [(device, device ^ 1) for device in range(DEVICES)])]
  transfers between devices with their start and end apart: 6 -> 6, of which waited for: 5 -> 3; matrix products, arithmetic and copies ran while one was open for 2% -> 2% of each run, Pallas kernels for 25% -> 29%
where the time goes in v3:
time: 96.2 us; the launch traced here: 95.7 us
  Pallas kernels  47.2 us (49%)
  starting transfers between devices  37.9 us (39%)
  waiting for transfers between devices  6.04 us (6%)
  other arithmetic  2.36 us (2%)
  local copies, waits for them, and re-layouts  1.17 us (1%)
    pallas_call x6, Pallas kernels, kernel_call(): pl.pallas_call(body, out_shape=[jax.ShapeDtypeStruct(shape, kind) for sha...  39.2 us
    all_to_all x3, starting transfers between devices, to_chips(): lax.all_to_all(x, AXIS, 0, 0, axis_index_groups=CHIP_ORDER, tiled=True)  34.1 us
    pallas_call x1, Pallas kernels, prepare(): pl.pallas_call(prepare_kernel, grid=(CHUNKS,), out_shape=jax.ShapeDtypeSt...  7.98 us
    ppermute x3, starting transfers between devices, to_core(): lax.ppermute(x, AXIS, [(device, device ^ 1) for device in range(DEVICES)])  3.8 us
    all_to_all x3, waiting for transfers between devices, to_chips(): lax.all_to_all(x, AXIS, 0, 0, axis_index_groups=CHIP_ORDER, tiled=True)  3.36 us
    ppermute x3, waiting for transfers between devices, to_core(): lax.ppermute(x, AXIS, [(device, device ^ 1) for device in range(DEVICES)])  2.68 us
  transfers between devices with their start and end apart: 6, of which 3 were waited for; matrix products, arithmetic and copies ran while one was open for 2% of the time, Pallas kernels for 29%

profile of v3, /device:TPU:1, one launch (start us, length us, event | category | flops | bytes accessed | tf_op | source)
XLA Modules:
  0.0 95.7 jit_solution(3571522852361488051)
XLA Ops:
  0.6 0.7 pad_maximum_fusion
  1.4 1.1 %broadcast_in_dim.14 = f32[64,32,108]{2,1,0:T(8,128)} broadcast(f32[32,108]{1,0:T(8,128)S(1)} %pad_maximum_fusion), dimensions={1,2} | broadcast | bytes 898560 | tf_op jit(solution)/shard_map/broadcast_in_dim | solution.py:353
  2.5 13.7 %all-to-all-start = ((f32[64,32,108]{2,1,0:T(8,128)}), f32[64,32,108]{2,1,0:T(8,128)S(1)}, u32[]{:S(2)}, u32[]{:S(2)}) async-start(f32[64,32,108]{2,1,0:T(8,128)} %broadcast_in_dim.14), calls=%async_computation | async-start | bytes 2097152 | tf_op jit(solution)/shard_map/all_to_all | solution.py:334
  16.2 1.0 %select_reduce_fusion = f32[108]{0:T(128)S(1)} fusion(f32[108,13824]{1,0:T(8,128)} %h_ref.1, s32[]{:T(128)S(6)} %select_n.34), kind=kLoop, calls=%fused_computation.1 | loop fusion | flops 34884 | bytes 47092 | tf_op jit(solution)/shard_map/reduce_sum | solution.py:345
  17.2 8.0 %prepare.1.h_ref = bf16[2,4,224,2048]{3,2,1,0:T(8,128)(2,1)} custom-call(f32[108,13824]{1,0:T(8,128)} %h_ref.1), custom_call_target="tpu_custom_call" | custom-call | flops 29859840 | bytes 14929920 | tf_op jit(solution)/shard_map/prepare/pallas_call | solution.py:94
  25.2 0.2 fusion.tile_ref
  25.4 3.4 %all-to-all-done.own_ref = f32[64,32,108]{2,1,0:T(8,128)S(1)} async-done(((f32[64,32,108]{2,1,0:T(8,128)}), f32[64,32,108]{2,1,0:T(8,128)S(1)}, u32[]{:S(2)}, u32[]{:S(2)}) %all-to-all-start) | async-done | bytes 884768 | tf_op jit(solution)/shard_map/all_to_all | solution.py:334
  28.8 1.6 %collective-permute-start = (f32[64,32,108]{2,1,0:T(8,128)S(1)}, f32[64,32,108]{2,1,0:T(8,128)S(1)}, u32[]{:S(2)}, u32[]{:S(2)}) collective-permute-start(f32[64,32,108]{2,1,0:T(8,128)S(1)} %all-to-all-done.own_ref), channel_id=1, source_target_pairs={{0,1},{1,0},{2,3},{3,2},{4,5},{5,4},{6,7},{7,6},{8,9},{9,8},{10,11... | collective-permute-start | bytes 2654216 | tf_op jit(solution)/shard_map/ppermute | solution.py:338
  30.3 3.6 %image_own.1.product_ref = f32[224,32]{1,0:T(8,128)S(1)} custom-call(bf16[2,4,224,2048]{3,2,1,0:T(8,128)(2,1)} %prepare.1.h_ref, f32[64,32,108]{2,1,0:T(8,128)S(1)} %all-to-all-done.own_ref), custom_call_target="tpu_custom_call" | custom-call | flops 1073741824 | bytes 4194304 | tf_op jit(solution)/shard_map/image_own/pallas_call | solution.py:321
  34.0 4.9 %image_other.1 = (f32[16,128]{1,0:T(8,128)S(1)}, f32[64,16,128]{2,1,0:T(8,128)}) custom-call(bf16[2,4,224,2048]{3,2,1,0:T(8,128)(2,1)} %prepare.1.h_ref, f32[64,32,108]{2,1,0:T(8,128)S(1)} %collective-permute-done.other_ref, f32[224,32]{1,0:T(8,128)S(1)} %image_own.1.product_ref, f32[16,128]{1,0:T(8,128)S(1)} %fusion.tile_ref), custom_call_target="tpu_custom_call" | custom-call | flops 1073741824 | bytes 4194304 | tf_op jit(solution)/shard_map/image_other/pallas_call | solution.py:321
  38.9 10.4 %all-to-all-start.1 = ((f32[64,16,128]{2,1,0:T(8,128)}), f32[64,16,128]{2,1,0:T(8,128)S(1)}, u32[]{:S(2)}, u32[]{:S(2)}) async-start(f32[64,16,128]{2,1,0:T(8,128)} %get-tuple-element.31), calls=%async_computation.1 | async-start | bytes 1048576 | tf_op jit(solution)/shard_map/all_to_all | solution.py:334
  49.4 0.0 copy-start.2
  49.4 0.0 copy-start.3
  49.4 7.6 %previous.1 = (f32[16,128]{1,0:T(8,128)S(1)}, bf16[2,32,8192]{2,1,0:T(8,128)(2,1)}, bf16[2,32,8192]{2,1,0:T(8,128)(2,1)}, f32[3,16,16]{2,1,0:T(8,128)S(1)}) custom-call(bf16[2,4,224,2048]{3,2,1,0:T(8,128)(2,1)} %prepare.1.h_ref, f32[64,32,108]{2,1,0:T(8,128)} %copy-done, f32[64,32,108]{2,1,0:T(8,128)} %copy-done.1), custom_call_target="tpu_custom_call" | custom-call | flops 6442450944 | bytes 4194304 | tf_op jit(solution)/shard_map/previous/pallas_call | solution.py:321
  57.0 0.0 all-to-all-done.1.own_ref
  57.1 1.6 %collective-permute-start.1 = (f32[64,16,128]{2,1,0:T(8,128)S(1)}, f32[64,16,128]{2,1,0:T(8,128)S(1)}, u32[]{:S(2)}, u32[]{:S(2)}) collective-permute-start(f32[64,16,128]{2,1,0:T(8,128)S(1)} %all-to-all-done.1.own_ref), channel_id=1, source_target_pairs={{0,1},{1,0},{2,3},{3,2},{4,5},{5,4},{6,7},{7,6},{8,9},{9,8},{10,11... | collective-permute-start | bytes 1572872 | tf_op jit(solution)/shard_map/ppermute | solution.py:338
  58.6 1.5 %collective-permute-done.1.other_ref = f32[64,16,128]{2,1,0:T(8,128)S(1)} collective-permute-done((f32[64,16,128]{2,1,0:T(8,128)S(1)}, f32[64,16,128]{2,1,0:T(8,128)S(1)}, u32[]{:S(2)}, u32[]{:S(2)}) %collective-permute-start.1) | collective-permute-done | bytes 524320 | tf_op jit(solution)/shard_map/ppermute | solution.py:338
  60.2 11.2 %search.1 = (f32[16,128]{1,0:T(8,128)S(1)}, f32[16,1]{1,0:T(8,128)S(1)}, f32[16,16]{1,0:T(8,128)S(1)}, f32[64,8,128]{2,1,0:T(8,128)}, bf16[2,32,8192]{2,1,0:T(8,128)(2,1)}, /*index=5*/bf16[2,32,8192]{2,1,0:T(8,128)(2,1)}) custom-call(bf16[2,4,224,2048]{3,2,1,0:T(8,128)(2,1)} %prepare.1.h_ref, f32[64,16,128]{2,1,0:T(8,128)S(1)} %all-to-all-done.1.own_ref, ...), custom_call_target="tpu_custom_call" | custom-call | flops 6442450944 | bytes 4194304 | tf_op jit(solution)/shard_map/search/pallas_call | solution.py:321
  71.4 10.0 %all-to-all-start.2 = ((f32[64,8,128]{2,1,0:T(8,128)}), f32[64,8,128]{2,1,0:T(8,128)S(1)}, u32[]{:S(2)}, u32[]{:S(2)}) async-start(f32[64,8,128]{2,1,0:T(8,128)} %get-tuple-element.38), calls=%async_computation.2 | async-start | bytes 524288 | tf_op jit(solution)/shard_map/all_to_all | solution.py:334
  81.4 8.1 %factor.1 = (f32[48,48]{1,0:T(8,128)S(1)}, f32[48,48]{1,0:T(8,128)S(1)}) custom-call(bf16[2,32,8192]{2,1,0:T(8,128)(2,1)} %get-tuple-element.39.s_hbm, bf16[2,32,8192]{2,1,0:T(8,128)(2,1)} %get-tuple-element.35.c_hbm, bf16[2,32,8192]{2,1,0:T(8,128)(2,1)} %get-tuple-element.40.p_hbm, bf16[2,32,8192]{2,1,0:T(8,128)(2,1)} %get-tuple-element.41.i_hbm, ...), custom_call_target="tpu_custom_call" | custom-call | flops 6442450944 | bytes 4194304 | tf_op jit(solution)/shard_map/factor/pallas_call | solution.py:321
  89.5 0.6 reduce
  90.1 0.7 collective-permute-start.2
  90.8 1.2 %collective-permute-done.2.other_ref = f32[64,8,128]{2,1,0:T(8,128)S(1)} collective-permute-done((f32[64,8,128]{2,1,0:T(8,128)S(1)}, f32[64,8,128]{2,1,0:T(8,128)S(1)}, u32[]{:S(2)}, u32[]{:S(2)}) %collective-permute-start.2) | collective-permute-done | bytes 262176 | tf_op jit(solution)/shard_map/ppermute | solution.py:338
  92.0 3.7 %finish.1 = (f32[16,108]{1,0:T(8,128)}, f32[16,108]{1,0:T(8,128)}) custom-call(f32[48,48]{1,0:T(8,128)S(1)} %get-tuple-element.46.inverse_ref, f32[48,48]{1,0:T(8,128)S(1)} %get-tuple-element.47.stiff_ref, f32[64,8,128]{2,1,0:T(8,128)S(1)} %all-to-all-done.2.own_ref, f32[64,8,128]{2,1,0:T(8,128)S(1)} %collective-permute-done.2.other_ref, ...), custom_call_target="tpu_custom_call" | custom-call | flops 268435456 | bytes 4194304 | tf_op jit(solution)/shard_map/finish/pallas_call | solution.py:321
  (11 shorter events, 0.0 us)
Async XLA Ops:
  2.5 26.3 %all-to-all-start = ((f32[64,32,108]{2,1,0:T(8,128)}), f32[64,32,108]{2,1,0:T(8,128)S(1)}, u32[]{:S(2)}, u32[]{:S(2)}) async-start(f32[64,32,108]{2,1,0:T(8,128)} %broadcast_in_dim.14), calls=%async_computation | async-start | bytes 2097152 | tf_op jit(solution)/shard_map/all_to_all | solution.py:334
  28.8 10.1 %copy-start = (f32[64,32,108]{2,1,0:T(8,128)}, f32[64,32,108]{2,1,0:T(8,128)S(1)}, u32[]{:S(2)}) copy-start(f32[64,32,108]{2,1,0:T(8,128)S(1)} %all-to-all-done.own_ref) | copy-start | bytes 2654212
  28.8 5.2 %collective-permute-start = (f32[64,32,108]{2,1,0:T(8,128)S(1)}, f32[64,32,108]{2,1,0:T(8,128)S(1)}, u32[]{:S(2)}, u32[]{:S(2)}) collective-permute-start(f32[64,32,108]{2,1,0:T(8,128)S(1)} %all-to-all-done.own_ref), channel_id=1, source_target_pairs={{0,1},{1,0},{2,3},{3,2},{4,5},{5,4},{6,7},{7,6},{8,9},{9,8},{10,11... | collective-permute-start | bytes 2654216 | tf_op jit(solution)/shard_map/ppermute | solution.py:338
  34.0 15.4 %copy-start.1 = (f32[64,32,108]{2,1,0:T(8,128)}, f32[64,32,108]{2,1,0:T(8,128)S(1)}, u32[]{:S(2)}) copy-start(f32[64,32,108]{2,1,0:T(8,128)S(1)} %collective-permute-done.other_ref) | copy-start | bytes 2654212
  38.9 18.1 %all-to-all-start.1 = ((f32[64,16,128]{2,1,0:T(8,128)}), f32[64,16,128]{2,1,0:T(8,128)S(1)}, u32[]{:S(2)}, u32[]{:S(2)}) async-start(f32[64,16,128]{2,1,0:T(8,128)} %get-tuple-element.31), calls=%async_computation.1 | async-start | bytes 1048576 | tf_op jit(solution)/shard_map/all_to_all | solution.py:334
  49.4 9.2 %copy-start.2 = (f32[108,16]{0,1:T(8,128)S(1)}, f32[108,16]{0,1:T(8,128)}, u32[]{:S(2)}) copy-start(f32[108,16]{0,1:T(8,128)} %param.4) | copy-start | bytes 20740
  49.4 9.2 %copy-start.3 = (f32[108,16]{0,1:T(8,128)S(1)}, f32[108,16]{0,1:T(8,128)}, u32[]{:S(2)}) copy-start(f32[108,16]{0,1:T(8,128)} %param.5) | copy-start | bytes 20740
  57.1 3.1 %collective-permute-start.1 = (f32[64,16,128]{2,1,0:T(8,128)S(1)}, f32[64,16,128]{2,1,0:T(8,128)S(1)}, u32[]{:S(2)}, u32[]{:S(2)}) collective-permute-start(f32[64,16,128]{2,1,0:T(8,128)S(1)} %all-to-all-done.1.own_ref), channel_id=1, source_target_pairs={{0,1},{1,0},{2,3},{3,2},{4,5},{5,4},{6,7},{7,6},{8,9},{9,8},{10,11... | collective-permute-start | bytes 1572872 | tf_op jit(solution)/shard_map/ppermute | solution.py:338
  71.4 18.7 %all-to-all-start.2 = ((f32[64,8,128]{2,1,0:T(8,128)}), f32[64,8,128]{2,1,0:T(8,128)S(1)}, u32[]{:S(2)}, u32[]{:S(2)}) async-start(f32[64,8,128]{2,1,0:T(8,128)} %get-tuple-element.38), calls=%async_computation.2 | async-start | bytes 524288 | tf_op jit(solution)/shard_map/all_to_all | solution.py:334
  90.1 1.8 %collective-permute-start.2 = (f32[64,8,128]{2,1,0:T(8,128)S(1)}, f32[64,8,128]{2,1,0:T(8,128)S(1)}, u32[]{:S(2)}, u32[]{:S(2)}) collective-permute-start(f32[64,8,128]{2,1,0:T(8,128)S(1)} %all-to-all-done.2.own_ref), channel_id=1, source_target_pairs={{0,1},{1,0},{2,3},{3,2},{4,5},{5,4},{6,7},{7,6},{8,9},{9,8},{10,11... | collective-permute-start | bytes 786440 | tf_op jit(solution)/shard_map/ppermute | solution.py:338

commit v4 on v3

--- a/solution.py
+++ b/solution.py
@@ -21,7 +21,8 @@
 CHUNK = HALF // CHUNKS
 EPS = 1e-06
 AXIS = "device"
-CHIP_ORDER = [[2 * chip + core for chip in reversed(range(CHIPS))] for core in range(2)]
+FORWARD = [[2 * chip + core for chip in range(CHIPS)] for core in range(2)]
+BACKWARD = [[2 * chip + core for chip in reversed(range(CHIPS))] for core in range(2)]
 F32, BF16 = jnp.float32, jnp.bfloat16
 HIGHEST = lax.Precision.HIGHEST
 VMEM = pl.BlockSpec(memory_space=pltpu.VMEM)
@@ -29,6 +30,7 @@
 LIMIT = 53 << 20
 LIMIT_IMAGE = 48 << 20
 LIMIT_SEARCH = 52 << 20
+LIMIT_OWN = 52 << 20
 PARTS = 2
 STACK = PARTS * NEIG
 SPARE = ROWS
@@ -83,40 +85,29 @@
     core = lax.rem(lax.axis_index(AXIS), 2)
     for block in range(2 * CHIPS // CHUNKS):
         chip, owner = divmod(block, 2)
-        place = CHIPS // CHUNKS - 1 - chip
         half = jnp.where(core == owner, 0, 1)
         x = padded(h_ref[:, ROWS * block : ROWS * block + ROWS])
         for number, part in enumerate(split(x)):
-            parts_ref[half, 0, TALL * number : TALL * number + ROWS, LANES * place : LANES * (place + 1)] = part
+            parts_ref[half, TALL * number : TALL * number + ROWS, LANES * chip : LANES * (chip + 1)] = part
 
 
 def prepare(hamiltonian):
     return pl.pallas_call(
         prepare_kernel,
         grid=(CHUNKS,),
-        out_shape=jax.ShapeDtypeStruct((2, CHUNKS, PARTS * TALL, CHUNK), BF16),
+        out_shape=jax.ShapeDtypeStruct((2, PARTS * TALL, HALF), BF16),
         in_specs=[pl.BlockSpec((ROWS, ORDER // CHUNKS), lambda i: (0, i))],
-        out_specs=pl.BlockSpec((2, 1, PARTS * TALL, CHUNK), lambda i: (0, CHUNKS - 1 - i, 0, 0)),
+        out_specs=pl.BlockSpec((2, PARTS * TALL, CHUNK), lambda i: (0, 0, i)),
         compiler_params=pltpu.CompilerParams(vmem_limit_bytes=58 << 20),
         cost_estimate=pl.CostEstimate(flops=20 * ROWS * ORDER, bytes_accessed=10 * ROWS * ORDER, transcendentals=0),
         name="prepare",
     )(hamiltonian)
 
 
-def half_copies(h_ref, h_vmem, half, sems):
-    copies = [pltpu.make_async_copy(h_ref.at[half, n], h_vmem.at[n], sems.at[n]) for n in range(CHUNKS)]
-    for copy in copies:
-        copy.start()
-    return copies
-
-
-def times(h_vmem, parts, copies):
-    product = None
-    for n, copy in enumerate(copies):
-        copy.wait()
-        term = nt(h_vmem[n], parts[:, CHUNK * n : CHUNK * (n + 1)])
-        product = term if product is None else product + term
-    return product
+def started(source, target, sem):
+    copy = pltpu.make_async_copy(source, target, sem)
+    copy.start()
+    return copy
 
 
 def take_parts(tile_of, parts_ref):
@@ -125,35 +116,36 @@
             parts_ref[NEIG * number : NEIG * (number + 1), LANES * chip : LANES * (chip + 1)] = part
 
 
-def image_own_kernel(h_ref, own_ref, product_ref, h_vmem, parts, sems):
-    copies = half_copies(h_ref, h_vmem, 0, sems)
-    take_parts(lambda chip: padded(own_ref[chip, 0:NEIG]), parts)
-    product_ref[...] = times(h_vmem, parts, copies)
-
-
-def image_other_kernel(h_ref, other_ref, product_ref, tile_ref, image_ref, sent_ref, h_vmem, parts, sems):
-    copies = half_copies(h_ref, h_vmem, 1, sems)
-    take_parts(lambda chip: padded(other_ref[chip, 0:NEIG]), parts)
-    image = fold_rows(product_ref[...] + times(h_vmem, parts, copies))
+def image_own_kernel(h_ref, own_ref, product_ref, h_vmem, parts, sem):
+    copy = started(h_ref.at[0], h_vmem, sem)
+    take_parts(lambda chip: padded(own_ref[CHIPS - 1 - chip, 0:NEIG]), parts)
+    copy.wait()
+    product_ref[...] = nt(h_vmem[...], parts[...])
+
+
+def image_other_kernel(h_ref, other_ref, product_ref, tile_ref, image_ref, sent_ref, h_vmem, parts, sem):
+    copy = started(h_ref.at[1], h_vmem, sem)
+    take_parts(lambda chip: padded(other_ref[CHIPS - 1 - chip, 0:NEIG]), parts)
+    copy.wait()
+    image = fold_rows(product_ref[...] + nt(h_vmem[...], parts[...]))
     image_ref[...] = image
     sent = image + tile_ref[...]
     for chip in range(CHIPS):
         sent_ref[chip] = sent
 
 
-def previous_kernel(h_ref, own_ref, other_ref, image_ref, c_out, p_out, gram_ref, h_vmem, c_ref, p_ref, sems, h_sems):
-    copies = [half_copies(h_ref, h_vmem.at[half], half, h_sems.at[half]) for half in range(2)]
+def previous_kernel(h_ref, own_ref, other_ref, image_ref, c_out, p_out, gram_ref, h_vmem, c_ref, p_ref, sems):
+    copy = started(h_ref, h_vmem, sems.at[0])
     for half, ref in ((0, own_ref), (1, other_ref)):
-        take_parts(lambda chip: padded(ref[chip, 0:NEIG]), c_ref.at[half])
-        take_parts(lambda chip: padded(ref[chip, NEIG : 2 * NEIG]), p_ref.at[half])
-    out_c = pltpu.make_async_copy(c_ref, c_out, sems.at[0])
-    out_p = pltpu.make_async_copy(p_ref, p_out, sems.at[1])
-    out_c.start()
-    out_p.start()
+        take_parts(lambda chip: padded(ref[CHIPS - 1 - chip, 0:NEIG]), c_ref.at[half])
+        take_parts(lambda chip: padded(ref[CHIPS - 1 - chip, NEIG : 2 * NEIG]), p_ref.at[half])
+    out_c = started(c_ref, c_out, sems.at[1])
+    out_p = started(p_ref, p_out, sems.at[2])
     gram_ref[0] = fold(nt(c_ref[0], c_ref[0]) + nt(c_ref[1], c_ref[1]))
     gram_ref[1] = fold(nt(p_ref[0], c_ref[0]) + nt(p_ref[1], c_ref[1]))
     gram_ref[2] = fold(nt(p_ref[0], p_ref[0]) + nt(p_ref[1], p_ref[1]))
-    image_ref[...] = fold_rows(times(h_vmem.at[0], p_ref[0], copies[0]) + times(h_vmem.at[1], p_ref[1], copies[1]))
+    copy.wait()
+    image_ref[...] = fold_rows(nt(h_vmem[0], p_ref[0]) + nt(h_vmem[1], p_ref[1]))
     out_c.wait()
     out_p.wait()
 
@@ -165,20 +157,28 @@
     return jnp.sum(jnp.where(lane % NEIG == row, spread, 0.0), axis=0, keepdims=True)
 
 
+def own_kernel(own_ref, c_hbm, i_ref, cross_ref, diag_ref, c_ref, sem):
+    copy = started(c_hbm.at[0], c_ref, sem)
+    take_parts(lambda chip: real_lanes(own_ref[chip]), i_ref)
+    for chip in range(CHIPS):
+        diag_ref[chip : chip + 1, :] = diagonal_of(own_ref[chip])
+    copy.wait()
+    cross_ref[...] = nt(i_ref[...], c_ref[...])
+
+
 def search_kernel(
-    h_ref, own_ref, other_ref, c_hbm, cvec_ref, pvec_ref, pimage_ref, image_ref, tile_ref,
-    search_ref, rms_ref, cross_ref, sent_ref, s_out, i_out,
-    h_vmem, c_ref, i_ref, s_ref, resid_ref, sems, h_sems,
+    h_ref, own_ref, other_ref, c_hbm, i_own_ref, half_cross_ref, diag_ref, cvec_ref, pvec_ref, pimage_ref, image_ref, tile_ref,
+    search_ref, rms_ref, cross_ref, sent_ref, kept_ref,
+    h_vmem, c_ref, i_ref, s_ref, resid_ref, other_diag_ref, sems,
 ):
-    copy_c = pltpu.make_async_copy(c_hbm, c_ref, sems.at[0])
-    copy_c.start()
-    copies = [half_copies(h_ref, h_vmem.at[half], half, h_sems.at[half]) for half in range(2)]
-    take_parts(lambda chip: real_lanes(own_ref[chip]), i_ref.at[0])
-    take_parts(lambda chip: real_lanes(other_ref[chip]), i_ref.at[1])
-    out_i = pltpu.make_async_copy(i_ref, i_out, sems.at[1])
-    out_i.start()
+    copy_c = started(c_hbm, c_ref, sems.at[3])
+    take_parts(lambda chip: real_lanes(other_ref[chip]), i_ref)
+    for chip in range(CHIPS):
+        other_diag_ref[chip : chip + 1, :] = diagonal_of(other_ref[chip])
     copy_c.wait()
-    cross_t = fold(nt(i_ref[0], c_ref[0]) + nt(i_ref[1], c_ref[1]))
+    copy_h = started(h_ref, h_vmem, sems.at[0])
+    kept = [started(i_own_ref, kept_ref.at[2], sems.at[1]), started(i_ref, kept_ref.at[3], sems.at[2])]
+    cross_t = fold(half_cross_ref[...] + nt(i_ref[...], c_ref[1]))
     cross_ref[...] = cross_t
     ritz_t = cross_t / ORDER
     stacked = jnp.concatenate(split3(ritz_t), axis=0)
@@ -202,17 +202,20 @@
     value = jnp.broadcast_to(value, (NEIG, LANES))
     rms = jnp.broadcast_to(rms, (NEIG, LANES))
 
-    def scaled(resid, tile):
-        return resid / (jnp.maximum(jnp.abs(diagonal_of(tile) - value), 1.0) * rms)
+    def scaled(resid, diag):
+        return resid / (jnp.maximum(jnp.abs(diag - value), 1.0) * rms)
 
     resid = image_ref[...] - dot_exact(ritz_t, cvec_ref[...])
-    search = scaled(resid, tile_ref[...])
+    search = scaled(resid, diagonal_of(tile_ref[...]))
     search_ref[...] = search
-    for half, ref in ((0, own_ref), (1, other_ref)):
-        take_parts(lambda chip: scaled(resid_ref[half, :, LANES * chip : LANES * (chip + 1)], ref[chip]), s_ref.at[half])
-    out_s = pltpu.make_async_copy(s_ref, s_out, sems.at[2])
-    out_s.start()
-    simage = fold_rows(times(h_vmem.at[0], s_ref[0], copies[0]) + times(h_vmem.at[1], s_ref[1], copies[1]))
+    for half, diag in ((0, diag_ref), (1, other_diag_ref)):
+        take_parts(
+            lambda chip: scaled(resid_ref[half, :, LANES * chip : LANES * (chip + 1)], diag[chip : chip + 1, :]),
+            s_ref.at[half],
+        )
+    kept.append(started(s_ref, kept_ref.at[pl.ds(0, 2)], sems.at[4]))
+    copy_h.wait()
+    simage = fold_rows(nt(h_vmem[0], s_ref[0]) + nt(h_vmem[1], s_ref[1]))
     pvec = pvec_ref[...]
     terms = jnp.concatenate(
         [nt_exact(simage, search), nt_exact(simage, pvec), nt_exact(pimage_ref[...], pvec), jnp.zeros((NEIG, NEIG), F32)],
@@ -221,19 +224,16 @@
     packed = jnp.concatenate([terms[0:8], terms[8:16]], axis=1)
     for chip in range(CHIPS):
         sent_ref[chip] = packed
-    out_s.wait()
-    out_i.wait()
+    for copy in kept:
+        copy.wait()
 
 
 def factor_kernel(
-    s_hbm, c_hbm, p_hbm, i_hbm, gram_ref, cross_ref, inverse_ref, stiff_ref,
-    s_ref, c_ref, p_ref, i_ref, sems,
+    kept_hbm, c_hbm, p_hbm, gram_ref, cross_ref, inverse_ref, stiff_ref, kept_ref, c_ref, p_ref, sems,
 ):
-    pairs = ((s_hbm, s_ref), (c_hbm, c_ref), (p_hbm, p_ref), (i_hbm, i_ref))
-    copies = [pltpu.make_async_copy(a, b, sems.at[n]) for n, (a, b) in enumerate(pairs)]
-    for copy in copies:
-        copy.start()
-    for copy in copies:
+    pairs = ((kept_hbm, kept_ref), (c_hbm, c_ref), (p_hbm, p_ref))
+    s_ref, i_ref = kept_ref.at[pl.ds(0, 2)], kept_ref.at[pl.ds(2, 2)]
+    for copy in [started(a, b, sems.at[n]) for n, (a, b) in enumerate(pairs)]:
         copy.wait()
 
     def gram(left, right):
@@ -330,8 +330,8 @@
     )(*args)
 
 
-def to_chips(x):
-    return lax.all_to_all(x, AXIS, 0, 0, axis_index_groups=CHIP_ORDER, tiled=True)
+def to_chips(x, groups):
+    return lax.all_to_all(x, AXIS, 0, 0, axis_index_groups=groups, tiled=True)
 
 
 def to_core(x):
@@ -350,51 +350,59 @@
 
 def body(hamiltonian, current, previous):
     both = jnp.concatenate([current.T, previous.T], axis=0)
-    v_own = to_chips(jnp.broadcast_to(both[None], (CHIPS, 2 * NEIG, ROWS)))
+    v_own = to_chips(jnp.broadcast_to(both[None], (CHIPS, 2 * NEIG, ROWS)), BACKWARD)
     tile = diagonal_tile(hamiltonian)
     cvec = jnp.pad(current.T, ((0, 0), (0, LANES - ROWS)))
     pvec = jnp.pad(previous.T, ((0, 0), (0, LANES - ROWS)))
     h_parts = prepare(hamiltonian)
     v_own, h_parts, tile = lax.optimization_barrier((v_own, h_parts, tile))
     v_other = to_core(v_own)
-    block, parts = ((NEIG, LANES), F32), ((2, STACK, HALF), BF16)
-    parts_vmem, half_vmem = pltpu.VMEM(*parts), pltpu.VMEM((STACK, HALF), BF16)
-    h_vmem = pltpu.VMEM((2, CHUNKS, PARTS * TALL, CHUNK), BF16)
-    h_half = pltpu.VMEM((CHUNKS, PARTS * TALL, CHUNK), BF16)
+    block, parts, half = ((NEIG, LANES), F32), ((2, STACK, HALF), BF16), ((STACK, HALF), BF16)
+    parts_vmem, half_vmem = pltpu.VMEM(*parts), pltpu.VMEM(*half)
+    h_vmem = pltpu.VMEM((2, PARTS * TALL, HALF), BF16)
+    h_half = pltpu.VMEM((PARTS * TALL, HALF), BF16)
     dma = pltpu.SemaphoreType.DMA
     (product,) = kernel_call(
         image_own_kernel, [((PARTS * TALL, STACK), F32)], (h_parts, v_own), 1 << 30, "image_own",
-        [h_half, half_vmem, dma((CHUNKS,))], (0,), limit=LIMIT_IMAGE,
+        [h_half, half_vmem, dma(())], (0,), limit=LIMIT_IMAGE,
     )
     image, sent = kernel_call(
         image_other_kernel, [block, ((CHIPS, NEIG, LANES), F32)], (h_parts, v_other, product, tile), 1 << 30, "image_other",
-        [h_half, half_vmem, dma((CHUNKS,))], (0,), limit=LIMIT_IMAGE,
-    )
-    i_own = to_chips(sent)
+        [h_half, half_vmem, dma(())], (0,), limit=LIMIT_IMAGE,
+    )
+    i_own = to_chips(sent, FORWARD)
     p_image, c_parts, p_parts, grams = kernel_call(
         previous_kernel,
         [block, parts, parts, ((3, NEIG, NEIG), F32)],
         (h_parts, v_own, v_other),
         6 << 30,
         "previous",
-        [h_vmem, parts_vmem, parts_vmem, dma((2,)), dma((2, CHUNKS))], (0,), (1, 2),
+        [h_vmem, parts_vmem, parts_vmem, dma((3,))], (0,), (1, 2),
     )
     i_own, p_image, c_parts = lax.optimization_barrier((i_own, p_image, c_parts))
     i_other = to_core(i_own)
-    search, rms, cross, sent, s_parts, i_parts = kernel_call(
+    i_own_parts, half_cross, diag = kernel_call(
+        own_kernel,
+        [half, ((STACK, STACK), F32), ((CHIPS, LANES), F32)],
+        (i_own, c_parts),
+        1 << 30,
+        "own",
+        [half_vmem, dma(())], (1,), limit=LIMIT_OWN,
+    )
+    search, rms, cross, sent, kept = kernel_call(
         search_kernel,
-        [block, ((NEIG, 1), F32), ((NEIG, NEIG), F32), ((CHIPS, 8, LANES), F32), parts, parts],
-        (h_parts, i_own, i_other, c_parts, cvec, pvec, p_image, image, tile),
+        [block, ((NEIG, 1), F32), ((NEIG, NEIG), F32), ((CHIPS, 8, LANES), F32), ((4, STACK, HALF), BF16)],
+        (h_parts, i_own, i_other, c_parts, i_own_parts, half_cross, diag, cvec, pvec, p_image, image, tile),
         6 << 30,
         "search",
-        [h_vmem, parts_vmem, parts_vmem, parts_vmem, pltpu.VMEM((2, NEIG, HALF), F32), dma((3,)), dma((2, CHUNKS))],
-        (0, 3), (4, 5), limit=LIMIT_SEARCH,
-    )
-    r_own = to_chips(sent)
+        [h_vmem, parts_vmem, half_vmem, parts_vmem, pltpu.VMEM((2, NEIG, HALF), F32), pltpu.VMEM((CHIPS, LANES), F32), dma((5,))],
+        (0, 3), (4,), limit=LIMIT_SEARCH,
+    )
+    r_own = to_chips(sent, FORWARD)
     square = ((3 * NEIG, 3 * NEIG), F32)
     inverse, stiff = kernel_call(
-        factor_kernel, [square, square], (s_parts, c_parts, p_parts, i_parts, grams, cross), 6 << 30, "factor",
-        [parts_vmem] * 4 + [dma((4,))], (0, 1, 2, 3),
+        factor_kernel, [square, square], (kept, c_parts, p_parts, grams, cross), 6 << 30, "factor",
+        [pltpu.VMEM((4, STACK, HALF), BF16), parts_vmem, parts_vmem, dma((3,))], (0, 1, 2),
     )
     r_own, inverse, rms = lax.optimization_barrier((r_own, inverse, rms[:, 0]))
     r_other = to_core(r_own)

time: 96.2 us -> 94.2 us (0.979)
  starting transfers between devices: 37.9 us -> 31.9 us
  waiting for transfers between devices: 6.04 us -> 10.5 us
    all_to_all x3, starting transfers between devices: 34.1 us -> 26.9 us  [to_chips(): return lax.all_to_all(x, AXIS, 0, 0, axis_index_groups=groups, tiled=True)]
    all_to_all x3, waiting for transfers between devices: 3.36 us -> 9.13 us  [to_chips(): return lax.all_to_all(x, AXIS, 0, 0, axis_index_groups=groups, tiled=True)]
    ppermute x3, waiting for transfers between devices: 2.68 us -> 1.34 us  [to_core(): lax.ppermute(x, AXIS, [(device, device ^ 1) for device in range(DEVICES)])]
    ppermute x3, starting transfers between devices: 3.8 us -> 4.97 us  [to_core(): lax.ppermute(x, AXIS, [(device, device ^ 1) for device in range(DEVICES)])]
    pallas_call x6 -> x7, Pallas kernels: 39.2 us -> 38.6 us  [kernel_call(): pl.pallas_call(body, out_shape=[jax.ShapeDtypeStruct(shape, kind) for sha...]
  transfers between devices with their start and end apart: 6 -> 6, of which waited for: 3 -> 5; matrix products, arithmetic and copies ran while one was open for 2% -> 2% of each run, Pallas kernels for 29% -> 30%
where the time goes in v4:
time: 94.2 us; the launch traced here: 93.4 us
  Pallas kernels  46.6 us (49%)
  starting transfers between devices  31.9 us (34%)
  waiting for transfers between devices  10.5 us (11%)
  other arithmetic  2.36 us (3%)
  local copies, waits for them, and re-layouts  1.17 us (1%)
    pallas_call x7, Pallas kernels, kernel_call(): pl.pallas_call(body, out_shape=[jax.ShapeDtypeStruct(shape, kind) for sha...  38.6 us
    all_to_all x3, starting transfers between devices, to_chips(): return lax.all_to_all(x, AXIS, 0, 0, axis_index_groups=groups, tiled=True)  26.9 us
    all_to_all x3, waiting for transfers between devices, to_chips(): return lax.all_to_all(x, AXIS, 0, 0, axis_index_groups=groups, tiled=True)  9.13 us
    pallas_call x1, Pallas kernels, prepare(): pl.pallas_call(prepare_kernel, grid=(CHUNKS,), out_shape=jax.ShapeDtypeSt...  8.01 us
    ppermute x3, starting transfers between devices, to_core(): lax.ppermute(x, AXIS, [(device, device ^ 1) for device in range(DEVICES)])  4.97 us
  transfers between devices with their start and end apart: 6, of which 5 were waited for; matrix products, arithmetic and copies ran while one was open for 2% of the time, Pallas kernels for 30%

profile of v4, /device:TPU:1, one launch (start us, length us, event | category | flops | bytes accessed | tf_op | source)
XLA Modules:
  0.0 93.4 jit_solution(1513094969446987450)
XLA Ops:
  0.6 0.7 pad_maximum_fusion
  1.4 1.1 %broadcast_in_dim.14 = f32[64,32,108]{2,1,0:T(8,128)} broadcast(f32[32,108]{1,0:T(8,128)S(1)} %pad_maximum_fusion), dimensions={1,2} | broadcast | bytes 898560 | tf_op jit(solution)/shard_map/broadcast_in_dim | solution.py:353
  2.5 13.7 %all-to-all-start = ((f32[64,32,108]{2,1,0:T(8,128)}), f32[64,32,108]{2,1,0:T(8,128)S(1)}, u32[]{:S(2)}, u32[]{:S(2)}) async-start(f32[64,32,108]{2,1,0:T(8,128)} %broadcast_in_dim.14), calls=%async_computation | async-start | bytes 2097152 | tf_op jit(solution)/shard_map/all_to_all | solution.py:334
  16.2 1.0 %select_reduce_fusion = f32[108]{0:T(128)S(1)} fusion(f32[108,13824]{1,0:T(8,128)} %h_ref.1, s32[]{:T(128)S(6)} %select_n.34), kind=kLoop, calls=%fused_computation.1 | loop fusion | flops 34884 | bytes 47092 | tf_op jit(solution)/shard_map/reduce_sum | solution.py:345
  17.3 8.0 %prepare.1.h_ref = bf16[2,224,8192]{2,1,0:T(8,128)(2,1)} custom-call(f32[108,13824]{1,0:T(8,128)} %h_ref.1), custom_call_target="tpu_custom_call" | custom-call | flops 29859840 | bytes 14929920 | tf_op jit(solution)/shard_map/prepare/pallas_call | solution.py:95
  25.3 0.2 fusion.tile_ref
  25.5 3.3 %all-to-all-done.own_ref = f32[64,32,108]{2,1,0:T(8,128)S(1)} async-done(((f32[64,32,108]{2,1,0:T(8,128)}), f32[64,32,108]{2,1,0:T(8,128)S(1)}, u32[]{:S(2)}, u32[]{:S(2)}) %all-to-all-start) | async-done | bytes 884768 | tf_op jit(solution)/shard_map/all_to_all | solution.py:334
  28.8 1.6 %collective-permute-start = (f32[64,32,108]{2,1,0:T(8,128)S(1)}, f32[64,32,108]{2,1,0:T(8,128)S(1)}, u32[]{:S(2)}, u32[]{:S(2)}) collective-permute-start(f32[64,32,108]{2,1,0:T(8,128)S(1)} %all-to-all-done.own_ref), channel_id=1, source_target_pairs={{0,1},{1,0},{2,3},{3,2},{4,5},{5,4},{6,7},{7,6},{8,9},{9,8},{10,11... | collective-permute-start | bytes 2654216 | tf_op jit(solution)/shard_map/ppermute | solution.py:338
  30.3 3.1 %image_own.1.product_ref = f32[224,32]{1,0:T(8,128)S(1)} custom-call(bf16[2,224,8192]{2,1,0:T(8,128)(2,1)} %prepare.1.h_ref, f32[64,32,108]{2,1,0:T(8,128)S(1)} %all-to-all-done.own_ref), custom_call_target="tpu_custom_call" | custom-call | flops 1073741824 | bytes 4194304 | tf_op jit(solution)/shard_map/image_own/pallas_call | solution.py:321
  33.5 4.4 %image_other.1 = (f32[16,128]{1,0:T(8,128)S(1)}, f32[64,16,128]{2,1,0:T(8,128)}) custom-call(bf16[2,224,8192]{2,1,0:T(8,128)(2,1)} %prepare.1.h_ref, f32[64,32,108]{2,1,0:T(8,128)S(1)} %collective-permute-done.other_ref, f32[224,32]{1,0:T(8,128)S(1)} %image_own.1.product_ref, f32[16,128]{1,0:T(8,128)S(1)} %fusion.tile_ref), custom_call_target="tpu_custom_call" | custom-call | flops 1073741824 | bytes 4194304 | tf_op jit(solution)/shard_map/image_other/pallas_call | solution.py:321
  37.9 8.4 %all-to-all-start.1 = ((f32[64,16,128]{2,1,0:T(8,128)}), f32[64,16,128]{2,1,0:T(8,128)S(1)}, u32[]{:S(2)}, u32[]{:S(2)}) async-start(f32[64,16,128]{2,1,0:T(8,128)} %get-tuple-element.33), calls=%async_computation.1 | async-start | bytes 1048576 | tf_op jit(solution)/shard_map/all_to_all | solution.py:334
  46.3 7.8 %previous.1 = (f32[16,128]{1,0:T(8,128)S(1)}, bf16[2,32,8192]{2,1,0:T(8,128)(2,1)}, bf16[2,32,8192]{2,1,0:T(8,128)(2,1)}, f32[3,16,16]{2,1,0:T(8,128)S(1)}) custom-call(bf16[2,224,8192]{2,1,0:T(8,128)(2,1)} %prepare.1.h_ref, f32[64,32,108]{2,1,0:T(8,128)} %copy-done, f32[64,32,108]{2,1,0:T(8,128)} %copy-done.1), custom_call_target="tpu_custom_call" | custom-call | flops 6442450944 | bytes 4194304 | tf_op jit(solution)/shard_map/previous/pallas_call | solution.py:321
  54.1 4.6 %all-to-all-done.1.own_ref = f32[64,16,128]{2,1,0:T(8,128)S(1)} async-done(((f32[64,16,128]{2,1,0:T(8,128)}), f32[64,16,128]{2,1,0:T(8,128)S(1)}, u32[]{:S(2)}, u32[]{:S(2)}) %all-to-all-start.1) | async-done | bytes 524320 | tf_op jit(solution)/shard_map/all_to_all | solution.py:334
  58.7 2.0 %collective-permute-start.1 = (f32[64,16,128]{2,1,0:T(8,128)S(1)}, f32[64,16,128]{2,1,0:T(8,128)S(1)}, u32[]{:S(2)}, u32[]{:S(2)}) collective-permute-start(f32[64,16,128]{2,1,0:T(8,128)S(1)} %all-to-all-done.1.own_ref), channel_id=1, source_target_pairs={{0,1},{1,0},{2,3},{3,2},{4,5},{5,4},{6,7},{7,6},{8,9},{9,8},{10,11... | collective-permute-start | bytes 1572872 | tf_op jit(solution)/shard_map/ppermute | solution.py:338
  60.7 1.3 %own.1 = (bf16[32,8192]{1,0:T(8,128)(2,1)S(1)}, f32[32,32]{1,0:T(8,128)S(1)}, f32[64,128]{1,0:T(8,128)S(1)}) custom-call(f32[64,16,128]{2,1,0:T(8,128)S(1)} %all-to-all-done.1.own_ref, bf16[2,32,8192]{2,1,0:T(8,128)(2,1)} %get-tuple-element.37.c_hbm), custom_call_target="tpu_custom_call" | custom-call | flops 1073741824 | bytes 4194304 | tf_op jit(solution)/shard_map/own/pallas_call | solution.py:321
  62.1 0.2 collective-permute-done.1.other_ref
  62.2 10.1 %search.1 = (f32[16,128]{1,0:T(8,128)S(1)}, f32[16,1]{1,0:T(8,128)S(1)}, f32[16,16]{1,0:T(8,128)S(1)}, f32[64,8,128]{2,1,0:T(8,128)}, bf16[4,32,8192]{2,1,0:T(8,128)(2,1)}) custom-call(bf16[2,224,8192]{2,1,0:T(8,128)(2,1)} %prepare.1.h_ref, f32[64,16,128]{2,1,0:T(8,128)S(1)} %all-to-all-done.1.own_ref, f32[64,16,128]{2,1,0:T(8,128)S(1)} %collective-permute-done.1.other_ref, ...), custom_call_target="tpu_custom_call" | custom-call | flops 6442450944 | bytes 4194304 | tf_op jit(solution)/shard_map/search/pallas_call | solution.py:321
  72.4 4.8 %all-to-all-start.2 = ((f32[64,8,128]{2,1,0:T(8,128)}), f32[64,8,128]{2,1,0:T(8,128)S(1)}, u32[]{:S(2)}, u32[]{:S(2)}) async-start(f32[64,8,128]{2,1,0:T(8,128)} %get-tuple-element.43), calls=%async_computation.2 | async-start | bytes 524288 | tf_op jit(solution)/shard_map/all_to_all | solution.py:334
  77.2 8.1 %factor.1 = (f32[48,48]{1,0:T(8,128)S(1)}, f32[48,48]{1,0:T(8,128)S(1)}) custom-call(bf16[4,32,8192]{2,1,0:T(8,128)(2,1)} %get-tuple-element.44.kept_hbm, bf16[2,32,8192]{2,1,0:T(8,128)(2,1)} %get-tuple-element.37.c_hbm, bf16[2,32,8192]{2,1,0:T(8,128)(2,1)} %get-tuple-element.45.p_hbm, f32[3,16,16]{2,1,0:T(8,128)S(1)} %get-tuple-element.46.gram_ref, ...), custom_call_target="tpu_custom_call" | custom-call | flops 6442450944 | bytes 4194304 | tf_op jit(solution)/shard_map/factor/pallas_call | solution.py:321
  85.3 0.6 reduce
  85.9 1.2 %all-to-all-done.2.own_ref = f32[64,8,128]{2,1,0:T(8,128)S(1)} async-done(((f32[64,8,128]{2,1,0:T(8,128)}), f32[64,8,128]{2,1,0:T(8,128)S(1)}, u32[]{:S(2)}, u32[]{:S(2)}) %all-to-all-start.2) | async-done | bytes 262176 | tf_op jit(solution)/shard_map/all_to_all | solution.py:334
  87.1 1.4 %collective-permute-start.2 = (f32[64,8,128]{2,1,0:T(8,128)S(1)}, f32[64,8,128]{2,1,0:T(8,128)S(1)}, u32[]{:S(2)}, u32[]{:S(2)}) collective-permute-start(f32[64,8,128]{2,1,0:T(8,128)S(1)} %all-to-all-done.2.own_ref), channel_id=1, source_target_pairs={{0,1},{1,0},{2,3},{3,2},{4,5},{5,4},{6,7},{7,6},{8,9},{9,8},{10,11... | collective-permute-start | bytes 786440 | tf_op jit(solution)/shard_map/ppermute | solution.py:338
  88.6 1.2 %collective-permute-done.2.other_ref = f32[64,8,128]{2,1,0:T(8,128)S(1)} collective-permute-done((f32[64,8,128]{2,1,0:T(8,128)S(1)}, f32[64,8,128]{2,1,0:T(8,128)S(1)}, u32[]{:S(2)}, u32[]{:S(2)}) %collective-permute-start.2) | collective-permute-done | bytes 262176 | tf_op jit(solution)/shard_map/ppermute | solution.py:338
  89.7 3.7 %finish.1 = (f32[16,108]{1,0:T(8,128)}, f32[16,108]{1,0:T(8,128)}) custom-call(f32[48,48]{1,0:T(8,128)S(1)} %get-tuple-element.50.inverse_ref, f32[48,48]{1,0:T(8,128)S(1)} %get-tuple-element.51.stiff_ref, f32[64,8,128]{2,1,0:T(8,128)S(1)} %all-to-all-done.2.own_ref, f32[64,8,128]{2,1,0:T(8,128)S(1)} %collective-permute-done.2.other_ref, ...), custom_call_target="tpu_custom_call" | custom-call | flops 268435456 | bytes 4194304 | tf_op jit(solution)/shard_map/finish/pallas_call | solution.py:321
  (12 shorter events, 0.0 us)
Async XLA Ops:
  2.5 26.3 %all-to-all-start = ((f32[64,32,108]{2,1,0:T(8,128)}), f32[64,32,108]{2,1,0:T(8,128)S(1)}, u32[]{:S(2)}, u32[]{:S(2)}) async-start(f32[64,32,108]{2,1,0:T(8,128)} %broadcast_in_dim.14), calls=%async_computation | async-start | bytes 2097152 | tf_op jit(solution)/shard_map/all_to_all | solution.py:334
  28.8 9.1 %copy-start = (f32[64,32,108]{2,1,0:T(8,128)}, f32[64,32,108]{2,1,0:T(8,128)S(1)}, u32[]{:S(2)}) copy-start(f32[64,32,108]{2,1,0:T(8,128)S(1)} %all-to-all-done.own_ref) | copy-start | bytes 2654212
  28.8 4.7 %collective-permute-start = (f32[64,32,108]{2,1,0:T(8,128)S(1)}, f32[64,32,108]{2,1,0:T(8,128)S(1)}, u32[]{:S(2)}, u32[]{:S(2)}) collective-permute-start(f32[64,32,108]{2,1,0:T(8,128)S(1)} %all-to-all-done.own_ref), channel_id=1, source_target_pairs={{0,1},{1,0},{2,3},{3,2},{4,5},{5,4},{6,7},{7,6},{8,9},{9,8},{10,11... | collective-permute-start | bytes 2654216 | tf_op jit(solution)/shard_map/ppermute | solution.py:338
  33.5 12.8 %copy-start.1 = (f32[64,32,108]{2,1,0:T(8,128)}, f32[64,32,108]{2,1,0:T(8,128)S(1)}, u32[]{:S(2)}) copy-start(f32[64,32,108]{2,1,0:T(8,128)S(1)} %collective-permute-done.other_ref) | copy-start | bytes 2654212
  37.9 20.8 %all-to-all-start.1 = ((f32[64,16,128]{2,1,0:T(8,128)}), f32[64,16,128]{2,1,0:T(8,128)S(1)}, u32[]{:S(2)}, u32[]{:S(2)}) async-start(f32[64,16,128]{2,1,0:T(8,128)} %get-tuple-element.33), calls=%async_computation.1 | async-start | bytes 1048576 | tf_op jit(solution)/shard_map/all_to_all | solution.py:334
  46.3 14.4 %copy-start.2 = (f32[108,16]{0,1:T(8,128)S(1)}, f32[108,16]{0,1:T(8,128)}, u32[]{:S(2)}) copy-start(f32[108,16]{0,1:T(8,128)} %param.4) | copy-start | bytes 20740
  46.3 14.4 %copy-start.3 = (f32[108,16]{0,1:T(8,128)S(1)}, f32[108,16]{0,1:T(8,128)}, u32[]{:S(2)}) copy-start(f32[108,16]{0,1:T(8,128)} %param.5) | copy-start | bytes 20740
  58.7 3.5 %collective-permute-start.1 = (f32[64,16,128]{2,1,0:T(8,128)S(1)}, f32[64,16,128]{2,1,0:T(8,128)S(1)}, u32[]{:S(2)}, u32[]{:S(2)}) collective-permute-start(f32[64,16,128]{2,1,0:T(8,128)S(1)} %all-to-all-done.1.own_ref), channel_id=1, source_target_pairs={{0,1},{1,0},{2,3},{3,2},{4,5},{5,4},{6,7},{7,6},{8,9},{9,8},{10,11... | collective-permute-start | bytes 1572872 | tf_op jit(solution)/shard_map/ppermute | solution.py:338
  72.4 14.7 %all-to-all-start.2 = ((f32[64,8,128]{2,1,0:T(8,128)}), f32[64,8,128]{2,1,0:T(8,128)S(1)}, u32[]{:S(2)}, u32[]{:S(2)}) async-start(f32[64,8,128]{2,1,0:T(8,128)} %get-tuple-element.43), calls=%async_computation.2 | async-start | bytes 524288 | tf_op jit(solution)/shard_map/all_to_all | solution.py:334
  87.1 2.6 %collective-permute-start.2 = (f32[64,8,128]{2,1,0:T(8,128)S(1)}, f32[64,8,128]{2,1,0:T(8,128)S(1)}, u32[]{:S(2)}, u32[]{:S(2)}) collective-permute-start(f32[64,8,128]{2,1,0:T(8,128)S(1)} %all-to-all-done.2.own_ref), channel_id=1, source_target_pairs={{0,1},{1,0},{2,3},{3,2},{4,5},{5,4},{6,7},{7,6},{8,9},{9,8},{10,11... | collective-permute-start | bytes 786440 | tf_op jit(solution)/shard_map/ppermute | solution.py:338

commit v5 on v4

--- a/solution.py
+++ b/solution.py
@@ -15,14 +15,17 @@
 ROWS = ORDER // DEVICES
 CHIPS = DEVICES // 2
 LANES = 128
+FORWARD = list(range(CHIPS))
+BACKWARD = FORWARD[::-1]
+ORDERS = (BACKWARD, BACKWARD, FORWARD)
+SLOTS = [[order.index(chip) for chip in range(CHIPS)] for order in ORDERS]
 HALF = CHIPS * LANES
 TALL = 112
 CHUNKS = 4
 CHUNK = HALF // CHUNKS
 EPS = 1e-06
 AXIS = "device"
-FORWARD = [[2 * chip + core for chip in range(CHIPS)] for core in range(2)]
-BACKWARD = [[2 * chip + core for chip in reversed(range(CHIPS))] for core in range(2)]
+
 F32, BF16 = jnp.float32, jnp.bfloat16
 HIGHEST = lax.Precision.HIGHEST
 VMEM = pl.BlockSpec(memory_space=pltpu.VMEM)
@@ -116,18 +119,18 @@
             parts_ref[NEIG * number : NEIG * (number + 1), LANES * chip : LANES * (chip + 1)] = part
 
 
-def image_own_kernel(h_ref, own_ref, product_ref, h_vmem, parts, sem):
-    copy = started(h_ref.at[0], h_vmem, sem)
-    take_parts(lambda chip: padded(own_ref[CHIPS - 1 - chip, 0:NEIG]), parts)
+def image_own_kernel(h_ref, own_ref, product_ref, next_ref, h_vmem, parts, sems):
+    copy = started(h_ref.at[0], h_vmem, sems.at[0])
+    following = started(h_ref.at[1], next_ref, sems.at[1])
+    take_parts(lambda chip: padded(own_ref[SLOTS[0][chip], 0:NEIG]), parts)
     copy.wait()
     product_ref[...] = nt(h_vmem[...], parts[...])
-
-
-def image_other_kernel(h_ref, other_ref, product_ref, tile_ref, image_ref, sent_ref, h_vmem, parts, sem):
-    copy = started(h_ref.at[1], h_vmem, sem)
-    take_parts(lambda chip: padded(other_ref[CHIPS - 1 - chip, 0:NEIG]), parts)
-    copy.wait()
-    image = fold_rows(product_ref[...] + nt(h_vmem[...], parts[...]))
+    following.wait()
+
+
+def image_other_kernel(h_ref, other_ref, product_ref, tile_ref, image_ref, sent_ref, parts):
+    take_parts(lambda chip: padded(other_ref[SLOTS[0][chip], 0:NEIG]), parts)
+    image = fold_rows(product_ref[...] + nt(h_ref[...], parts[...]))
     image_ref[...] = image
     sent = image + tile_ref[...]
     for chip in range(CHIPS):
@@ -137,8 +140,8 @@
 def previous_kernel(h_ref, own_ref, other_ref, image_ref, c_out, p_out, gram_ref, h_vmem, c_ref, p_ref, sems):
     copy = started(h_ref, h_vmem, sems.at[0])
     for half, ref in ((0, own_ref), (1, other_ref)):
-        take_parts(lambda chip: padded(ref[CHIPS - 1 - chip, 0:NEIG]), c_ref.at[half])
-        take_parts(lambda chip: padded(ref[CHIPS - 1 - chip, NEIG : 2 * NEIG]), p_ref.at[half])
+        take_parts(lambda chip: padded(ref[SLOTS[0][chip], 0:NEIG]), c_ref.at[half])
+        take_parts(lambda chip: padded(ref[SLOTS[0][chip], NEIG : 2 * NEIG]), p_ref.at[half])
     out_c = started(c_ref, c_out, sems.at[1])
     out_p = started(p_ref, p_out, sems.at[2])
     gram_ref[0] = fold(nt(c_ref[0], c_ref[0]) + nt(c_ref[1], c_ref[1]))
@@ -159,9 +162,9 @@
 
 def own_kernel(own_ref, c_hbm, i_ref, cross_ref, diag_ref, c_ref, sem):
     copy = started(c_hbm.at[0], c_ref, sem)
-    take_parts(lambda chip: real_lanes(own_ref[chip]), i_ref)
+    take_parts(lambda chip: real_lanes(own_ref[SLOTS[1][chip]]), i_ref)
     for chip in range(CHIPS):
-        diag_ref[chip : chip + 1, :] = diagonal_of(own_ref[chip])
+        diag_ref[chip : chip + 1, :] = diagonal_of(own_ref[SLOTS[1][chip]])
     copy.wait()
     cross_ref[...] = nt(i_ref[...], c_ref[...])
 
@@ -169,14 +172,14 @@
 def search_kernel(
     h_ref, own_ref, other_ref, c_hbm, i_own_ref, half_cross_ref, diag_ref, cvec_ref, pvec_ref, pimage_ref, image_ref, tile_ref,
     search_ref, rms_ref, cross_ref, sent_ref, kept_ref,
-    h_vmem, c_ref, i_ref, s_ref, resid_ref, other_diag_ref, sems,
+    h_vmem, c_ref, i_ref, s_ref, resid_ref, other_diag_ref, sems, h_sems,
 ):
     copy_c = started(c_hbm, c_ref, sems.at[3])
-    take_parts(lambda chip: real_lanes(other_ref[chip]), i_ref)
+    copies = [started(h_ref.at[half], h_vmem.at[half], h_sems.at[half]) for half in range(2)]
+    take_parts(lambda chip: real_lanes(other_ref[SLOTS[1][chip]]), i_ref)
     for chip in range(CHIPS):
-        other_diag_ref[chip : chip + 1, :] = diagonal_of(other_ref[chip])
+        other_diag_ref[chip : chip + 1, :] = diagonal_of(other_ref[SLOTS[1][chip]])
     copy_c.wait()
-    copy_h = started(h_ref, h_vmem, sems.at[0])
     kept = [started(i_own_ref, kept_ref.at[2], sems.at[1]), started(i_ref, kept_ref.at[3], sems.at[2])]
     cross_t = fold(half_cross_ref[...] + nt(i_ref[...], c_ref[1]))
     cross_ref[...] = cross_t
@@ -190,7 +193,7 @@
         part = jnp.zeros((NEIG, LANES), F32)
         for chip in range(CHIPS):
             lanes = slice(LANES * chip, LANES * (chip + 1))
-            resid = real_lanes(ref[chip]) - moved[:, lanes]
+            resid = real_lanes(ref[SLOTS[1][chip]]) - moved[:, lanes]
             resid_ref[half, :, lanes] = resid
             part = part + resid * resid
         square = square + part
@@ -213,9 +216,11 @@
             lambda chip: scaled(resid_ref[half, :, LANES * chip : LANES * (chip + 1)], diag[chip : chip + 1, :]),
             s_ref.at[half],
         )
-    kept.append(started(s_ref, kept_ref.at[pl.ds(0, 2)], sems.at[4]))
-    copy_h.wait()
-    simage = fold_rows(nt(h_vmem[0], s_ref[0]) + nt(h_vmem[1], s_ref[1]))
+    kept.append(started(s_ref, kept_ref.at[pl.ds(0, 2)], sems.at[0]))
+    copies[0].wait()
+    product = nt(h_vmem[0], s_ref[0])
+    copies[1].wait()
+    simage = fold_rows(product + nt(h_vmem[1], s_ref[1]))
     pvec = pvec_ref[...]
     terms = jnp.concatenate(
         [nt_exact(simage, search), nt_exact(simage, pvec), nt_exact(pimage_ref[...], pvec), jnp.zeros((NEIG, NEIG), F32)],
@@ -330,7 +335,8 @@
     )(*args)
 
 
-def to_chips(x, groups):
+def to_chips(x, number):
+    groups = [[2 * chip + core for chip in ORDERS[number]] for core in range(2)]
     return lax.all_to_all(x, AXIS, 0, 0, axis_index_groups=groups, tiled=True)
 
 
@@ -350,7 +356,7 @@
 
 def body(hamiltonian, current, previous):
     both = jnp.concatenate([current.T, previous.T], axis=0)
-    v_own = to_chips(jnp.broadcast_to(both[None], (CHIPS, 2 * NEIG, ROWS)), BACKWARD)
+    v_own = to_chips(jnp.broadcast_to(both[None], (CHIPS, 2 * NEIG, ROWS)), 0)
     tile = diagonal_tile(hamiltonian)
     cvec = jnp.pad(current.T, ((0, 0), (0, LANES - ROWS)))
     pvec = jnp.pad(previous.T, ((0, 0), (0, LANES - ROWS)))
@@ -362,15 +368,19 @@
     h_vmem = pltpu.VMEM((2, PARTS * TALL, HALF), BF16)
     h_half = pltpu.VMEM((PARTS * TALL, HALF), BF16)
     dma = pltpu.SemaphoreType.DMA
-    (product,) = kernel_call(
-        image_own_kernel, [((PARTS * TALL, STACK), F32)], (h_parts, v_own), 1 << 30, "image_own",
-        [h_half, half_vmem, dma(())], (0,), limit=LIMIT_IMAGE,
+    product, h_next = kernel_call(
+        image_own_kernel,
+        [((PARTS * TALL, STACK), F32), ((PARTS * TALL, HALF), BF16)],
+        (h_parts, v_own),
+        1 << 30,
+        "image_own",
+        [h_half, half_vmem, dma((2,))], (0,), limit=LIMIT_IMAGE,
     )
     image, sent = kernel_call(
-        image_other_kernel, [block, ((CHIPS, NEIG, LANES), F32)], (h_parts, v_other, product, tile), 1 << 30, "image_other",
-        [h_half, half_vmem, dma(())], (0,), limit=LIMIT_IMAGE,
-    )
-    i_own = to_chips(sent, FORWARD)
+        image_other_kernel, [block, ((CHIPS, NEIG, LANES), F32)], (h_next, v_other, product, tile), 1 << 30, "image_other",
+        [half_vmem], limit=LIMIT_IMAGE,
+    )
+    i_own = to_chips(sent, 1)
     p_image, c_parts, p_parts, grams = kernel_call(
         previous_kernel,
         [block, parts, parts, ((3, NEIG, NEIG), F32)],
@@ -395,10 +405,10 @@
         (h_parts, i_own, i_other, c_parts, i_own_parts, half_cross, diag, cvec, pvec, p_image, image, tile),
         6 << 30,
         "search",
-        [h_vmem, parts_vmem, half_vmem, parts_vmem, pltpu.VMEM((2, NEIG, HALF), F32), pltpu.VMEM((CHIPS, LANES), F32), dma((5,))],
+        [h_vmem, parts_vmem, half_vmem, parts_vmem, pltpu.VMEM((2, NEIG, HALF), F32), pltpu.VMEM((CHIPS, LANES), F32), dma((4,)), dma((2,))],
         (0, 3), (4,), limit=LIMIT_SEARCH,
     )
-    r_own = to_chips(sent, FORWARD)
+    r_own = to_chips(sent, 2)
     square = ((3 * NEIG, 3 * NEIG), F32)
     inverse, stiff = kernel_call(
         factor_kernel, [square, square], (kept, c_parts, p_parts, grams, cross), 6 << 30, "factor",

time: 94.2 us -> 88.4 us (0.938)
  Pallas kernels: 46.6 us -> 40.9 us
  waiting for transfers between devices: 10.5 us -> 5.79 us
  starting transfers between devices: 31.9 us -> 36.5 us
    pallas_call x7, Pallas kernels: 38.6 us -> 33 us  [kernel_call(): pl.pallas_call(body, out_shape=[jax.ShapeDtypeStruct(shape, kind) for sha...]
    all_to_all x3, starting transfers between devices: 26.9 us -> 32 us  [to_chips(): return lax.all_to_all(x, AXIS, 0, 0, axis_index_groups=groups, tiled=True)]
    all_to_all x3, waiting for transfers between devices: 9.13 us -> 4.45 us  [to_chips(): return lax.all_to_all(x, AXIS, 0, 0, axis_index_groups=groups, tiled=True)]
  transfers between devices with their start and end apart: 6 -> 6, of which waited for: 5 -> 4; matrix products, arithmetic and copies ran while one was open for 2% -> 2% of each run, Pallas kernels for 30% -> 32%
where the time goes in v5:
time: 88.4 us; the launch traced here: 87.8 us
  Pallas kernels  40.9 us (46%)
  starting transfers between devices  36.5 us (41%)
  waiting for transfers between devices  5.79 us (7%)
  other arithmetic  2.36 us (3%)
  local copies, waits for them, and re-layouts  1.17 us (1%)
    pallas_call x7, Pallas kernels, kernel_call(): pl.pallas_call(body, out_shape=[jax.ShapeDtypeStruct(shape, kind) for sha...  33 us
    all_to_all x3, starting transfers between devices, to_chips(): return lax.all_to_all(x, AXIS, 0, 0, axis_index_groups=groups, tiled=True)  32 us
    pallas_call x1, Pallas kernels, prepare(): pl.pallas_call(prepare_kernel, grid=(CHUNKS,), out_shape=jax.ShapeDtypeSt...  7.93 us
    ppermute x3, starting transfers between devices, to_core(): lax.ppermute(x, AXIS, [(device, device ^ 1) for device in range(DEVICES)])  4.56 us
    all_to_all x3, waiting for transfers between devices, to_chips(): return lax.all_to_all(x, AXIS, 0, 0, axis_index_groups=groups, tiled=True)  4.45 us
  transfers between devices with their start and end apart: 6, of which 4 were waited for; matrix products, arithmetic and copies ran while one was open for 2% of the time, Pallas kernels for 32%

profile of v5, /device:TPU:1, one launch (start us, length us, event | category | flops | bytes accessed | tf_op | source)
XLA Modules:
  0.0 87.8 jit_solution(10540315424739068967)
XLA Ops:
  0.6 0.7 pad_maximum_fusion
  1.4 1.1 %broadcast_in_dim.14 = f32[64,32,108]{2,1,0:T(8,128)} broadcast(f32[32,108]{1,0:T(8,128)S(1)} %pad_maximum_fusion), dimensions={1,2} | broadcast | bytes 898560 | tf_op jit(solution)/shard_map/broadcast_in_dim | solution.py:359
  2.5 13.7 %all-to-all-start = ((f32[64,32,108]{2,1,0:T(8,128)}), f32[64,32,108]{2,1,0:T(8,128)S(1)}, u32[]{:S(2)}, u32[]{:S(2)}) async-start(f32[64,32,108]{2,1,0:T(8,128)} %broadcast_in_dim.14), calls=%async_computation | async-start | bytes 2097152 | tf_op jit(solution)/shard_map/all_to_all | solution.py:340
  16.2 1.0 %select_reduce_fusion = f32[108]{0:T(128)S(1)} fusion(f32[108,13824]{1,0:T(8,128)} %h_ref.1, s32[]{:T(128)S(6)} %select_n.34), kind=kLoop, calls=%fused_computation.1 | loop fusion | flops 34884 | bytes 47092 | tf_op jit(solution)/shard_map/reduce_sum | solution.py:351
  17.3 7.9 %prepare.1.h_ref = bf16[2,224,8192]{2,1,0:T(8,128)(2,1)} custom-call(f32[108,13824]{1,0:T(8,128)} %h_ref.1), custom_call_target="tpu_custom_call" | custom-call | flops 29859840 | bytes 14929920 | tf_op jit(solution)/shard_map/prepare/pallas_call | solution.py:98
  25.2 0.2 fusion.tile_ref
  25.4 3.4 %all-to-all-done.own_ref = f32[64,32,108]{2,1,0:T(8,128)S(1)} async-done(((f32[64,32,108]{2,1,0:T(8,128)}), f32[64,32,108]{2,1,0:T(8,128)S(1)}, u32[]{:S(2)}, u32[]{:S(2)}) %all-to-all-start) | async-done | bytes 884768 | tf_op jit(solution)/shard_map/all_to_all | solution.py:340
  28.8 1.6 %collective-permute-start = (f32[64,32,108]{2,1,0:T(8,128)S(1)}, f32[64,32,108]{2,1,0:T(8,128)S(1)}, u32[]{:S(2)}, u32[]{:S(2)}) collective-permute-start(f32[64,32,108]{2,1,0:T(8,128)S(1)} %all-to-all-done.own_ref), channel_id=1, source_target_pairs={{0,1},{1,0},{2,3},{3,2},{4,5},{5,4},{6,7},{7,6},{8,9},{9,8},{10,11... | collective-permute-start | bytes 2654216 | tf_op jit(solution)/shard_map/ppermute | solution.py:344
  30.3 3.2 %image_own.1 = (f32[224,32]{1,0:T(8,128)S(1)}, bf16[224,8192]{1,0:T(8,128)(2,1)S(1)}) custom-call(bf16[2,224,8192]{2,1,0:T(8,128)(2,1)} %prepare.1.h_ref, f32[64,32,108]{2,1,0:T(8,128)S(1)} %all-to-all-done.own_ref), custom_call_target="tpu_custom_call" | custom-call | flops 1073741824 | bytes 4194304 | tf_op jit(solution)/shard_map/image_own/pallas_call | solution.py:326
  33.5 2.0 %image_other.1 = (f32[16,128]{1,0:T(8,128)S(1)}, f32[64,16,128]{2,1,0:T(8,128)}) custom-call(bf16[224,8192]{1,0:T(8,128)(2,1)S(1)} %get-tuple-element.34.h_ref, f32[64,32,108]{2,1,0:T(8,128)S(1)} %collective-permute-done.other_ref, f32[224,32]{1,0:T(8,128)S(1)} %get-tuple-element.35.product_ref, f32[16,128]{1,0:T(8,128)S(1)} %fusion.tile_ref), custom_call_target="tpu_custom_call" | custom-call | flops 1073741824 | bytes 4194304 | tf_op jit(solution)/shard_map/image_other/pallas_call | solution.py:326
  35.6 10.4 %all-to-all-start.1 = ((f32[64,16,128]{2,1,0:T(8,128)}), f32[64,16,128]{2,1,0:T(8,128)S(1)}, u32[]{:S(2)}, u32[]{:S(2)}) async-start(f32[64,16,128]{2,1,0:T(8,128)} %get-tuple-element.37), calls=%async_computation.1 | async-start | bytes 1048576 | tf_op jit(solution)/shard_map/all_to_all | solution.py:340
  46.0 0.0 copy-start.2
  46.0 7.8 %previous.1 = (f32[16,128]{1,0:T(8,128)S(1)}, bf16[2,32,8192]{2,1,0:T(8,128)(2,1)}, bf16[2,32,8192]{2,1,0:T(8,128)(2,1)}, f32[3,16,16]{2,1,0:T(8,128)S(1)}) custom-call(bf16[2,224,8192]{2,1,0:T(8,128)(2,1)} %prepare.1.h_ref, f32[64,32,108]{2,1,0:T(8,128)} %copy-done, f32[64,32,108]{2,1,0:T(8,128)} %copy-done.1), custom_call_target="tpu_custom_call" | custom-call | flops 6442450944 | bytes 4194304 | tf_op jit(solution)/shard_map/previous/pallas_call | solution.py:326
  53.8 1.4 %collective-permute-start.1 = (f32[64,16,128]{2,1,0:T(8,128)S(1)}, f32[64,16,128]{2,1,0:T(8,128)S(1)}, u32[]{:S(2)}, u32[]{:S(2)}) collective-permute-start(f32[64,16,128]{2,1,0:T(8,128)S(1)} %all-to-all-done.1.own_ref), channel_id=1, source_target_pairs={{0,1},{1,0},{2,3},{3,2},{4,5},{5,4},{6,7},{7,6},{8,9},{9,8},{10,11... | collective-permute-start | bytes 1572872 | tf_op jit(solution)/shard_map/ppermute | solution.py:344
  55.3 1.3 %own.1 = (bf16[32,8192]{1,0:T(8,128)(2,1)S(1)}, f32[32,32]{1,0:T(8,128)S(1)}, f32[64,128]{1,0:T(8,128)S(1)}) custom-call(f32[64,16,128]{2,1,0:T(8,128)S(1)} %all-to-all-done.1.own_ref, bf16[2,32,8192]{2,1,0:T(8,128)(2,1)} %get-tuple-element.41.c_hbm), custom_call_target="tpu_custom_call" | custom-call | flops 1073741824 | bytes 4194304 | tf_op jit(solution)/shard_map/own/pallas_call | solution.py:326
  56.6 0.2 collective-permute-done.1.other_ref
  56.8 6.9 %search.1 = (f32[16,128]{1,0:T(8,128)S(1)}, f32[16,1]{1,0:T(8,128)S(1)}, f32[16,16]{1,0:T(8,128)S(1)}, f32[64,8,128]{2,1,0:T(8,128)}, bf16[4,32,8192]{2,1,0:T(8,128)(2,1)}) custom-call(bf16[2,224,8192]{2,1,0:T(8,128)(2,1)} %prepare.1.h_ref, f32[64,16,128]{2,1,0:T(8,128)S(1)} %all-to-all-done.1.own_ref, f32[64,16,128]{2,1,0:T(8,128)S(1)} %collective-permute-done.1.other_ref, ...), custom_call_target="tpu_custom_call" | custom-call | flops 6442450944 | bytes 4194304 | tf_op jit(solution)/shard_map/search/pallas_call | solution.py:326
  63.7 7.8 %all-to-all-start.2 = ((f32[64,8,128]{2,1,0:T(8,128)}), f32[64,8,128]{2,1,0:T(8,128)S(1)}, u32[]{:S(2)}, u32[]{:S(2)}) async-start(f32[64,8,128]{2,1,0:T(8,128)} %get-tuple-element.47), calls=%async_computation.2 | async-start | bytes 524288 | tf_op jit(solution)/shard_map/all_to_all | solution.py:340
  71.5 8.1 %factor.1 = (f32[48,48]{1,0:T(8,128)S(1)}, f32[48,48]{1,0:T(8,128)S(1)}) custom-call(bf16[4,32,8192]{2,1,0:T(8,128)(2,1)} %get-tuple-element.48.kept_hbm, bf16[2,32,8192]{2,1,0:T(8,128)(2,1)} %get-tuple-element.41.c_hbm, bf16[2,32,8192]{2,1,0:T(8,128)(2,1)} %get-tuple-element.49.p_hbm, f32[3,16,16]{2,1,0:T(8,128)S(1)} %get-tuple-element.50.gram_ref, ...), custom_call_target="tpu_custom_call" | custom-call | flops 6442450944 | bytes 4194304 | tf_op jit(solution)/shard_map/factor/pallas_call | solution.py:326
  79.7 0.6 reduce
  80.3 1.0 %all-to-all-done.2.own_ref = f32[64,8,128]{2,1,0:T(8,128)S(1)} async-done(((f32[64,8,128]{2,1,0:T(8,128)}), f32[64,8,128]{2,1,0:T(8,128)S(1)}, u32[]{:S(2)}, u32[]{:S(2)}) %all-to-all-start.2) | async-done | bytes 262176 | tf_op jit(solution)/shard_map/all_to_all | solution.py:340
  81.3 1.6 %collective-permute-start.2 = (f32[64,8,128]{2,1,0:T(8,128)S(1)}, f32[64,8,128]{2,1,0:T(8,128)S(1)}, u32[]{:S(2)}, u32[]{:S(2)}) collective-permute-start(f32[64,8,128]{2,1,0:T(8,128)S(1)} %all-to-all-done.2.own_ref), channel_id=1, source_target_pairs={{0,1},{1,0},{2,3},{3,2},{4,5},{5,4},{6,7},{7,6},{8,9},{9,8},{10,11... | collective-permute-start | bytes 786440 | tf_op jit(solution)/shard_map/ppermute | solution.py:344
  82.9 1.2 %collective-permute-done.2.other_ref = f32[64,8,128]{2,1,0:T(8,128)S(1)} collective-permute-done((f32[64,8,128]{2,1,0:T(8,128)S(1)}, f32[64,8,128]{2,1,0:T(8,128)S(1)}, u32[]{:S(2)}, u32[]{:S(2)}) %collective-permute-start.2) | collective-permute-done | bytes 262176 | tf_op jit(solution)/shard_map/ppermute | solution.py:344
  84.1 3.7 %finish.1 = (f32[16,108]{1,0:T(8,128)}, f32[16,108]{1,0:T(8,128)}) custom-call(f32[48,48]{1,0:T(8,128)S(1)} %get-tuple-element.54.inverse_ref, f32[48,48]{1,0:T(8,128)S(1)} %get-tuple-element.55.stiff_ref, f32[64,8,128]{2,1,0:T(8,128)S(1)} %all-to-all-done.2.own_ref, f32[64,8,128]{2,1,0:T(8,128)S(1)} %collective-permute-done.2.other_ref, ...), custom_call_target="tpu_custom_call" | custom-call | flops 268435456 | bytes 4194304 | tf_op jit(solution)/shard_map/finish/pallas_call | solution.py:326
  (12 shorter events, 0.0 us)
Async XLA Ops:
  2.5 26.3 %all-to-all-start = ((f32[64,32,108]{2,1,0:T(8,128)}), f32[64,32,108]{2,1,0:T(8,128)S(1)}, u32[]{:S(2)}, u32[]{:S(2)}) async-start(f32[64,32,108]{2,1,0:T(8,128)} %broadcast_in_dim.14), calls=%async_computation | async-start | bytes 2097152 | tf_op jit(solution)/shard_map/all_to_all | solution.py:340
  28.8 6.8 %copy-start = (f32[64,32,108]{2,1,0:T(8,128)}, f32[64,32,108]{2,1,0:T(8,128)S(1)}, u32[]{:S(2)}) copy-start(f32[64,32,108]{2,1,0:T(8,128)S(1)} %all-to-all-done.own_ref) | copy-start | bytes 2654212
  28.8 4.7 %collective-permute-start = (f32[64,32,108]{2,1,0:T(8,128)S(1)}, f32[64,32,108]{2,1,0:T(8,128)S(1)}, u32[]{:S(2)}, u32[]{:S(2)}) collective-permute-start(f32[64,32,108]{2,1,0:T(8,128)S(1)} %all-to-all-done.own_ref), channel_id=1, source_target_pairs={{0,1},{1,0},{2,3},{3,2},{4,5},{5,4},{6,7},{7,6},{8,9},{9,8},{10,11... | collective-permute-start | bytes 2654216 | tf_op jit(solution)/shard_map/ppermute | solution.py:344
  33.5 12.5 %copy-start.1 = (f32[64,32,108]{2,1,0:T(8,128)}, f32[64,32,108]{2,1,0:T(8,128)S(1)}, u32[]{:S(2)}) copy-start(f32[64,32,108]{2,1,0:T(8,128)S(1)} %collective-permute-done.other_ref) | copy-start | bytes 2654212
  35.6 18.3 %all-to-all-start.1 = ((f32[64,16,128]{2,1,0:T(8,128)}), f32[64,16,128]{2,1,0:T(8,128)S(1)}, u32[]{:S(2)}, u32[]{:S(2)}) async-start(f32[64,16,128]{2,1,0:T(8,128)} %get-tuple-element.37), calls=%async_computation.1 | async-start | bytes 1048576 | tf_op jit(solution)/shard_map/all_to_all | solution.py:340
  46.0 9.2 %copy-start.2 = (f32[108,16]{0,1:T(8,128)S(1)}, f32[108,16]{0,1:T(8,128)}, u32[]{:S(2)}) copy-start(f32[108,16]{0,1:T(8,128)} %param.4) | copy-start | bytes 20740
  46.0 9.2 %copy-start.3 = (f32[108,16]{0,1:T(8,128)S(1)}, f32[108,16]{0,1:T(8,128)}, u32[]{:S(2)}) copy-start(f32[108,16]{0,1:T(8,128)} %param.5) | copy-start | bytes 20740
  53.8 3.0 %collective-permute-start.1 = (f32[64,16,128]{2,1,0:T(8,128)S(1)}, f32[64,16,128]{2,1,0:T(8,128)S(1)}, u32[]{:S(2)}, u32[]{:S(2)}) collective-permute-start(f32[64,16,128]{2,1,0:T(8,128)S(1)} %all-to-all-done.1.own_ref), channel_id=1, source_target_pairs={{0,1},{1,0},{2,3},{3,2},{4,5},{5,4},{6,7},{7,6},{8,9},{9,8},{10,11... | collective-permute-start | bytes 1572872 | tf_op jit(solution)/shard_map/ppermute | solution.py:344
  63.7 17.6 %all-to-all-start.2 = ((f32[64,8,128]{2,1,0:T(8,128)}), f32[64,8,128]{2,1,0:T(8,128)S(1)}, u32[]{:S(2)}, u32[]{:S(2)}) async-start(f32[64,8,128]{2,1,0:T(8,128)} %get-tuple-element.47), calls=%async_computation.2 | async-start | bytes 524288 | tf_op jit(solution)/shard_map/all_to_all | solution.py:340
  81.3 2.7 %collective-permute-start.2 = (f32[64,8,128]{2,1,0:T(8,128)S(1)}, f32[64,8,128]{2,1,0:T(8,128)S(1)}, u32[]{:S(2)}, u32[]{:S(2)}) collective-permute-start(f32[64,8,128]{2,1,0:T(8,128)S(1)} %all-to-all-done.2.own_ref), channel_id=1, source_target_pairs={{0,1},{1,0},{2,3},{3,2},{4,5},{5,4},{6,7},{7,6},{8,9},{9,8},{10,11... | collective-permute-start | bytes 786440 | tf_op jit(solution)/shard_map/ppermute | solution.py:344

commit v6 on v5

--- a/solution.py
+++ b/solution.py
@@ -119,10 +119,18 @@
             parts_ref[NEIG * number : NEIG * (number + 1), LANES * chip : LANES * (chip + 1)] = part
 
 
+def take_both(tile_of, parts_ref):
+    for chip in range(CHIPS):
+        lanes = slice(LANES * chip, LANES * (chip + 1))
+        for number, part in enumerate(split(tile_of(chip))):
+            parts_ref[NEIG * number : NEIG * (number + 1), lanes] = part[:NEIG]
+            parts_ref[STACK + NEIG * number : STACK + NEIG * (number + 1), lanes] = part[NEIG:]
+
+
 def image_own_kernel(h_ref, own_ref, product_ref, next_ref, h_vmem, parts, sems):
     copy = started(h_ref.at[0], h_vmem, sems.at[0])
     following = started(h_ref.at[1], next_ref, sems.at[1])
-    take_parts(lambda chip: padded(own_ref[SLOTS[0][chip], 0:NEIG]), parts)
+    take_both(lambda chip: padded(own_ref[SLOTS[0][chip]]), parts)
     copy.wait()
     product_ref[...] = nt(h_vmem[...], parts[...])
     following.wait()
@@ -130,27 +138,25 @@
 
 def image_other_kernel(h_ref, other_ref, product_ref, tile_ref, image_ref, sent_ref, parts):
     take_parts(lambda chip: padded(other_ref[SLOTS[0][chip], 0:NEIG]), parts)
-    image = fold_rows(product_ref[...] + nt(h_ref[...], parts[...]))
+    image = fold_rows(product_ref[:, 0:STACK] + nt(h_ref[...], parts[...]))
     image_ref[...] = image
     sent = image + tile_ref[...]
     for chip in range(CHIPS):
         sent_ref[chip] = sent
 
 
-def previous_kernel(h_ref, own_ref, other_ref, image_ref, c_out, p_out, gram_ref, h_vmem, c_ref, p_ref, sems):
-    copy = started(h_ref, h_vmem, sems.at[0])
-    for half, ref in ((0, own_ref), (1, other_ref)):
-        take_parts(lambda chip: padded(ref[SLOTS[0][chip], 0:NEIG]), c_ref.at[half])
-        take_parts(lambda chip: padded(ref[SLOTS[0][chip], NEIG : 2 * NEIG]), p_ref.at[half])
-    out_c = started(c_ref, c_out, sems.at[1])
-    out_p = started(p_ref, p_out, sems.at[2])
-    gram_ref[0] = fold(nt(c_ref[0], c_ref[0]) + nt(c_ref[1], c_ref[1]))
-    gram_ref[1] = fold(nt(p_ref[0], c_ref[0]) + nt(p_ref[1], c_ref[1]))
-    gram_ref[2] = fold(nt(p_ref[0], p_ref[0]) + nt(p_ref[1], p_ref[1]))
+def previous_kernel(h_ref, own_ref, other_ref, product_ref, image_ref, both_out, gram_ref, h_vmem, both_ref, sems):
+    copy = started(h_ref.at[1], h_vmem, sems.at[0])
+    take_both(lambda chip: padded(own_ref[SLOTS[0][chip]]), both_ref.at[0])
+    take_both(lambda chip: padded(other_ref[SLOTS[0][chip]]), both_ref.at[1])
+    out = started(both_ref, both_out, sems.at[1])
+    product = nt(both_ref[0], both_ref[0]) + nt(both_ref[1], both_ref[1])
+    gram_ref[0] = fold(product[:STACK, :STACK])
+    gram_ref[1] = fold(product[STACK:, :STACK])
+    gram_ref[2] = fold(product[STACK:, STACK:])
     copy.wait()
-    image_ref[...] = fold_rows(nt(h_vmem[0], p_ref[0]) + nt(h_vmem[1], p_ref[1]))
-    out_c.wait()
-    out_p.wait()
+    image_ref[...] = fold_rows(product_ref[:, STACK:] + nt(h_vmem[...], both_ref[1, STACK:]))
+    out.wait()
 
 
 def diagonal_of(tile):
@@ -160,8 +166,8 @@
     return jnp.sum(jnp.where(lane % NEIG == row, spread, 0.0), axis=0, keepdims=True)
 
 
-def own_kernel(own_ref, c_hbm, i_ref, cross_ref, diag_ref, c_ref, sem):
-    copy = started(c_hbm.at[0], c_ref, sem)
+def own_kernel(own_ref, both_hbm, i_ref, cross_ref, diag_ref, c_ref, sem):
+    copy = started(both_hbm.at[0, pl.ds(0, STACK)], c_ref, sem)
     take_parts(lambda chip: real_lanes(own_ref[SLOTS[1][chip]]), i_ref)
     for chip in range(CHIPS):
         diag_ref[chip : chip + 1, :] = diagonal_of(own_ref[SLOTS[1][chip]])
@@ -170,11 +176,11 @@
 
 
 def search_kernel(
-    h_ref, own_ref, other_ref, c_hbm, i_own_ref, half_cross_ref, diag_ref, cvec_ref, pvec_ref, pimage_ref, image_ref, tile_ref,
+    h_ref, own_ref, other_ref, both_hbm, i_own_ref, half_cross_ref, diag_ref, cvec_ref, pvec_ref, pimage_ref, image_ref, tile_ref,
     search_ref, rms_ref, cross_ref, sent_ref, kept_ref,
     h_vmem, c_ref, i_ref, s_ref, resid_ref, other_diag_ref, sems, h_sems,
 ):
-    copy_c = started(c_hbm, c_ref, sems.at[3])
+    copy_c = started(both_hbm.at[:, pl.ds(0, STACK)], c_ref, sems.at[3])
     copies = [started(h_ref.at[half], h_vmem.at[half], h_sems.at[half]) for half in range(2)]
     take_parts(lambda chip: real_lanes(other_ref[SLOTS[1][chip]]), i_ref)
     for chip in range(CHIPS):
@@ -233,24 +239,29 @@
         copy.wait()
 
 
-def factor_kernel(
-    kept_hbm, c_hbm, p_hbm, gram_ref, cross_ref, inverse_ref, stiff_ref, kept_ref, c_ref, p_ref, sems,
-):
-    pairs = ((kept_hbm, kept_ref), (c_hbm, c_ref), (p_hbm, p_ref))
-    s_ref, i_ref = kept_ref.at[pl.ds(0, 2)], kept_ref.at[pl.ds(2, 2)]
-    for copy in [started(a, b, sems.at[n]) for n, (a, b) in enumerate(pairs)]:
+def factor_kernel(kept_hbm, both_hbm, gram_ref, cross_ref, inverse_ref, stiff_ref, all_ref, sems):
+    copies = []
+    for half in range(2):
+        places = (
+            (kept_hbm.at[half], pl.ds(0, STACK)),
+            (kept_hbm.at[2 + half], pl.ds(STACK, STACK)),
+            (both_hbm.at[half], pl.ds(2 * STACK, 2 * STACK)),
+        )
+        for number, (source, rows) in enumerate(places):
+            copies.append(started(source, all_ref.at[half, rows], sems.at[half, number]))
+    for copy in copies:
         copy.wait()
-
-    def gram(left, right):
-        return fold(nt(left[0], right[0]) + nt(left[1], right[1]))
-
+    with_search = nt(all_ref[0], all_ref[0, :STACK]) + nt(all_ref[1], all_ref[1, :STACK])
+    ss, i_s, cs, ps = [fold(with_search[STACK * n : STACK * (n + 1)]) for n in range(4)]
+    p_image = fold(
+        nt(all_ref[0, 3 * STACK :], all_ref[0, STACK : 2 * STACK]) + nt(all_ref[1, 3 * STACK :], all_ref[1, STACK : 2 * STACK])
+    )
     empty = jnp.zeros((NEIG, NEIG), F32)
     cc, pc, pp = gram_ref[0], gram_ref[1], gram_ref[2]
-    sc, ss, ps = gram(s_ref, c_ref), gram(s_ref, s_ref), gram(p_ref, s_ref)
     low = jnp.concatenate(
         [
-            jnp.concatenate([0.5 * cc, empty, empty], axis=1),
-            jnp.concatenate([sc, 0.5 * ss, empty], axis=1),
+            jnp.concatenate([0.5 * cc, cs, empty], axis=1),
+            jnp.concatenate([empty, 0.5 * ss, empty], axis=1),
             jnp.concatenate([pc, ps, 0.5 * pp], axis=1),
         ],
         axis=0,
@@ -258,9 +269,9 @@
     mass = low + low.T
     low = jnp.concatenate(
         [
-            jnp.concatenate([0.5 * cross_ref[...], empty, empty], axis=1),
-            jnp.concatenate([gram(s_ref, i_ref), empty, empty], axis=1),
-            jnp.concatenate([gram(p_ref, i_ref), empty, empty], axis=1),
+            jnp.concatenate([0.5 * cross_ref[...], i_s, empty], axis=1),
+            jnp.concatenate([empty, empty, empty], axis=1),
+            jnp.concatenate([p_image, empty, empty], axis=1),
         ],
         axis=0,
     )
@@ -363,38 +374,38 @@
     h_parts = prepare(hamiltonian)
     v_own, h_parts, tile = lax.optimization_barrier((v_own, h_parts, tile))
     v_other = to_core(v_own)
-    block, parts, half = ((NEIG, LANES), F32), ((2, STACK, HALF), BF16), ((STACK, HALF), BF16)
-    parts_vmem, half_vmem = pltpu.VMEM(*parts), pltpu.VMEM(*half)
+    block, half, both_parts = ((NEIG, LANES), F32), ((STACK, HALF), BF16), ((2, 2 * STACK, HALF), BF16)
+    half_vmem, parts_vmem = pltpu.VMEM(*half), pltpu.VMEM((2, STACK, HALF), BF16)
     h_vmem = pltpu.VMEM((2, PARTS * TALL, HALF), BF16)
     h_half = pltpu.VMEM((PARTS * TALL, HALF), BF16)
     dma = pltpu.SemaphoreType.DMA
     product, h_next = kernel_call(
         image_own_kernel,
-        [((PARTS * TALL, STACK), F32), ((PARTS * TALL, HALF), BF16)],
+        [((PARTS * TALL, 2 * STACK), F32), ((PARTS * TALL, HALF), BF16)],
         (h_parts, v_own),
         1 << 30,
         "image_own",
-        [h_half, half_vmem, dma((2,))], (0,), limit=LIMIT_IMAGE,
+        [h_half, pltpu.VMEM((2 * STACK, HALF), BF16), dma((2,))], (0,), limit=LIMIT_IMAGE,
     )
     image, sent = kernel_call(
         image_other_kernel, [block, ((CHIPS, NEIG, LANES), F32)], (h_next, v_other, product, tile), 1 << 30, "image_other",
         [half_vmem], limit=LIMIT_IMAGE,
     )
     i_own = to_chips(sent, 1)
-    p_image, c_parts, p_parts, grams = kernel_call(
+    p_image, both_parts, grams = kernel_call(
         previous_kernel,
-        [block, parts, parts, ((3, NEIG, NEIG), F32)],
-        (h_parts, v_own, v_other),
+        [block, both_parts, ((3, NEIG, NEIG), F32)],
+        (h_parts, v_own, v_other, product),
         6 << 30,
         "previous",
-        [h_vmem, parts_vmem, parts_vmem, dma((3,))], (0,), (1, 2),
-    )
-    i_own, p_image, c_parts = lax.optimization_barrier((i_own, p_image, c_parts))
+        [h_half, pltpu.VMEM(*both_parts), dma((2,))], (0,), (1,),
+    )
+    i_own, p_image, both_parts = lax.optimization_barrier((i_own, p_image, both_parts))
     i_other = to_core(i_own)
     i_own_parts, half_cross, diag = kernel_call(
         own_kernel,
         [half, ((STACK, STACK), F32), ((CHIPS, LANES), F32)],
-        (i_own, c_parts),
+        (i_own, both_parts),
         1 << 30,
         "own",
         [half_vmem, dma(())], (1,), limit=LIMIT_OWN,
@@ -402,7 +413,7 @@
     search, rms, cross, sent, kept = kernel_call(
         search_kernel,
         [block, ((NEIG, 1), F32), ((NEIG, NEIG), F32), ((CHIPS, 8, LANES), F32), ((4, STACK, HALF), BF16)],
-        (h_parts, i_own, i_other, c_parts, i_own_parts, half_cross, diag, cvec, pvec, p_image, image, tile),
+        (h_parts, i_own, i_other, both_parts, i_own_parts, half_cross, diag, cvec, pvec, p_image, image, tile),
         6 << 30,
         "search",
         [h_vmem, parts_vmem, half_vmem, parts_vmem, pltpu.VMEM((2, NEIG, HALF), F32), pltpu.VMEM((CHIPS, LANES), F32), dma((4,)), dma((2,))],
@@ -411,8 +422,8 @@
     r_own = to_chips(sent, 2)
     square = ((3 * NEIG, 3 * NEIG), F32)
     inverse, stiff = kernel_call(
-        factor_kernel, [square, square], (kept, c_parts, p_parts, grams, cross), 6 << 30, "factor",
-        [pltpu.VMEM((4, STACK, HALF), BF16), parts_vmem, parts_vmem, dma((3,))], (0, 1, 2),
+        factor_kernel, [square, square], (kept, both_parts, grams, cross), 6 << 30, "factor",
+        [pltpu.VMEM((2, 4 * STACK, HALF), BF16), dma((2, 3))], (0, 1),
     )
     r_own, inverse, rms = lax.optimization_barrier((r_own, inverse, rms[:, 0]))
     r_other = to_core(r_own)

time: 88.4 us -> 90.4 us (1.023)
  waiting for transfers between devices: 5.79 us -> 7.27 us
    all_to_all x3, waiting for transfers between devices: 4.45 us -> 5.93 us  [to_chips(): return lax.all_to_all(x, AXIS, 0, 0, axis_index_groups=groups, tiled=True)]
  transfers between devices with their start and end apart: 6 -> 6, of which waited for: 4 -> 5; matrix products, arithmetic and copies ran while one was open for 2% -> 2% of each run, Pallas kernels for 32% -> 29%
where the time goes in v6:
time: 90.4 us; the launch traced here: 89.8 us
  Pallas kernels  40.9 us (45%)
  starting transfers between devices  37.2 us (41%)
  waiting for transfers between devices  7.27 us (8%)
  other arithmetic  2.36 us (3%)
  local copies, waits for them, and re-layouts  1.17 us (1%)
    pallas_call x7, Pallas kernels, kernel_call(): pl.pallas_call(body, out_shape=[jax.ShapeDtypeStruct(shape, kind) for sha...  32.9 us
    all_to_all x3, starting transfers between devices, to_chips(): return lax.all_to_all(x, AXIS, 0, 0, axis_index_groups=groups, tiled=True)  32 us
    pallas_call x1, Pallas kernels, prepare(): pl.pallas_call(prepare_kernel, grid=(CHUNKS,), out_shape=jax.ShapeDtypeSt...  7.93 us
    all_to_all x3, waiting for transfers between devices, to_chips(): return lax.all_to_all(x, AXIS, 0, 0, axis_index_groups=groups, tiled=True)  5.93 us
    ppermute x3, starting transfers between devices, to_core(): lax.ppermute(x, AXIS, [(device, device ^ 1) for device in range(DEVICES)])  5.22 us
  transfers between devices with their start and end apart: 6, of which 5 were waited for; matrix products, arithmetic and copies ran while one was open for 2% of the time, Pallas kernels for 29%

profile of v6, /device:TPU:1, one launch (start us, length us, event | category | flops | bytes accessed | tf_op | source)
XLA Modules:
  0.0 89.8 jit_solution(18224491296829580091)
XLA Ops:
  0.6 0.7 pad_maximum_fusion
  1.4 1.1 %broadcast_in_dim.14 = f32[64,32,108]{2,1,0:T(8,128)} broadcast(f32[32,108]{1,0:T(8,128)S(1)} %pad_maximum_fusion), dimensions={1,2} | broadcast | bytes 898560 | tf_op jit(solution)/shard_map/broadcast_in_dim | solution.py:370
  2.5 13.7 %all-to-all-start = ((f32[64,32,108]{2,1,0:T(8,128)}), f32[64,32,108]{2,1,0:T(8,128)S(1)}, u32[]{:S(2)}, u32[]{:S(2)}) async-start(f32[64,32,108]{2,1,0:T(8,128)} %broadcast_in_dim.14), calls=%async_computation | async-start | bytes 2097152 | tf_op jit(solution)/shard_map/all_to_all | solution.py:351
  16.2 1.0 %select_reduce_fusion = f32[108]{0:T(128)S(1)} fusion(f32[108,13824]{1,0:T(8,128)} %h_ref.1, s32[]{:T(128)S(6)} %select_n.34), kind=kLoop, calls=%fused_computation.1 | loop fusion | flops 34884 | bytes 47092 | tf_op jit(solution)/shard_map/reduce_sum | solution.py:362
  17.3 7.9 %prepare.1.h_ref = bf16[2,224,8192]{2,1,0:T(8,128)(2,1)} custom-call(f32[108,13824]{1,0:T(8,128)} %h_ref.1), custom_call_target="tpu_custom_call" | custom-call | flops 29859840 | bytes 14929920 | tf_op jit(solution)/shard_map/prepare/pallas_call | solution.py:98
  25.2 0.2 fusion.tile_ref
  25.4 3.4 %all-to-all-done.own_ref = f32[64,32,108]{2,1,0:T(8,128)S(1)} async-done(((f32[64,32,108]{2,1,0:T(8,128)}), f32[64,32,108]{2,1,0:T(8,128)S(1)}, u32[]{:S(2)}, u32[]{:S(2)}) %all-to-all-start) | async-done | bytes 884768 | tf_op jit(solution)/shard_map/all_to_all | solution.py:351
  28.8 1.6 %collective-permute-start = (f32[64,32,108]{2,1,0:T(8,128)S(1)}, f32[64,32,108]{2,1,0:T(8,128)S(1)}, u32[]{:S(2)}, u32[]{:S(2)}) collective-permute-start(f32[64,32,108]{2,1,0:T(8,128)S(1)} %all-to-all-done.own_ref), channel_id=1, source_target_pairs={{0,1},{1,0},{2,3},{3,2},{4,5},{5,4},{6,7},{7,6},{8,9},{9,8},{10,11... | collective-permute-start | bytes 2654216 | tf_op jit(solution)/shard_map/ppermute | solution.py:355
  30.3 3.2 %image_own.1 = (f32[224,64]{1,0:T(8,128)S(1)}, bf16[224,8192]{1,0:T(8,128)(2,1)S(1)}) custom-call(bf16[2,224,8192]{2,1,0:T(8,128)(2,1)} %prepare.1.h_ref, f32[64,32,108]{2,1,0:T(8,128)S(1)} %all-to-all-done.own_ref), custom_call_target="tpu_custom_call" | custom-call | flops 1073741824 | bytes 4194304 | tf_op jit(solution)/shard_map/image_own/pallas_call | solution.py:337
  33.5 2.0 %image_other.1 = (f32[16,128]{1,0:T(8,128)S(1)}, f32[64,16,128]{2,1,0:T(8,128)}) custom-call(bf16[224,8192]{1,0:T(8,128)(2,1)S(1)} %get-tuple-element.33.h_ref, f32[64,32,108]{2,1,0:T(8,128)S(1)} %collective-permute-done.other_ref, f32[224,64]{1,0:T(8,128)S(1)} %get-tuple-element.34.product_ref, f32[16,128]{1,0:T(8,128)S(1)} %fusion.tile_ref), custom_call_target="tpu_custom_call" | custom-call | flops 1073741824 | bytes 4194304 | tf_op jit(solution)/shard_map/image_other/pallas_call | solution.py:337
  35.6 10.4 %all-to-all-start.1 = ((f32[64,16,128]{2,1,0:T(8,128)}), f32[64,16,128]{2,1,0:T(8,128)S(1)}, u32[]{:S(2)}, u32[]{:S(2)}) async-start(f32[64,16,128]{2,1,0:T(8,128)} %get-tuple-element.36), calls=%async_computation.1 | async-start | bytes 1048576 | tf_op jit(solution)/shard_map/all_to_all | solution.py:351
  46.0 5.4 %previous.1 = (f32[16,128]{1,0:T(8,128)S(1)}, bf16[2,64,8192]{2,1,0:T(8,128)(2,1)}, f32[3,16,16]{2,1,0:T(8,128)S(1)}) custom-call(bf16[2,224,8192]{2,1,0:T(8,128)(2,1)} %prepare.1.h_ref, f32[64,32,108]{2,1,0:T(8,128)} %copy-done, f32[64,32,108]{2,1,0:T(8,128)} %copy-done.1, f32[224,64]{1,0:T(8,128)S(1)} %get-tuple-element.34.product_ref), custom_call_target="tpu_custom_call" | custom-call | flops 6442450944 | bytes 4194304 | tf_op jit(solution)/shard_map/previous/pallas_call | solution.py:337
  51.4 1.7 %all-to-all-done.1.own_ref = f32[64,16,128]{2,1,0:T(8,128)S(1)} async-done(((f32[64,16,128]{2,1,0:T(8,128)}), f32[64,16,128]{2,1,0:T(8,128)S(1)}, u32[]{:S(2)}, u32[]{:S(2)}) %all-to-all-start.1) | async-done | bytes 524320 | tf_op jit(solution)/shard_map/all_to_all | solution.py:351
  53.2 2.1 %collective-permute-start.1 = (f32[64,16,128]{2,1,0:T(8,128)S(1)}, f32[64,16,128]{2,1,0:T(8,128)S(1)}, u32[]{:S(2)}, u32[]{:S(2)}) collective-permute-start(f32[64,16,128]{2,1,0:T(8,128)S(1)} %all-to-all-done.1.own_ref), channel_id=1, source_target_pairs={{0,1},{1,0},{2,3},{3,2},{4,5},{5,4},{6,7},{7,6},{8,9},{9,8},{10,11... | collective-permute-start | bytes 1572872 | tf_op jit(solution)/shard_map/ppermute | solution.py:355
  55.3 1.3 %own.1 = (bf16[32,8192]{1,0:T(8,128)(2,1)S(1)}, f32[32,32]{1,0:T(8,128)S(1)}, f32[64,128]{1,0:T(8,128)S(1)}) custom-call(f32[64,16,128]{2,1,0:T(8,128)S(1)} %all-to-all-done.1.own_ref, bf16[2,64,8192]{2,1,0:T(8,128)(2,1)} %get-tuple-element.40.both_hbm), custom_call_target="tpu_custom_call" | custom-call | flops 1073741824 | bytes 4194304 | tf_op jit(solution)/shard_map/own/pallas_call | solution.py:337
  56.6 0.2 collective-permute-done.1.other_ref
  56.8 9.0 %search.1 = (f32[16,128]{1,0:T(8,128)S(1)}, f32[16,1]{1,0:T(8,128)S(1)}, f32[16,16]{1,0:T(8,128)S(1)}, f32[64,8,128]{2,1,0:T(8,128)}, bf16[4,32,8192]{2,1,0:T(8,128)(2,1)}) custom-call(bf16[2,224,8192]{2,1,0:T(8,128)(2,1)} %prepare.1.h_ref, f32[64,16,128]{2,1,0:T(8,128)S(1)} %all-to-all-done.1.own_ref, f32[64,16,128]{2,1,0:T(8,128)S(1)} %collective-permute-done.1.other_ref, ...), custom_call_target="tpu_custom_call" | custom-call | flops 6442450944 | bytes 4194304 | tf_op jit(solution)/shard_map/search/pallas_call | solution.py:337
  65.8 7.8 %all-to-all-start.2 = ((f32[64,8,128]{2,1,0:T(8,128)}), f32[64,8,128]{2,1,0:T(8,128)S(1)}, u32[]{:S(2)}, u32[]{:S(2)}) async-start(f32[64,8,128]{2,1,0:T(8,128)} %get-tuple-element.46), calls=%async_computation.2 | async-start | bytes 524288 | tf_op jit(solution)/shard_map/all_to_all | solution.py:351
  73.6 8.3 %factor.1 = (f32[48,48]{1,0:T(8,128)S(1)}, f32[48,48]{1,0:T(8,128)S(1)}) custom-call(bf16[4,32,8192]{2,1,0:T(8,128)(2,1)} %get-tuple-element.47.kept_hbm, bf16[2,64,8192]{2,1,0:T(8,128)(2,1)} %get-tuple-element.40.both_hbm, f32[3,16,16]{2,1,0:T(8,128)S(1)} %get-tuple-element.48.gram_ref, f32[16,16]{1,0:T(8,128)S(1)} %get-tuple-element.49.cross_ref), custom_call_target="tpu_custom_call" | custom-call | flops 6442450944 | bytes 4194304 | tf_op jit(solution)/shard_map/factor/pallas_call | solution.py:337
  81.9 0.6 reduce
  82.6 0.8 all-to-all-done.2.own_ref
  83.4 1.6 %collective-permute-start.2 = (f32[64,8,128]{2,1,0:T(8,128)S(1)}, f32[64,8,128]{2,1,0:T(8,128)S(1)}, u32[]{:S(2)}, u32[]{:S(2)}) collective-permute-start(f32[64,8,128]{2,1,0:T(8,128)S(1)} %all-to-all-done.2.own_ref), channel_id=1, source_target_pairs={{0,1},{1,0},{2,3},{3,2},{4,5},{5,4},{6,7},{7,6},{8,9},{9,8},{10,11... | collective-permute-start | bytes 786440 | tf_op jit(solution)/shard_map/ppermute | solution.py:355
  85.0 1.2 %collective-permute-done.2.other_ref = f32[64,8,128]{2,1,0:T(8,128)S(1)} collective-permute-done((f32[64,8,128]{2,1,0:T(8,128)S(1)}, f32[64,8,128]{2,1,0:T(8,128)S(1)}, u32[]{:S(2)}, u32[]{:S(2)}) %collective-permute-start.2) | collective-permute-done | bytes 262176 | tf_op jit(solution)/shard_map/ppermute | solution.py:355
  86.1 3.7 %finish.1 = (f32[16,108]{1,0:T(8,128)}, f32[16,108]{1,0:T(8,128)}) custom-call(f32[48,48]{1,0:T(8,128)S(1)} %get-tuple-element.52.inverse_ref, f32[48,48]{1,0:T(8,128)S(1)} %get-tuple-element.53.stiff_ref, f32[64,8,128]{2,1,0:T(8,128)S(1)} %all-to-all-done.2.own_ref, f32[64,8,128]{2,1,0:T(8,128)S(1)} %collective-permute-done.2.other_ref, ...), custom_call_target="tpu_custom_call" | custom-call | flops 268435456 | bytes 4194304 | tf_op jit(solution)/shard_map/finish/pallas_call | solution.py:337
  (12 shorter events, 0.0 us)
Async XLA Ops:
  2.5 26.3 %all-to-all-start = ((f32[64,32,108]{2,1,0:T(8,128)}), f32[64,32,108]{2,1,0:T(8,128)S(1)}, u32[]{:S(2)}, u32[]{:S(2)}) async-start(f32[64,32,108]{2,1,0:T(8,128)} %broadcast_in_dim.14), calls=%async_computation | async-start | bytes 2097152 | tf_op jit(solution)/shard_map/all_to_all | solution.py:351
  28.8 6.8 %copy-start = (f32[64,32,108]{2,1,0:T(8,128)}, f32[64,32,108]{2,1,0:T(8,128)S(1)}, u32[]{:S(2)}) copy-start(f32[64,32,108]{2,1,0:T(8,128)S(1)} %all-to-all-done.own_ref) | copy-start | bytes 2654212
  28.8 4.7 %collective-permute-start = (f32[64,32,108]{2,1,0:T(8,128)S(1)}, f32[64,32,108]{2,1,0:T(8,128)S(1)}, u32[]{:S(2)}, u32[]{:S(2)}) collective-permute-start(f32[64,32,108]{2,1,0:T(8,128)S(1)} %all-to-all-done.own_ref), channel_id=1, source_target_pairs={{0,1},{1,0},{2,3},{3,2},{4,5},{5,4},{6,7},{7,6},{8,9},{9,8},{10,11... | collective-permute-start | bytes 2654216 | tf_op jit(solution)/shard_map/ppermute | solution.py:355
  33.5 12.5 %copy-start.1 = (f32[64,32,108]{2,1,0:T(8,128)}, f32[64,32,108]{2,1,0:T(8,128)S(1)}, u32[]{:S(2)}) copy-start(f32[64,32,108]{2,1,0:T(8,128)S(1)} %collective-permute-done.other_ref) | copy-start | bytes 2654212
  35.6 17.6 %all-to-all-start.1 = ((f32[64,16,128]{2,1,0:T(8,128)}), f32[64,16,128]{2,1,0:T(8,128)S(1)}, u32[]{:S(2)}, u32[]{:S(2)}) async-start(f32[64,16,128]{2,1,0:T(8,128)} %get-tuple-element.36), calls=%async_computation.1 | async-start | bytes 1048576 | tf_op jit(solution)/shard_map/all_to_all | solution.py:351
  46.0 9.2 %copy-start.2 = (f32[108,16]{0,1:T(8,128)S(1)}, f32[108,16]{0,1:T(8,128)}, u32[]{:S(2)}) copy-start(f32[108,16]{0,1:T(8,128)} %param.4) | copy-start | bytes 20740
  46.0 9.2 %copy-start.3 = (f32[108,16]{0,1:T(8,128)S(1)}, f32[108,16]{0,1:T(8,128)}, u32[]{:S(2)}) copy-start(f32[108,16]{0,1:T(8,128)} %param.5) | copy-start | bytes 20740
  53.2 3.6 %collective-permute-start.1 = (f32[64,16,128]{2,1,0:T(8,128)S(1)}, f32[64,16,128]{2,1,0:T(8,128)S(1)}, u32[]{:S(2)}, u32[]{:S(2)}) collective-permute-start(f32[64,16,128]{2,1,0:T(8,128)S(1)} %all-to-all-done.1.own_ref), channel_id=1, source_target_pairs={{0,1},{1,0},{2,3},{3,2},{4,5},{5,4},{6,7},{7,6},{8,9},{9,8},{10,11... | collective-permute-start | bytes 1572872 | tf_op jit(solution)/shard_map/ppermute | solution.py:355
  65.8 17.6 %all-to-all-start.2 = ((f32[64,8,128]{2,1,0:T(8,128)}), f32[64,8,128]{2,1,0:T(8,128)S(1)}, u32[]{:S(2)}, u32[]{:S(2)}) async-start(f32[64,8,128]{2,1,0:T(8,128)} %get-tuple-element.46), calls=%async_computation.2 | async-start | bytes 524288 | tf_op jit(solution)/shard_map/all_to_all | solution.py:351
  83.4 2.7 %collective-permute-start.2 = (f32[64,8,128]{2,1,0:T(8,128)S(1)}, f32[64,8,128]{2,1,0:T(8,128)S(1)}, u32[]{:S(2)}, u32[]{:S(2)}) collective-permute-start(f32[64,8,128]{2,1,0:T(8,128)S(1)} %all-to-all-done.2.own_ref), channel_id=1, source_target_pairs={{0,1},{1,0},{2,3},{3,2},{4,5},{5,4},{6,7},{7,6},{8,9},{9,8},{10,11... | collective-permute-start | bytes 786440 | tf_op jit(solution)/shard_map/ppermute | solution.py:355

commit v7 on v5

--- a/solution.py
+++ b/solution.py
@@ -119,10 +119,44 @@
             parts_ref[NEIG * number : NEIG * (number + 1), LANES * chip : LANES * (chip + 1)] = part
 
 
+def take_both(tile_of, first_ref, second_ref):
+    for chip in range(CHIPS):
+        lanes = slice(LANES * chip, LANES * (chip + 1))
+        for number, part in enumerate(split(tile_of(chip))):
+            first_ref[NEIG * number : NEIG * (number + 1), lanes] = part[:NEIG]
+            second_ref[NEIG * number : NEIG * (number + 1), lanes] = part[NEIG:]
+
+
+def stacked_dot(left, right):
+    high, low = split(left)
+    right_high, right_low = split(right)
+    both = jnp.dot(jnp.concatenate([high, low], axis=0), right_high, preferred_element_type=F32)
+    size = left.shape[0]
+    return both[:size] + (both[size:] + jnp.dot(high, right_low, preferred_element_type=F32))
+
+
+def eliminated(matrix):
+    size = matrix.shape[0]
+    row = lax.broadcasted_iota(jnp.int32, (size, size), 0)
+    column = lax.broadcasted_iota(jnp.int32, (size, size), 1)
+    identity = jnp.where(row == column, 1.0, 0.0).astype(F32)
+    work = jnp.concatenate([matrix, identity], axis=1)
+    below = lax.broadcasted_iota(jnp.int32, (size, 1), 0)
+    for k in range(size):
+        factor = jnp.where(below > k, work[:, k : k + 1] / work[k : k + 1, k : k + 1], 0.0)
+        work = work - factor * work[k : k + 1, :]
+    pivots = jnp.sum(work[:, :size] * identity, axis=1, keepdims=True)
+    return work[:, size:] / jnp.sqrt(pivots)
+
+
+def joined(blocks):
+    return jnp.concatenate([jnp.concatenate(row, axis=1) for row in blocks], axis=0)
+
+
 def image_own_kernel(h_ref, own_ref, product_ref, next_ref, h_vmem, parts, sems):
     copy = started(h_ref.at[0], h_vmem, sems.at[0])
     following = started(h_ref.at[1], next_ref, sems.at[1])
-    take_parts(lambda chip: padded(own_ref[SLOTS[0][chip], 0:NEIG]), parts)
+    take_both(lambda chip: padded(own_ref[SLOTS[0][chip]]), parts.at[pl.ds(0, STACK)], parts.at[pl.ds(STACK, STACK)])
     copy.wait()
     product_ref[...] = nt(h_vmem[...], parts[...])
     following.wait()
@@ -130,25 +164,27 @@
 
 def image_other_kernel(h_ref, other_ref, product_ref, tile_ref, image_ref, sent_ref, parts):
     take_parts(lambda chip: padded(other_ref[SLOTS[0][chip], 0:NEIG]), parts)
-    image = fold_rows(product_ref[...] + nt(h_ref[...], parts[...]))
+    image = fold_rows(product_ref[:, 0:STACK] + nt(h_ref[...], parts[...]))
     image_ref[...] = image
     sent = image + tile_ref[...]
     for chip in range(CHIPS):
         sent_ref[chip] = sent
 
 
-def previous_kernel(h_ref, own_ref, other_ref, image_ref, c_out, p_out, gram_ref, h_vmem, c_ref, p_ref, sems):
-    copy = started(h_ref, h_vmem, sems.at[0])
-    for half, ref in ((0, own_ref), (1, other_ref)):
-        take_parts(lambda chip: padded(ref[SLOTS[0][chip], 0:NEIG]), c_ref.at[half])
-        take_parts(lambda chip: padded(ref[SLOTS[0][chip], NEIG : 2 * NEIG]), p_ref.at[half])
+def previous_kernel(h_ref, own_ref, other_ref, product_ref, image_ref, c_out, p_out, inverse_ref, h_vmem, c_ref, p_ref, sems):
+    copy = started(h_ref.at[1], h_vmem, sems.at[0])
+    take_both(lambda chip: padded(own_ref[SLOTS[0][chip]]), c_ref.at[0], p_ref.at[0])
+    take_both(lambda chip: padded(other_ref[SLOTS[0][chip]]), c_ref.at[1], p_ref.at[1])
     out_c = started(c_ref, c_out, sems.at[1])
     out_p = started(p_ref, p_out, sems.at[2])
-    gram_ref[0] = fold(nt(c_ref[0], c_ref[0]) + nt(c_ref[1], c_ref[1]))
-    gram_ref[1] = fold(nt(p_ref[0], c_ref[0]) + nt(p_ref[1], c_ref[1]))
-    gram_ref[2] = fold(nt(p_ref[0], p_ref[0]) + nt(p_ref[1], p_ref[1]))
+    cc = fold(nt(c_ref[0], c_ref[0]) + nt(c_ref[1], c_ref[1]))
+    pc = fold(nt(p_ref[0], c_ref[0]) + nt(p_ref[1], c_ref[1]))
+    pp = fold(nt(p_ref[0], p_ref[0]) + nt(p_ref[1], p_ref[1]))
+    empty = jnp.zeros((NEIG, NEIG), F32)
+    low = joined([[0.5 * cc, empty], [pc, 0.5 * pp]])
+    inverse_ref[...] = eliminated(low + low.T)
     copy.wait()
-    image_ref[...] = fold_rows(nt(h_vmem[0], p_ref[0]) + nt(h_vmem[1], p_ref[1]))
+    image_ref[...] = fold_rows(product_ref[:, STACK:] + nt(h_vmem[...], p_ref[1]))
     out_c.wait()
     out_p.wait()
 
@@ -172,9 +208,9 @@
 def search_kernel(
     h_ref, own_ref, other_ref, c_hbm, i_own_ref, half_cross_ref, diag_ref, cvec_ref, pvec_ref, pimage_ref, image_ref, tile_ref,
     search_ref, rms_ref, cross_ref, sent_ref, kept_ref,
-    h_vmem, c_ref, i_ref, s_ref, resid_ref, other_diag_ref, sems, h_sems,
+    h_vmem, c_ref, i_ref, s_ref, resid_ref, other_diag_ref, sems, h_sems, c_sem,
 ):
-    copy_c = started(c_hbm, c_ref, sems.at[3])
+    copy_c = started(c_hbm, c_ref, c_sem)
     copies = [started(h_ref.at[half], h_vmem.at[half], h_sems.at[half]) for half in range(2)]
     take_parts(lambda chip: real_lanes(other_ref[SLOTS[1][chip]]), i_ref)
     for chip in range(CHIPS):
@@ -233,49 +269,29 @@
         copy.wait()
 
 
-def factor_kernel(
-    kept_hbm, c_hbm, p_hbm, gram_ref, cross_ref, inverse_ref, stiff_ref, kept_ref, c_ref, p_ref, sems,
-):
-    pairs = ((kept_hbm, kept_ref), (c_hbm, c_ref), (p_hbm, p_ref))
-    s_ref, i_ref = kept_ref.at[pl.ds(0, 2)], kept_ref.at[pl.ds(2, 2)]
-    for copy in [started(a, b, sems.at[n]) for n, (a, b) in enumerate(pairs)]:
-        copy.wait()
-
-    def gram(left, right):
-        return fold(nt(left[0], right[0]) + nt(left[1], right[1]))
-
+def factor_kernel(kept_hbm, c_hbm, p_hbm, first_ref, cross_ref, inverse_ref, stiff_ref, all_ref, sems):
+    copies = []
+    for half in range(2):
+        for number, source in enumerate((kept_hbm.at[half], kept_hbm.at[2 + half], c_hbm.at[half], p_hbm.at[half])):
+            copies.append(started(source, all_ref.at[half, pl.ds(STACK * number, STACK)], sems.at[half, number]))
+    with_search, p_image = None, None
+    for half in range(2):
+        for copy in copies[4 * half : 4 * half + 4]:
+            copy.wait()
+        terms = nt(all_ref[half], all_ref[half, :STACK])
+        with_search = terms if half == 0 else with_search + terms
+        terms = nt(all_ref[half, 3 * STACK :], all_ref[half, STACK : 2 * STACK])
+        p_image = terms if half == 0 else p_image + terms
+    ss, i_s, cs, ps = [fold(with_search[STACK * n : STACK * (n + 1)]) for n in range(4)]
+    first = first_ref[...]
+    row = nt_exact(jnp.concatenate([cs.T, ps.T], axis=1), first)
+    last = eliminated(ss - nt_exact(row, row))
+    inverse_ref[...] = joined(
+        [[first, jnp.zeros((2 * NEIG, NEIG), F32)], [-dot_exact(last, dot_exact(row, first)), last]]
+    )
     empty = jnp.zeros((NEIG, NEIG), F32)
-    cc, pc, pp = gram_ref[0], gram_ref[1], gram_ref[2]
-    sc, ss, ps = gram(s_ref, c_ref), gram(s_ref, s_ref), gram(p_ref, s_ref)
-    low = jnp.concatenate(
-        [
-            jnp.concatenate([0.5 * cc, empty, empty], axis=1),
-            jnp.concatenate([sc, 0.5 * ss, empty], axis=1),
-            jnp.concatenate([pc, ps, 0.5 * pp], axis=1),
-        ],
-        axis=0,
-    )
-    mass = low + low.T
-    low = jnp.concatenate(
-        [
-            jnp.concatenate([0.5 * cross_ref[...], empty, empty], axis=1),
-            jnp.concatenate([gram(s_ref, i_ref), empty, empty], axis=1),
-            jnp.concatenate([gram(p_ref, i_ref), empty, empty], axis=1),
-        ],
-        axis=0,
-    )
+    low = joined([[0.5 * cross_ref[...], empty, i_s], [fold(p_image), empty, empty], [empty, empty, empty]])
     stiff_ref[...] = low + low.T
-    size = 3 * NEIG
-    row = lax.broadcasted_iota(jnp.int32, (size, size), 0)
-    column = lax.broadcasted_iota(jnp.int32, (size, size), 1)
-    identity = jnp.where(row == column, 1.0, 0.0).astype(F32)
-    work = jnp.concatenate([mass, identity], axis=1)
-    below = lax.broadcasted_iota(jnp.int32, (size, 1), 0)
-    for k in range(size):
-        factor = jnp.where(below > k, work[:, k : k + 1] / work[k : k + 1, k : k + 1], 0.0)
-        work = work - factor * work[k : k + 1, :]
-    pivots = jnp.sum(work[:, :size] * identity, axis=1, keepdims=True)
-    inverse_ref[...] = work[:, size:] / jnp.sqrt(pivots)
 
 
 def finish_kernel(inverse_ref, stiff_ref, own_ref, other_ref, c_ref, s_ref, p_ref, current_ref, previous_ref):
@@ -286,15 +302,8 @@
     terms = jnp.concatenate([total[:, 0 : 3 * NEIG], total[:, 4 * NEIG : 7 * NEIG]], axis=0)
     ss, sp, pp = terms[:, 0:16], terms[:, 16:32], terms[:, 32:48]
     empty = jnp.zeros((NEIG, NEIG), F32)
-    up = jnp.concatenate(
-        [
-            jnp.zeros((NEIG, size), F32),
-            jnp.concatenate([empty, 0.5 * ss, sp], axis=1),
-            jnp.concatenate([empty, empty, 0.5 * pp], axis=1),
-        ],
-        axis=0,
-    )
-    stiff = stiff_ref[...] + (up + up.T)
+    low = joined([[empty, empty, empty], [empty, 0.5 * pp, empty], [empty, sp, 0.5 * ss]])
+    stiff = stiff_ref[...] + (low + low.T)
     inverse = inverse_ref[...]
     reduced = nt_exact(dot_exact(inverse, stiff), inverse)
     row = lax.broadcasted_iota(jnp.int32, (size, size), 0)
@@ -303,20 +312,20 @@
     diagonal = jnp.sum(reduced * identity, axis=1, keepdims=True)
     level = jnp.max(diagonal[:NEIG], axis=0, keepdims=True)
     signed = level * identity - reduced
-    square = dot_exact(signed, signed)
+    square = stacked_dot(signed, signed)
     total = jnp.sum(jnp.sum(signed * signed, axis=1, keepdims=True), axis=0, keepdims=True)
     square = square / total
     signed = signed / jnp.sqrt(total)
     for step in range(SIGN_STEPS):
         if step > 0:
-            square = dot_exact(signed, signed)
-        signed = dot_exact(signed, 1.5 * identity - 0.5 * square)
+            square = stacked_dot(signed, signed)
+        signed = stacked_dot(signed, 1.5 * identity - 0.5 * square)
     projector = 0.5 * (identity + signed)
     wanted = jnp.where(lax.broadcasted_iota(jnp.int32, (size, size), 1) < NEIG, projector, 0.0)
     tn = (((0,), (0,)), ((), ()))
     coeffs_t = lax.dot_general(wanted, inverse, tn, precision=HIGHEST, preferred_element_type=F32)[0:NEIG]
     coeffs_t = coeffs_t * math.sqrt(ORDER)
-    basis = jnp.concatenate([c_ref[...], s_ref[...], p_ref[...]], axis=0)
+    basis = jnp.concatenate([c_ref[...], p_ref[...], s_ref[...]], axis=0)
     current_ref[...] = dot_exact(coeffs_t, basis)[:, :ROWS]
     lane = lax.broadcasted_iota(jnp.int32, (NEIG, size), 1)
     previous_ref[...] = dot_exact(jnp.where(lane < NEIG, 0.0, coeffs_t), basis)[:, :ROWS]
@@ -363,31 +372,31 @@
     h_parts = prepare(hamiltonian)
     v_own, h_parts, tile = lax.optimization_barrier((v_own, h_parts, tile))
     v_other = to_core(v_own)
-    block, parts, half = ((NEIG, LANES), F32), ((2, STACK, HALF), BF16), ((STACK, HALF), BF16)
-    parts_vmem, half_vmem = pltpu.VMEM(*parts), pltpu.VMEM(*half)
+    block, half, parts = ((NEIG, LANES), F32), ((STACK, HALF), BF16), ((2, STACK, HALF), BF16)
+    half_vmem, parts_vmem = pltpu.VMEM(*half), pltpu.VMEM(*parts)
     h_vmem = pltpu.VMEM((2, PARTS * TALL, HALF), BF16)
     h_half = pltpu.VMEM((PARTS * TALL, HALF), BF16)
     dma = pltpu.SemaphoreType.DMA
     product, h_next = kernel_call(
         image_own_kernel,
-        [((PARTS * TALL, STACK), F32), ((PARTS * TALL, HALF), BF16)],
+        [((PARTS * TALL, 2 * STACK), F32), ((PARTS * TALL, HALF), BF16)],
         (h_parts, v_own),
         1 << 30,
         "image_own",
-        [h_half, half_vmem, dma((2,))], (0,), limit=LIMIT_IMAGE,
+        [h_half, pltpu.VMEM((2 * STACK, HALF), BF16), dma((2,))], (0,), limit=LIMIT_IMAGE,
     )
     image, sent = kernel_call(
         image_other_kernel, [block, ((CHIPS, NEIG, LANES), F32)], (h_next, v_other, product, tile), 1 << 30, "image_other",
         [half_vmem], limit=LIMIT_IMAGE,
     )
     i_own = to_chips(sent, 1)
-    p_image, c_parts, p_parts, grams = kernel_call(
+    p_image, c_parts, p_parts, first = kernel_call(
         previous_kernel,
-        [block, parts, parts, ((3, NEIG, NEIG), F32)],
-        (h_parts, v_own, v_other),
+        [block, parts, parts, ((2 * NEIG, 2 * NEIG), F32)],
+        (h_parts, v_own, v_other, product),
         6 << 30,
         "previous",
-        [h_vmem, parts_vmem, parts_vmem, dma((3,))], (0,), (1, 2),
+        [h_half, parts_vmem, parts_vmem, dma((3,))], (0,), (1, 2),
     )
     i_own, p_image, c_parts = lax.optimization_barrier((i_own, p_image, c_parts))
     i_other = to_core(i_own)
@@ -405,14 +414,14 @@
         (h_parts, i_own, i_other, c_parts, i_own_parts, half_cross, diag, cvec, pvec, p_image, image, tile),
         6 << 30,
         "search",
-        [h_vmem, parts_vmem, half_vmem, parts_vmem, pltpu.VMEM((2, NEIG, HALF), F32), pltpu.VMEM((CHIPS, LANES), F32), dma((4,)), dma((2,))],
+        [h_vmem, parts_vmem, half_vmem, parts_vmem, pltpu.VMEM((2, NEIG, HALF), F32), pltpu.VMEM((CHIPS, LANES), F32), dma((3,)), dma((2,)), dma(())],
         (0, 3), (4,), limit=LIMIT_SEARCH,
     )
     r_own = to_chips(sent, 2)
     square = ((3 * NEIG, 3 * NEIG), F32)
     inverse, stiff = kernel_call(
-        factor_kernel, [square, square], (kept, c_parts, p_parts, grams, cross), 6 << 30, "factor",
-        [pltpu.VMEM((4, STACK, HALF), BF16), parts_vmem, parts_vmem, dma((3,))], (0, 1, 2),
+        factor_kernel, [square, square], (kept, c_parts, p_parts, first, cross), 6 << 30, "factor",
+        [pltpu.VMEM((2, 4 * STACK, HALF), BF16), dma((2, 4))], (0, 1, 2),
     )
     r_own, inverse, rms = lax.optimization_barrier((r_own, inverse, rms[:, 0]))
     r_other = to_core(r_own)

time: 88.4 us -> 87.9 us (level)
  Pallas kernels: 40.9 us -> 39.1 us
  waiting for transfers between devices: 5.79 us -> 7.55 us
    pallas_call x7, Pallas kernels: 33 us -> 31.2 us  [kernel_call(): pl.pallas_call(body, out_shape=[jax.ShapeDtypeStruct(shape, kind) for sha...]
    all_to_all x3, waiting for transfers between devices: 4.45 us -> 6.21 us  [to_chips(): return lax.all_to_all(x, AXIS, 0, 0, axis_index_groups=groups, tiled=True)]
  transfers between devices with their start and end apart: 6 -> 6, of which waited for: 4 -> 4; matrix products, arithmetic and copies ran while one was open for 2% -> 2% of each run, Pallas kernels for 32% -> 31%
where the time goes in v7:
time: 87.9 us; the launch traced here: 87.4 us
  Pallas kernels  39.1 us (44%)
  starting transfers between devices  36.2 us (41%)
  waiting for transfers between devices  7.55 us (9%)
  other arithmetic  2.36 us (3%)
  local copies, waits for them, and re-layouts  1.17 us (1%)
    all_to_all x3, starting transfers between devices, to_chips(): return lax.all_to_all(x, AXIS, 0, 0, axis_index_groups=groups, tiled=True)  31.8 us
    pallas_call x7, Pallas kernels, kernel_call(): pl.pallas_call(body, out_shape=[jax.ShapeDtypeStruct(shape, kind) for sha...  31.2 us
    pallas_call x1, Pallas kernels, prepare(): pl.pallas_call(prepare_kernel, grid=(CHUNKS,), out_shape=jax.ShapeDtypeSt...  7.93 us
    all_to_all x3, waiting for transfers between devices, to_chips(): return lax.all_to_all(x, AXIS, 0, 0, axis_index_groups=groups, tiled=True)  6.21 us
    ppermute x3, starting transfers between devices, to_core(): lax.ppermute(x, AXIS, [(device, device ^ 1) for device in range(DEVICES)])  4.41 us
  transfers between devices with their start and end apart: 6, of which 4 were waited for; matrix products, arithmetic and copies ran while one was open for 2% of the time, Pallas kernels for 31%

profile of v7, /device:TPU:1, one launch (start us, length us, event | category | flops | bytes accessed | tf_op | source)
XLA Modules:
  0.0 87.4 jit_solution(2976650225462980319)
XLA Ops:
  0.6 0.7 pad_maximum_fusion
  1.4 1.1 %broadcast_in_dim.14 = f32[64,32,108]{2,1,0:T(8,128)} broadcast(f32[32,108]{1,0:T(8,128)S(1)} %pad_maximum_fusion), dimensions={1,2} | broadcast | bytes 898560 | tf_op jit(solution)/shard_map/broadcast_in_dim | solution.py:368
  2.5 13.7 %all-to-all-start = ((f32[64,32,108]{2,1,0:T(8,128)}), f32[64,32,108]{2,1,0:T(8,128)S(1)}, u32[]{:S(2)}, u32[]{:S(2)}) async-start(f32[64,32,108]{2,1,0:T(8,128)} %broadcast_in_dim.14), calls=%async_computation | async-start | bytes 2097152 | tf_op jit(solution)/shard_map/all_to_all | solution.py:349
  16.2 1.0 %select_reduce_fusion = f32[108]{0:T(128)S(1)} fusion(f32[108,13824]{1,0:T(8,128)} %h_ref.1, s32[]{:T(128)S(6)} %select_n.34), kind=kLoop, calls=%fused_computation.1 | loop fusion | flops 34884 | bytes 47092 | tf_op jit(solution)/shard_map/reduce_sum | solution.py:360
  17.3 7.9 %prepare.1.h_ref = bf16[2,224,8192]{2,1,0:T(8,128)(2,1)} custom-call(f32[108,13824]{1,0:T(8,128)} %h_ref.1), custom_call_target="tpu_custom_call" | custom-call | flops 29859840 | bytes 14929920 | tf_op jit(solution)/shard_map/prepare/pallas_call | solution.py:98
  25.2 0.2 fusion.tile_ref
  25.4 3.4 %all-to-all-done.own_ref = f32[64,32,108]{2,1,0:T(8,128)S(1)} async-done(((f32[64,32,108]{2,1,0:T(8,128)}), f32[64,32,108]{2,1,0:T(8,128)S(1)}, u32[]{:S(2)}, u32[]{:S(2)}) %all-to-all-start) | async-done | bytes 884768 | tf_op jit(solution)/shard_map/all_to_all | solution.py:349
  28.8 1.6 %collective-permute-start = (f32[64,32,108]{2,1,0:T(8,128)S(1)}, f32[64,32,108]{2,1,0:T(8,128)S(1)}, u32[]{:S(2)}, u32[]{:S(2)}) collective-permute-start(f32[64,32,108]{2,1,0:T(8,128)S(1)} %all-to-all-done.own_ref), channel_id=1, source_target_pairs={{0,1},{1,0},{2,3},{3,2},{4,5},{5,4},{6,7},{7,6},{8,9},{9,8},{10,11... | collective-permute-start | bytes 2654216 | tf_op jit(solution)/shard_map/ppermute | solution.py:353
  30.3 3.2 %image_own.1 = (f32[224,64]{1,0:T(8,128)S(1)}, bf16[224,8192]{1,0:T(8,128)(2,1)S(1)}) custom-call(bf16[2,224,8192]{2,1,0:T(8,128)(2,1)} %prepare.1.h_ref, f32[64,32,108]{2,1,0:T(8,128)S(1)} %all-to-all-done.own_ref), custom_call_target="tpu_custom_call" | custom-call | flops 1073741824 | bytes 4194304 | tf_op jit(solution)/shard_map/image_own/pallas_call | solution.py:335
  33.5 2.0 %image_other.1 = (f32[16,128]{1,0:T(8,128)S(1)}, f32[64,16,128]{2,1,0:T(8,128)}) custom-call(bf16[224,8192]{1,0:T(8,128)(2,1)S(1)} %get-tuple-element.34.h_ref, f32[64,32,108]{2,1,0:T(8,128)S(1)} %collective-permute-done.other_ref, f32[224,64]{1,0:T(8,128)S(1)} %get-tuple-element.35.product_ref, f32[16,128]{1,0:T(8,128)S(1)} %fusion.tile_ref), custom_call_target="tpu_custom_call" | custom-call | flops 1073741824 | bytes 4194304 | tf_op jit(solution)/shard_map/image_other/pallas_call | solution.py:335
  35.6 10.4 %all-to-all-start.1 = ((f32[64,16,128]{2,1,0:T(8,128)}), f32[64,16,128]{2,1,0:T(8,128)S(1)}, u32[]{:S(2)}, u32[]{:S(2)}) async-start(f32[64,16,128]{2,1,0:T(8,128)} %get-tuple-element.37), calls=%async_computation.1 | async-start | bytes 1048576 | tf_op jit(solution)/shard_map/all_to_all | solution.py:349
  46.0 0.0 copy-start.3
  46.0 7.9 %previous.1 = (f32[16,128]{1,0:T(8,128)S(1)}, bf16[2,32,8192]{2,1,0:T(8,128)(2,1)}, bf16[2,32,8192]{2,1,0:T(8,128)(2,1)}, f32[32,32]{1,0:T(8,128)S(1)}) custom-call(bf16[2,224,8192]{2,1,0:T(8,128)(2,1)} %prepare.1.h_ref, f32[64,32,108]{2,1,0:T(8,128)} %copy-done, f32[64,32,108]{2,1,0:T(8,128)} %copy-done.1, f32[224,64]{1,0:T(8,128)S(1)} %get-tuple-element.35.product_ref), custom_call_target="tpu_custom_call" | custom-call | flops 6442450944 | bytes 4194304 | tf_op jit(solution)/shard_map/previous/pallas_call | solution.py:335
  53.9 1.3 %collective-permute-start.1 = (f32[64,16,128]{2,1,0:T(8,128)S(1)}, f32[64,16,128]{2,1,0:T(8,128)S(1)}, u32[]{:S(2)}, u32[]{:S(2)}) collective-permute-start(f32[64,16,128]{2,1,0:T(8,128)S(1)} %all-to-all-done.1.own_ref), channel_id=1, source_target_pairs={{0,1},{1,0},{2,3},{3,2},{4,5},{5,4},{6,7},{7,6},{8,9},{9,8},{10,11... | collective-permute-start | bytes 1572872 | tf_op jit(solution)/shard_map/ppermute | solution.py:353
  55.3 1.3 %own.1 = (bf16[32,8192]{1,0:T(8,128)(2,1)S(1)}, f32[32,32]{1,0:T(8,128)S(1)}, f32[64,128]{1,0:T(8,128)S(1)}) custom-call(f32[64,16,128]{2,1,0:T(8,128)S(1)} %all-to-all-done.1.own_ref, bf16[2,32,8192]{2,1,0:T(8,128)(2,1)} %get-tuple-element.41.c_hbm), custom_call_target="tpu_custom_call" | custom-call | flops 1073741824 | bytes 4194304 | tf_op jit(solution)/shard_map/own/pallas_call | solution.py:335
  56.6 0.2 collective-permute-done.1.other_ref
  56.8 6.9 %search.1 = (f32[16,128]{1,0:T(8,128)S(1)}, f32[16,1]{1,0:T(8,128)S(1)}, f32[16,16]{1,0:T(8,128)S(1)}, f32[64,8,128]{2,1,0:T(8,128)}, bf16[4,32,8192]{2,1,0:T(8,128)(2,1)}) custom-call(bf16[2,224,8192]{2,1,0:T(8,128)(2,1)} %prepare.1.h_ref, f32[64,16,128]{2,1,0:T(8,128)S(1)} %all-to-all-done.1.own_ref, f32[64,16,128]{2,1,0:T(8,128)S(1)} %collective-permute-done.1.other_ref, ...), custom_call_target="tpu_custom_call" | custom-call | flops 6442450944 | bytes 4194304 | tf_op jit(solution)/shard_map/search/pallas_call | solution.py:335
  63.7 7.6 %all-to-all-start.2 = ((f32[64,8,128]{2,1,0:T(8,128)}), f32[64,8,128]{2,1,0:T(8,128)S(1)}, u32[]{:S(2)}, u32[]{:S(2)}) async-start(f32[64,8,128]{2,1,0:T(8,128)} %get-tuple-element.47), calls=%async_computation.2 | async-start | bytes 524288 | tf_op jit(solution)/shard_map/all_to_all | solution.py:349
  71.4 6.5 %factor.1 = (f32[48,48]{1,0:T(8,128)S(1)}, f32[48,48]{1,0:T(8,128)S(1)}) custom-call(bf16[4,32,8192]{2,1,0:T(8,128)(2,1)} %get-tuple-element.48.kept_hbm, bf16[2,32,8192]{2,1,0:T(8,128)(2,1)} %get-tuple-element.41.c_hbm, bf16[2,32,8192]{2,1,0:T(8,128)(2,1)} %get-tuple-element.49.p_hbm, f32[32,32]{1,0:T(8,128)S(1)} %get-tuple-element.50.first_ref, ...), custom_call_target="tpu_custom_call" | custom-call | flops 6442450944 | bytes 4194304 | tf_op jit(solution)/shard_map/factor/pallas_call | solution.py:335
  77.9 0.6 reduce
  78.5 2.8 %all-to-all-done.2.own_ref = f32[64,8,128]{2,1,0:T(8,128)S(1)} async-done(((f32[64,8,128]{2,1,0:T(8,128)}), f32[64,8,128]{2,1,0:T(8,128)S(1)}, u32[]{:S(2)}, u32[]{:S(2)}) %all-to-all-start.2) | async-done | bytes 262176 | tf_op jit(solution)/shard_map/all_to_all | solution.py:349
  81.4 1.6 %collective-permute-start.2 = (f32[64,8,128]{2,1,0:T(8,128)S(1)}, f32[64,8,128]{2,1,0:T(8,128)S(1)}, u32[]{:S(2)}, u32[]{:S(2)}) collective-permute-start(f32[64,8,128]{2,1,0:T(8,128)S(1)} %all-to-all-done.2.own_ref), channel_id=1, source_target_pairs={{0,1},{1,0},{2,3},{3,2},{4,5},{5,4},{6,7},{7,6},{8,9},{9,8},{10,11... | collective-permute-start | bytes 786440 | tf_op jit(solution)/shard_map/ppermute | solution.py:353
  82.9 1.2 %collective-permute-done.2.other_ref = f32[64,8,128]{2,1,0:T(8,128)S(1)} collective-permute-done((f32[64,8,128]{2,1,0:T(8,128)S(1)}, f32[64,8,128]{2,1,0:T(8,128)S(1)}, u32[]{:S(2)}, u32[]{:S(2)}) %collective-permute-start.2) | collective-permute-done | bytes 262176 | tf_op jit(solution)/shard_map/ppermute | solution.py:353
  84.1 3.3 %finish.1 = (f32[16,108]{1,0:T(8,128)}, f32[16,108]{1,0:T(8,128)}) custom-call(f32[48,48]{1,0:T(8,128)S(1)} %get-tuple-element.54.inverse_ref, f32[48,48]{1,0:T(8,128)S(1)} %get-tuple-element.55.stiff_ref, f32[64,8,128]{2,1,0:T(8,128)S(1)} %all-to-all-done.2.own_ref, f32[64,8,128]{2,1,0:T(8,128)S(1)} %collective-permute-done.2.other_ref, ...), custom_call_target="tpu_custom_call" | custom-call | flops 268435456 | bytes 4194304 | tf_op jit(solution)/shard_map/finish/pallas_call | solution.py:335
  (12 shorter events, 0.0 us)
Async XLA Ops:
  2.5 26.3 %all-to-all-start = ((f32[64,32,108]{2,1,0:T(8,128)}), f32[64,32,108]{2,1,0:T(8,128)S(1)}, u32[]{:S(2)}, u32[]{:S(2)}) async-start(f32[64,32,108]{2,1,0:T(8,128)} %broadcast_in_dim.14), calls=%async_computation | async-start | bytes 2097152 | tf_op jit(solution)/shard_map/all_to_all | solution.py:349
  28.8 6.8 %copy-start = (f32[64,32,108]{2,1,0:T(8,128)}, f32[64,32,108]{2,1,0:T(8,128)S(1)}, u32[]{:S(2)}) copy-start(f32[64,32,108]{2,1,0:T(8,128)S(1)} %all-to-all-done.own_ref) | copy-start | bytes 2654212
  28.8 4.7 %collective-permute-start = (f32[64,32,108]{2,1,0:T(8,128)S(1)}, f32[64,32,108]{2,1,0:T(8,128)S(1)}, u32[]{:S(2)}, u32[]{:S(2)}) collective-permute-start(f32[64,32,108]{2,1,0:T(8,128)S(1)} %all-to-all-done.own_ref), channel_id=1, source_target_pairs={{0,1},{1,0},{2,3},{3,2},{4,5},{5,4},{6,7},{7,6},{8,9},{9,8},{10,11... | collective-permute-start | bytes 2654216 | tf_op jit(solution)/shard_map/ppermute | solution.py:353
  33.5 12.5 %copy-start.1 = (f32[64,32,108]{2,1,0:T(8,128)}, f32[64,32,108]{2,1,0:T(8,128)S(1)}, u32[]{:S(2)}) copy-start(f32[64,32,108]{2,1,0:T(8,128)S(1)} %collective-permute-done.other_ref) | copy-start | bytes 2654212
  35.6 18.4 %all-to-all-start.1 = ((f32[64,16,128]{2,1,0:T(8,128)}), f32[64,16,128]{2,1,0:T(8,128)S(1)}, u32[]{:S(2)}, u32[]{:S(2)}) async-start(f32[64,16,128]{2,1,0:T(8,128)} %get-tuple-element.37), calls=%async_computation.1 | async-start | bytes 1048576 | tf_op jit(solution)/shard_map/all_to_all | solution.py:349
  46.0 9.2 %copy-start.2 = (f32[108,16]{0,1:T(8,128)S(1)}, f32[108,16]{0,1:T(8,128)}, u32[]{:S(2)}) copy-start(f32[108,16]{0,1:T(8,128)} %param.4) | copy-start | bytes 20740
  46.0 9.2 %copy-start.3 = (f32[108,16]{0,1:T(8,128)S(1)}, f32[108,16]{0,1:T(8,128)}, u32[]{:S(2)}) copy-start(f32[108,16]{0,1:T(8,128)} %param.5) | copy-start | bytes 20740
  53.9 2.8 %collective-permute-start.1 = (f32[64,16,128]{2,1,0:T(8,128)S(1)}, f32[64,16,128]{2,1,0:T(8,128)S(1)}, u32[]{:S(2)}, u32[]{:S(2)}) collective-permute-start(f32[64,16,128]{2,1,0:T(8,128)S(1)} %all-to-all-done.1.own_ref), channel_id=1, source_target_pairs={{0,1},{1,0},{2,3},{3,2},{4,5},{5,4},{6,7},{7,6},{8,9},{9,8},{10,11... | collective-permute-start | bytes 1572872 | tf_op jit(solution)/shard_map/ppermute | solution.py:353
  63.7 17.6 %all-to-all-start.2 = ((f32[64,8,128]{2,1,0:T(8,128)}), f32[64,8,128]{2,1,0:T(8,128)S(1)}, u32[]{:S(2)}, u32[]{:S(2)}) async-start(f32[64,8,128]{2,1,0:T(8,128)} %get-tuple-element.47), calls=%async_computation.2 | async-start | bytes 524288 | tf_op jit(solution)/shard_map/all_to_all | solution.py:349
  81.4 2.7 %collective-permute-start.2 = (f32[64,8,128]{2,1,0:T(8,128)S(1)}, f32[64,8,128]{2,1,0:T(8,128)S(1)}, u32[]{:S(2)}, u32[]{:S(2)}) collective-permute-start(f32[64,8,128]{2,1,0:T(8,128)S(1)} %all-to-all-done.2.own_ref), channel_id=1, source_target_pairs={{0,1},{1,0},{2,3},{3,2},{4,5},{5,4},{6,7},{7,6},{8,9},{9,8},{10,11... | collective-permute-start | bytes 786440 | tf_op jit(solution)/shard_map/ppermute | solution.py:353

commit v8 on v7

--- a/solution.py
+++ b/solution.py
@@ -17,7 +17,7 @@
 LANES = 128
 FORWARD = list(range(CHIPS))
 BACKWARD = FORWARD[::-1]
-ORDERS = (BACKWARD, BACKWARD, FORWARD)
+ORDERS = (BACKWARD, BACKWARD, BACKWARD)
 SLOTS = [[order.index(chip) for chip in range(CHIPS)] for order in ORDERS]
 HALF = CHIPS * LANES
 TALL = 112
@@ -182,9 +182,9 @@
     pp = fold(nt(p_ref[0], p_ref[0]) + nt(p_ref[1], p_ref[1]))
     empty = jnp.zeros((NEIG, NEIG), F32)
     low = joined([[0.5 * cc, empty], [pc, 0.5 * pp]])
-    inverse_ref[...] = eliminated(low + low.T)
     copy.wait()
     image_ref[...] = fold_rows(product_ref[:, STACK:] + nt(h_vmem[...], p_ref[1]))
+    inverse_ref[...] = eliminated(low + low.T)
     out_c.wait()
     out_p.wait()
 
@@ -234,9 +234,9 @@
             part = part + resid * resid
         square = square + part
     rms = jnp.sqrt(jnp.sum(square, axis=1, keepdims=True) / ORDER + EPS)
-    rms_ref[...] = rms
     row = lax.broadcasted_iota(jnp.int32, (NEIG, NEIG), 0)
     column = lax.broadcasted_iota(jnp.int32, (NEIG, NEIG), 1)
+    rms_ref[...] = jnp.sum(jnp.where(row == column, rms, 0.0), axis=0)
     value = jnp.sum(jnp.where(row == column, ritz_t, 0.0), axis=1, keepdims=True)
     value = jnp.broadcast_to(value, (NEIG, LANES))
     rms = jnp.broadcast_to(rms, (NEIG, LANES))
@@ -305,6 +305,9 @@
     low = joined([[empty, empty, empty], [empty, 0.5 * pp, empty], [empty, sp, 0.5 * ss]])
     stiff = stiff_ref[...] + (low + low.T)
     inverse = inverse_ref[...]
+    basis = jnp.concatenate([c_ref[...], p_ref[...], s_ref[...]], axis=0)
+    rotated = dot_exact(inverse, basis)
+    rotated_rest = dot_exact(jnp.where(lax.broadcasted_iota(jnp.int32, (size, size), 1) < NEIG, 0.0, inverse), basis)
     reduced = nt_exact(dot_exact(inverse, stiff), inverse)
     row = lax.broadcasted_iota(jnp.int32, (size, size), 0)
     column = lax.broadcasted_iota(jnp.int32, (size, size), 1)
@@ -321,14 +324,12 @@
             square = stacked_dot(signed, signed)
         signed = stacked_dot(signed, 1.5 * identity - 0.5 * square)
     projector = 0.5 * (identity + signed)
-    wanted = jnp.where(lax.broadcasted_iota(jnp.int32, (size, size), 1) < NEIG, projector, 0.0)
-    tn = (((0,), (0,)), ((), ()))
-    coeffs_t = lax.dot_general(wanted, inverse, tn, precision=HIGHEST, preferred_element_type=F32)[0:NEIG]
-    coeffs_t = coeffs_t * math.sqrt(ORDER)
-    basis = jnp.concatenate([c_ref[...], p_ref[...], s_ref[...]], axis=0)
-    current_ref[...] = dot_exact(coeffs_t, basis)[:, :ROWS]
-    lane = lax.broadcasted_iota(jnp.int32, (NEIG, size), 1)
-    previous_ref[...] = dot_exact(jnp.where(lane < NEIG, 0.0, coeffs_t), basis)[:, :ROWS]
+    wanted = jnp.where(column < NEIG, projector, 0.0) * math.sqrt(ORDER)
+    applied = lax.dot_general(
+        wanted, jnp.concatenate([rotated, rotated_rest], axis=1), (((0,), (0,)), ((), ())), precision=HIGHEST, preferred_element_type=F32
+    )
+    current_ref[...] = applied[:NEIG, :ROWS]
+    previous_ref[...] = applied[:NEIG, LANES : LANES + ROWS]
 
 
 def kernel_call(body, outs, args, flops, name, scratch=(), in_hbm=(), out_hbm=(), limit=LIMIT):
@@ -410,7 +411,7 @@
     )
     search, rms, cross, sent, kept = kernel_call(
         search_kernel,
-        [block, ((NEIG, 1), F32), ((NEIG, NEIG), F32), ((CHIPS, 8, LANES), F32), ((4, STACK, HALF), BF16)],
+        [block, ((NEIG,), F32), ((NEIG, NEIG), F32), ((CHIPS, 8, LANES), F32), ((4, STACK, HALF), BF16)],
         (h_parts, i_own, i_other, c_parts, i_own_parts, half_cross, diag, cvec, pvec, p_image, image, tile),
         6 << 30,
         "search",
@@ -423,7 +424,7 @@
         factor_kernel, [square, square], (kept, c_parts, p_parts, first, cross), 6 << 30, "factor",
         [pltpu.VMEM((2, 4 * STACK, HALF), BF16), dma((2, 4))], (0, 1, 2),
     )
-    r_own, inverse, rms = lax.optimization_barrier((r_own, inverse, rms[:, 0]))
+    r_own, inverse = lax.optimization_barrier((r_own, inverse))
     r_other = to_core(r_own)
     new_current, new_previous = kernel_call(
         finish_kernel,

time: 87.9 us -> 85.8 us (0.976)
  waiting for transfers between devices: 7.55 us -> 4.81 us
  starting transfers between devices: 36.2 us -> 38.4 us
  Pallas kernels: 39.1 us -> 38.2 us
    all_to_all x3, waiting for transfers between devices: 6.21 us -> 3.47 us  [to_chips(): return lax.all_to_all(x, AXIS, 0, 0, axis_index_groups=groups, tiled=True)]
    all_to_all x3, starting transfers between devices: 31.8 us -> 34 us  [to_chips(): return lax.all_to_all(x, AXIS, 0, 0, axis_index_groups=groups, tiled=True)]
    pallas_call x7, Pallas kernels: 31.2 us -> 30.1 us  [kernel_call(): pl.pallas_call(body, out_shape=[jax.ShapeDtypeStruct(shape, kind) for sha...]
  transfers between devices with their start and end apart: 6 -> 6, of which waited for: 4 -> 4; matrix products, arithmetic and copies ran while one was open for 2% -> 1% of each run, Pallas kernels for 31% -> 31%
where the time goes in v8:
time: 85.8 us; the launch traced here: 85.2 us
  starting transfers between devices  38.4 us (45%)
  Pallas kernels  38.2 us (45%)
  waiting for transfers between devices  4.81 us (6%)
  other arithmetic  1.73 us (2%)
  local copies, waits for them, and re-layouts  1.19 us (1%)
    all_to_all x3, starting transfers between devices, to_chips(): return lax.all_to_all(x, AXIS, 0, 0, axis_index_groups=groups, tiled=True)  34 us
    pallas_call x7, Pallas kernels, kernel_call(): pl.pallas_call(body, out_shape=[jax.ShapeDtypeStruct(shape, kind) for sha...  30.1 us
    pallas_call x1, Pallas kernels, prepare(): pl.pallas_call(prepare_kernel, grid=(CHUNKS,), out_shape=jax.ShapeDtypeSt...  8.03 us
    ppermute x3, starting transfers between devices, to_core(): lax.ppermute(x, AXIS, [(device, device ^ 1) for device in range(DEVICES)])  4.39 us
    all_to_all x3, waiting for transfers between devices, to_chips(): return lax.all_to_all(x, AXIS, 0, 0, axis_index_groups=groups, tiled=True)  3.47 us
  transfers between devices with their start and end apart: 6, of which 4 were waited for; matrix products, arithmetic and copies ran while one was open for 1% of the time, Pallas kernels for 31%

profile of v8, /device:TPU:1, one launch (start us, length us, event | category | flops | bytes accessed | tf_op | source)
XLA Modules:
  0.0 85.2 jit_solution(4749804397203117348)
XLA Ops:
  0.6 0.7 pad_maximum_fusion
  1.4 1.2 %broadcast_in_dim.14 = f32[64,32,108]{2,1,0:T(8,128)} broadcast(f32[32,108]{1,0:T(8,128)S(1)} %pad_maximum_fusion), dimensions={1,2} | broadcast | bytes 898560 | tf_op jit(solution)/shard_map/broadcast_in_dim | solution.py:369
  2.5 13.7 %all-to-all-start = ((f32[64,32,108]{2,1,0:T(8,128)}), f32[64,32,108]{2,1,0:T(8,128)S(1)}, u32[]{:S(2)}, u32[]{:S(2)}) async-start(f32[64,32,108]{2,1,0:T(8,128)} %broadcast_in_dim.14), calls=%async_computation | async-start | bytes 2097152 | tf_op jit(solution)/shard_map/all_to_all | solution.py:350
  16.3 1.0 %select_reduce_fusion = f32[108]{0:T(128)S(1)} fusion(f32[108,13824]{1,0:T(8,128)} %h_ref.1, s32[]{:T(128)S(6)} %select_n.34), kind=kLoop, calls=%fused_computation.1 | loop fusion | flops 34884 | bytes 47092 | tf_op jit(solution)/shard_map/reduce_sum | solution.py:361
  17.3 8.0 %prepare.1.h_ref = bf16[2,224,8192]{2,1,0:T(8,128)(2,1)} custom-call(f32[108,13824]{1,0:T(8,128)} %h_ref.1), custom_call_target="tpu_custom_call" | custom-call | flops 29859840 | bytes 14929920 | tf_op jit(solution)/shard_map/prepare/pallas_call | solution.py:98
  25.3 0.2 fusion.tile_ref
  25.5 3.3 %all-to-all-done.own_ref = f32[64,32,108]{2,1,0:T(8,128)S(1)} async-done(((f32[64,32,108]{2,1,0:T(8,128)}), f32[64,32,108]{2,1,0:T(8,128)S(1)}, u32[]{:S(2)}, u32[]{:S(2)}) %all-to-all-start) | async-done | bytes 884768 | tf_op jit(solution)/shard_map/all_to_all | solution.py:350
  28.8 1.6 %collective-permute-start = (f32[64,32,108]{2,1,0:T(8,128)S(1)}, f32[64,32,108]{2,1,0:T(8,128)S(1)}, u32[]{:S(2)}, u32[]{:S(2)}) collective-permute-start(f32[64,32,108]{2,1,0:T(8,128)S(1)} %all-to-all-done.own_ref), channel_id=1, source_target_pairs={{0,1},{1,0},{2,3},{3,2},{4,5},{5,4},{6,7},{7,6},{8,9},{9,8},{10,11... | collective-permute-start | bytes 2654216 | tf_op jit(solution)/shard_map/ppermute | solution.py:354
  30.4 3.2 %image_own.1 = (f32[224,64]{1,0:T(8,128)S(1)}, bf16[224,8192]{1,0:T(8,128)(2,1)S(1)}) custom-call(bf16[2,224,8192]{2,1,0:T(8,128)(2,1)} %prepare.1.h_ref, f32[64,32,108]{2,1,0:T(8,128)S(1)} %all-to-all-done.own_ref), custom_call_target="tpu_custom_call" | custom-call | flops 1073741824 | bytes 4194304 | tf_op jit(solution)/shard_map/image_own/pallas_call | solution.py:336
  33.6 2.0 %image_other.1 = (f32[16,128]{1,0:T(8,128)S(1)}, f32[64,16,128]{2,1,0:T(8,128)}) custom-call(bf16[224,8192]{1,0:T(8,128)(2,1)S(1)} %get-tuple-element.33.h_ref, f32[64,32,108]{2,1,0:T(8,128)S(1)} %collective-permute-done.other_ref, f32[224,64]{1,0:T(8,128)S(1)} %get-tuple-element.34.product_ref, f32[16,128]{1,0:T(8,128)S(1)} %fusion.tile_ref), custom_call_target="tpu_custom_call" | custom-call | flops 1073741824 | bytes 4194304 | tf_op jit(solution)/shard_map/image_other/pallas_call | solution.py:336
  35.6 10.4 %all-to-all-start.1 = ((f32[64,16,128]{2,1,0:T(8,128)}), f32[64,16,128]{2,1,0:T(8,128)S(1)}, u32[]{:S(2)}, u32[]{:S(2)}) async-start(f32[64,16,128]{2,1,0:T(8,128)} %get-tuple-element.36), calls=%async_computation.1 | async-start | bytes 1048576 | tf_op jit(solution)/shard_map/all_to_all | solution.py:350
  46.0 0.0 copy-start.2
  46.0 0.0 copy-start.3
  46.0 7.0 %previous.1 = (f32[16,128]{1,0:T(8,128)S(1)}, bf16[2,32,8192]{2,1,0:T(8,128)(2,1)}, bf16[2,32,8192]{2,1,0:T(8,128)(2,1)}, f32[32,32]{1,0:T(8,128)S(1)}) custom-call(bf16[2,224,8192]{2,1,0:T(8,128)(2,1)} %prepare.1.h_ref, f32[64,32,108]{2,1,0:T(8,128)} %copy-done, f32[64,32,108]{2,1,0:T(8,128)} %copy-done.1, f32[224,64]{1,0:T(8,128)S(1)} %get-tuple-element.34.product_ref), custom_call_target="tpu_custom_call" | custom-call | flops 6442450944 | bytes 4194304 | tf_op jit(solution)/shard_map/previous/pallas_call | solution.py:336
  53.0 0.2 all-to-all-done.1.own_ref
  53.2 2.1 %collective-permute-start.1 = (f32[64,16,128]{2,1,0:T(8,128)S(1)}, f32[64,16,128]{2,1,0:T(8,128)S(1)}, u32[]{:S(2)}, u32[]{:S(2)}) collective-permute-start(f32[64,16,128]{2,1,0:T(8,128)S(1)} %all-to-all-done.1.own_ref), channel_id=1, source_target_pairs={{0,1},{1,0},{2,3},{3,2},{4,5},{5,4},{6,7},{7,6},{8,9},{9,8},{10,11... | collective-permute-start | bytes 1572872 | tf_op jit(solution)/shard_map/ppermute | solution.py:354
  55.3 1.3 %own.1 = (bf16[32,8192]{1,0:T(8,128)(2,1)S(1)}, f32[32,32]{1,0:T(8,128)S(1)}, f32[64,128]{1,0:T(8,128)S(1)}) custom-call(f32[64,16,128]{2,1,0:T(8,128)S(1)} %all-to-all-done.1.own_ref, bf16[2,32,8192]{2,1,0:T(8,128)(2,1)} %get-tuple-element.40.c_hbm), custom_call_target="tpu_custom_call" | custom-call | flops 1073741824 | bytes 4194304 | tf_op jit(solution)/shard_map/own/pallas_call | solution.py:336
  56.6 0.2 collective-permute-done.1.other_ref
  56.8 7.0 %search.1 = (f32[16,128]{1,0:T(8,128)S(1)}, f32[16]{0:T(128)}, f32[16,16]{1,0:T(8,128)S(1)}, f32[64,8,128]{2,1,0:T(8,128)}, bf16[4,32,8192]{2,1,0:T(8,128)(2,1)}) custom-call(bf16[2,224,8192]{2,1,0:T(8,128)(2,1)} %prepare.1.h_ref, f32[64,16,128]{2,1,0:T(8,128)S(1)} %all-to-all-done.1.own_ref, f32[64,16,128]{2,1,0:T(8,128)S(1)} %collective-permute-done.1.other_ref, ...), custom_call_target="tpu_custom_call" | custom-call | flops 6442450944 | bytes 4194304 | tf_op jit(solution)/shard_map/search/pallas_call | solution.py:336
  63.8 9.8 %all-to-all-start.2 = ((f32[64,8,128]{2,1,0:T(8,128)}), f32[64,8,128]{2,1,0:T(8,128)S(1)}, u32[]{:S(2)}, u32[]{:S(2)}) async-start(f32[64,8,128]{2,1,0:T(8,128)} %get-tuple-element.46), calls=%async_computation.2 | async-start | bytes 524288 | tf_op jit(solution)/shard_map/all_to_all | solution.py:350
  73.6 6.5 %factor.1 = (f32[48,48]{1,0:T(8,128)S(1)}, f32[48,48]{1,0:T(8,128)S(1)}) custom-call(bf16[4,32,8192]{2,1,0:T(8,128)(2,1)} %get-tuple-element.47.kept_hbm, bf16[2,32,8192]{2,1,0:T(8,128)(2,1)} %get-tuple-element.40.c_hbm, bf16[2,32,8192]{2,1,0:T(8,128)(2,1)} %get-tuple-element.48.p_hbm, f32[32,32]{1,0:T(8,128)S(1)} %get-tuple-element.49.first_ref, ...), custom_call_target="tpu_custom_call" | custom-call | flops 6442450944 | bytes 4194304 | tf_op jit(solution)/shard_map/factor/pallas_call | solution.py:336
  80.1 0.8 collective-permute-start.2
  80.9 1.2 %collective-permute-done.2.other_ref = f32[64,8,128]{2,1,0:T(8,128)S(1)} collective-permute-done((f32[64,8,128]{2,1,0:T(8,128)S(1)}, f32[64,8,128]{2,1,0:T(8,128)S(1)}, u32[]{:S(2)}, u32[]{:S(2)}) %collective-permute-start.2) | collective-permute-done | bytes 262176 | tf_op jit(solution)/shard_map/ppermute | solution.py:354
  82.0 3.2 %finish.1 = (f32[16,108]{1,0:T(8,128)}, f32[16,108]{1,0:T(8,128)}) custom-call(f32[48,48]{1,0:T(8,128)S(1)} %get-tuple-element.52.inverse_ref, f32[48,48]{1,0:T(8,128)S(1)} %get-tuple-element.53.stiff_ref, f32[64,8,128]{2,1,0:T(8,128)S(1)} %all-to-all-done.2.own_ref, f32[64,8,128]{2,1,0:T(8,128)S(1)} %collective-permute-done.2.other_ref, ...), custom_call_target="tpu_custom_call" | custom-call | flops 268435456 | bytes 4194304 | tf_op jit(solution)/shard_map/finish/pallas_call | solution.py:336
  (11 shorter events, 0.0 us)
Async XLA Ops:
  2.5 26.3 %all-to-all-start = ((f32[64,32,108]{2,1,0:T(8,128)}), f32[64,32,108]{2,1,0:T(8,128)S(1)}, u32[]{:S(2)}, u32[]{:S(2)}) async-start(f32[64,32,108]{2,1,0:T(8,128)} %broadcast_in_dim.14), calls=%async_computation | async-start | bytes 2097152 | tf_op jit(solution)/shard_map/all_to_all | solution.py:350
  28.8 6.8 %copy-start = (f32[64,32,108]{2,1,0:T(8,128)}, f32[64,32,108]{2,1,0:T(8,128)S(1)}, u32[]{:S(2)}) copy-start(f32[64,32,108]{2,1,0:T(8,128)S(1)} %all-to-all-done.own_ref) | copy-start | bytes 2654212
  28.8 4.7 %collective-permute-start = (f32[64,32,108]{2,1,0:T(8,128)S(1)}, f32[64,32,108]{2,1,0:T(8,128)S(1)}, u32[]{:S(2)}, u32[]{:S(2)}) collective-permute-start(f32[64,32,108]{2,1,0:T(8,128)S(1)} %all-to-all-done.own_ref), channel_id=1, source_target_pairs={{0,1},{1,0},{2,3},{3,2},{4,5},{5,4},{6,7},{7,6},{8,9},{9,8},{10,11... | collective-permute-start | bytes 2654216 | tf_op jit(solution)/shard_map/ppermute | solution.py:354
  33.6 12.5 %copy-start.1 = (f32[64,32,108]{2,1,0:T(8,128)}, f32[64,32,108]{2,1,0:T(8,128)S(1)}, u32[]{:S(2)}) copy-start(f32[64,32,108]{2,1,0:T(8,128)S(1)} %collective-permute-done.other_ref) | copy-start | bytes 2654212
  35.6 17.6 %all-to-all-start.1 = ((f32[64,16,128]{2,1,0:T(8,128)}), f32[64,16,128]{2,1,0:T(8,128)S(1)}, u32[]{:S(2)}, u32[]{:S(2)}) async-start(f32[64,16,128]{2,1,0:T(8,128)} %get-tuple-element.36), calls=%async_computation.1 | async-start | bytes 1048576 | tf_op jit(solution)/shard_map/all_to_all | solution.py:350
  46.0 9.2 %copy-start.2 = (f32[108,16]{0,1:T(8,128)S(1)}, f32[108,16]{0,1:T(8,128)}, u32[]{:S(2)}) copy-start(f32[108,16]{0,1:T(8,128)} %param.4) | copy-start | bytes 20740
  46.0 9.2 %copy-start.3 = (f32[108,16]{0,1:T(8,128)S(1)}, f32[108,16]{0,1:T(8,128)}, u32[]{:S(2)}) copy-start(f32[108,16]{0,1:T(8,128)} %param.5) | copy-start | bytes 20740
  53.2 3.6 %collective-permute-start.1 = (f32[64,16,128]{2,1,0:T(8,128)S(1)}, f32[64,16,128]{2,1,0:T(8,128)S(1)}, u32[]{:S(2)}, u32[]{:S(2)}) collective-permute-start(f32[64,16,128]{2,1,0:T(8,128)S(1)} %all-to-all-done.1.own_ref), channel_id=1, source_target_pairs={{0,1},{1,0},{2,3},{3,2},{4,5},{5,4},{6,7},{7,6},{8,9},{9,8},{10,11... | collective-permute-start | bytes 1572872 | tf_op jit(solution)/shard_map/ppermute | solution.py:354
  63.8 16.4 %all-to-all-start.2 = ((f32[64,8,128]{2,1,0:T(8,128)}), f32[64,8,128]{2,1,0:T(8,128)S(1)}, u32[]{:S(2)}, u32[]{:S(2)}) async-start(f32[64,8,128]{2,1,0:T(8,128)} %get-tuple-element.46), calls=%async_computation.2 | async-start | bytes 524288 | tf_op jit(solution)/shard_map/all_to_all | solution.py:350
  80.1 1.9 %collective-permute-start.2 = (f32[64,8,128]{2,1,0:T(8,128)S(1)}, f32[64,8,128]{2,1,0:T(8,128)S(1)}, u32[]{:S(2)}, u32[]{:S(2)}) collective-permute-start(f32[64,8,128]{2,1,0:T(8,128)S(1)} %all-to-all-done.2.own_ref), channel_id=1, source_target_pairs={{0,1},{1,0},{2,3},{3,2},{4,5},{5,4},{6,7},{7,6},{8,9},{9,8},{10,11... | collective-permute-start | bytes 786440 | tf_op jit(solution)/shard_map/ppermute | solution.py:354

commit v9 on v8

--- a/solution.py
+++ b/solution.py
@@ -19,9 +19,9 @@
 BACKWARD = FORWARD[::-1]
 ORDERS = (BACKWARD, BACKWARD, BACKWARD)
 SLOTS = [[order.index(chip) for chip in range(CHIPS)] for order in ORDERS]
-HALF = CHIPS * LANES
+HALF = CHIPS * ROWS
 TALL = 112
-CHUNKS = 4
+CHUNKS = 2
 CHUNK = HALF // CHUNKS
 EPS = 1e-06
 AXIS = "device"
@@ -32,8 +32,8 @@
 HBM = pl.BlockSpec(memory_space=pltpu.HBM)
 LIMIT = 53 << 20
 LIMIT_IMAGE = 48 << 20
-LIMIT_SEARCH = 52 << 20
-LIMIT_OWN = 52 << 20
+LIMIT_SEARCH = 54525952
+LIMIT_OWN = 54001664
 PARTS = 2
 STACK = PARTS * NEIG
 SPARE = ROWS
@@ -80,18 +80,14 @@
     return jnp.where(lane < ROWS, tile, 0.0)
 
 
-def padded(tile):
-    return jnp.concatenate([tile, jnp.zeros((tile.shape[0], LANES - ROWS), F32)], axis=1)
-
-
 def prepare_kernel(h_ref, parts_ref):
     core = lax.rem(lax.axis_index(AXIS), 2)
-    for block in range(2 * CHIPS // CHUNKS):
-        chip, owner = divmod(block, 2)
+    for owner in range(2):
         half = jnp.where(core == owner, 0, 1)
-        x = padded(h_ref[:, ROWS * block : ROWS * block + ROWS])
+        starts = [ROWS * (2 * chip + owner) for chip in range(CHIPS // CHUNKS)]
+        x = jnp.concatenate([h_ref[:, start : start + ROWS] for start in starts], axis=1)
         for number, part in enumerate(split(x)):
-            parts_ref[half, TALL * number : TALL * number + ROWS, LANES * chip : LANES * (chip + 1)] = part
+            parts_ref[half, TALL * number : TALL * number + ROWS, :] = part
 
 
 def prepare(hamiltonian):
@@ -113,18 +109,23 @@
     return copy
 
 
+def packed(tile_of):
+    return jnp.concatenate([tile_of(chip)[:, :ROWS] for chip in range(CHIPS)], axis=1)
+
+
+def store_parts(x, parts_ref):
+    for number, part in enumerate(split(x)):
+        parts_ref[NEIG * number : NEIG * (number + 1), :] = part
+
+
 def take_parts(tile_of, parts_ref):
-    for chip in range(CHIPS):
-        for number, part in enumerate(split(tile_of(chip))):
-            parts_ref[NEIG * number : NEIG * (number + 1), LANES * chip : LANES * (chip + 1)] = part
+    store_parts(packed(tile_of), parts_ref)
 
 
 def take_both(tile_of, first_ref, second_ref):
-    for chip in range(CHIPS):
-        lanes = slice(LANES * chip, LANES * (chip + 1))
-        for number, part in enumerate(split(tile_of(chip))):
-            first_ref[NEIG * number : NEIG * (number + 1), lanes] = part[:NEIG]
-            second_ref[NEIG * number : NEIG * (number + 1), lanes] = part[NEIG:]
+    x = packed(tile_of)
+    store_parts(x[:NEIG], first_ref)
+    store_parts(x[NEIG:], second_ref)
 
 
 def stacked_dot(left, right):
@@ -156,14 +157,14 @@
 def image_own_kernel(h_ref, own_ref, product_ref, next_ref, h_vmem, parts, sems):
     copy = started(h_ref.at[0], h_vmem, sems.at[0])
     following = started(h_ref.at[1], next_ref, sems.at[1])
-    take_both(lambda chip: padded(own_ref[SLOTS[0][chip]]), parts.at[pl.ds(0, STACK)], parts.at[pl.ds(STACK, STACK)])
+    take_both(lambda chip: own_ref[SLOTS[0][chip]], parts.at[pl.ds(0, STACK)], parts.at[pl.ds(STACK, STACK)])
     copy.wait()
     product_ref[...] = nt(h_vmem[...], parts[...])
     following.wait()
 
 
 def image_other_kernel(h_ref, other_ref, product_ref, tile_ref, image_ref, sent_ref, parts):
-    take_parts(lambda chip: padded(other_ref[SLOTS[0][chip], 0:NEIG]), parts)
+    take_parts(lambda chip: other_ref[SLOTS[0][chip], 0:NEIG], parts)
     image = fold_rows(product_ref[:, 0:STACK] + nt(h_ref[...], parts[...]))
     image_ref[...] = image
     sent = image + tile_ref[...]
@@ -173,10 +174,10 @@
 
 def previous_kernel(h_ref, own_ref, other_ref, product_ref, image_ref, c_out, p_out, inverse_ref, h_vmem, c_ref, p_ref, sems):
     copy = started(h_ref.at[1], h_vmem, sems.at[0])
-    take_both(lambda chip: padded(own_ref[SLOTS[0][chip]]), c_ref.at[0], p_ref.at[0])
-    take_both(lambda chip: padded(other_ref[SLOTS[0][chip]]), c_ref.at[1], p_ref.at[1])
-    out_c = started(c_ref, c_out, sems.at[1])
-    out_p = started(p_ref, p_out, sems.at[2])
+    take_both(lambda chip: own_ref[SLOTS[0][chip]], c_ref.at[0], p_ref.at[0])
+    take_both(lambda chip: other_ref[SLOTS[0][chip]], c_ref.at[1], p_ref.at[1])
+    out_c = started(c_ref, c_out.at[pl.ds(0, 2)], sems.at[1])
+    out_p = started(p_ref, p_out.at[pl.ds(0, 2)], sems.at[2])
     cc = fold(nt(c_ref[0], c_ref[0]) + nt(c_ref[1], c_ref[1]))
     pc = fold(nt(p_ref[0], c_ref[0]) + nt(p_ref[1], c_ref[1]))
     pp = fold(nt(p_ref[0], p_ref[0]) + nt(p_ref[1], p_ref[1]))
@@ -196,25 +197,27 @@
     return jnp.sum(jnp.where(lane % NEIG == row, spread, 0.0), axis=0, keepdims=True)
 
 
-def own_kernel(own_ref, c_hbm, i_ref, cross_ref, diag_ref, c_ref, sem):
+def own_kernel(own_ref, c_hbm, i_ref, x_ref, cross_ref, diag_ref, c_ref, sem):
     copy = started(c_hbm.at[0], c_ref, sem)
-    take_parts(lambda chip: real_lanes(own_ref[SLOTS[1][chip]]), i_ref)
-    for chip in range(CHIPS):
-        diag_ref[chip : chip + 1, :] = diagonal_of(own_ref[SLOTS[1][chip]])
+    x = packed(lambda chip: own_ref[SLOTS[1][chip]])
+    x_ref[...] = x
+    store_parts(x, i_ref)
+    diag_ref[...] = packed(lambda chip: diagonal_of(own_ref[SLOTS[1][chip]]))
     copy.wait()
     cross_ref[...] = nt(i_ref[...], c_ref[...])
 
 
 def search_kernel(
-    h_ref, own_ref, other_ref, c_hbm, i_own_ref, half_cross_ref, diag_ref, cvec_ref, pvec_ref, pimage_ref, image_ref, tile_ref,
+    h_ref, x_own_ref, other_ref, c_hbm, i_own_ref, half_cross_ref, diag_ref, cvec_ref, pvec_ref, pimage_ref, image_ref, tile_ref,
     search_ref, rms_ref, cross_ref, sent_ref, kept_ref,
     h_vmem, c_ref, i_ref, s_ref, resid_ref, other_diag_ref, sems, h_sems, c_sem,
 ):
-    copy_c = started(c_hbm, c_ref, c_sem)
+    copy_c = started(c_hbm.at[pl.ds(0, 2)], c_ref, c_sem)
     copies = [started(h_ref.at[half], h_vmem.at[half], h_sems.at[half]) for half in range(2)]
-    take_parts(lambda chip: real_lanes(other_ref[SLOTS[1][chip]]), i_ref)
-    for chip in range(CHIPS):
-        other_diag_ref[chip : chip + 1, :] = diagonal_of(other_ref[SLOTS[1][chip]])
+    x_other = packed(lambda chip: other_ref[SLOTS[1][chip]])
+    resid_ref[1] = x_other
+    store_parts(x_other, i_ref)
+    other_diag_ref[...] = packed(lambda chip: diagonal_of(other_ref[SLOTS[1][chip]]))
     copy_c.wait()
     kept = [started(i_own_ref, kept_ref.at[2], sems.at[1]), started(i_ref, kept_ref.at[3], sems.at[2])]
     cross_t = fold(half_cross_ref[...] + nt(i_ref[...], c_ref[1]))
@@ -222,24 +225,18 @@
     ritz_t = cross_t / ORDER
     stacked = jnp.concatenate(split3(ritz_t), axis=0)
     stacked = jnp.concatenate([stacked] * PARTS, axis=1)
-    square = jnp.zeros((NEIG, LANES), F32)
-    for half, ref in ((0, own_ref), (1, other_ref)):
+    square = jnp.zeros((NEIG, 1), F32)
+    for half, ref in ((0, x_own_ref), (1, resid_ref.at[1])):
         moved = jnp.dot(stacked, c_ref[half], preferred_element_type=F32)
         moved = (moved[32:48] + moved[16:32]) + moved[0:16]
-        part = jnp.zeros((NEIG, LANES), F32)
-        for chip in range(CHIPS):
-            lanes = slice(LANES * chip, LANES * (chip + 1))
-            resid = real_lanes(ref[SLOTS[1][chip]]) - moved[:, lanes]
-            resid_ref[half, :, lanes] = resid
-            part = part + resid * resid
-        square = square + part
-    rms = jnp.sqrt(jnp.sum(square, axis=1, keepdims=True) / ORDER + EPS)
+        resid = ref[...] - moved
+        resid_ref[half] = resid
+        square = square + jnp.sum(resid * resid, axis=1, keepdims=True)
+    rms = jnp.sqrt(square / ORDER + EPS)
     row = lax.broadcasted_iota(jnp.int32, (NEIG, NEIG), 0)
     column = lax.broadcasted_iota(jnp.int32, (NEIG, NEIG), 1)
     rms_ref[...] = jnp.sum(jnp.where(row == column, rms, 0.0), axis=0)
     value = jnp.sum(jnp.where(row == column, ritz_t, 0.0), axis=1, keepdims=True)
-    value = jnp.broadcast_to(value, (NEIG, LANES))
-    rms = jnp.broadcast_to(rms, (NEIG, LANES))
 
     def scaled(resid, diag):
         return resid / (jnp.maximum(jnp.abs(diag - value), 1.0) * rms)
@@ -248,10 +245,7 @@
     search = scaled(resid, diagonal_of(tile_ref[...]))
     search_ref[...] = search
     for half, diag in ((0, diag_ref), (1, other_diag_ref)):
-        take_parts(
-            lambda chip: scaled(resid_ref[half, :, LANES * chip : LANES * (chip + 1)], diag[chip : chip + 1, :]),
-            s_ref.at[half],
-        )
+        store_parts(scaled(resid_ref[half], diag[...]), s_ref.at[half])
     kept.append(started(s_ref, kept_ref.at[pl.ds(0, 2)], sems.at[0]))
     copies[0].wait()
     product = nt(h_vmem[0], s_ref[0])
@@ -262,9 +256,9 @@
         [nt_exact(simage, search), nt_exact(simage, pvec), nt_exact(pimage_ref[...], pvec), jnp.zeros((NEIG, NEIG), F32)],
         axis=1,
     )
-    packed = jnp.concatenate([terms[0:8], terms[8:16]], axis=1)
+    message = jnp.concatenate([terms[0:8], terms[8:16]], axis=1)
     for chip in range(CHIPS):
-        sent_ref[chip] = packed
+        sent_ref[chip] = message
     for copy in kept:
         copy.wait()
 
@@ -393,7 +387,7 @@
     i_own = to_chips(sent, 1)
     p_image, c_parts, p_parts, first = kernel_call(
         previous_kernel,
-        [block, parts, parts, ((2 * NEIG, 2 * NEIG), F32)],
+        [block, ((3, STACK, HALF), BF16), ((3, STACK, HALF), BF16), ((2 * NEIG, 2 * NEIG), F32)],
         (h_parts, v_own, v_other, product),
         6 << 30,
         "previous",
@@ -401,9 +395,9 @@
     )
     i_own, p_image, c_parts = lax.optimization_barrier((i_own, p_image, c_parts))
     i_other = to_core(i_own)
-    i_own_parts, half_cross, diag = kernel_call(
+    i_own_parts, x_own, half_cross, diag = kernel_call(
         own_kernel,
-        [half, ((STACK, STACK), F32), ((CHIPS, LANES), F32)],
+        [half, ((NEIG, HALF), F32), ((STACK, STACK), F32), ((1, HALF), F32)],
         (i_own, c_parts),
         1 << 30,
         "own",
@@ -412,10 +406,10 @@
     search, rms, cross, sent, kept = kernel_call(
         search_kernel,
         [block, ((NEIG,), F32), ((NEIG, NEIG), F32), ((CHIPS, 8, LANES), F32), ((4, STACK, HALF), BF16)],
-        (h_parts, i_own, i_other, c_parts, i_own_parts, half_cross, diag, cvec, pvec, p_image, image, tile),
+        (h_parts, x_own, i_other, c_parts, i_own_parts, half_cross, diag, cvec, pvec, p_image, image, tile),
         6 << 30,
         "search",
-        [h_vmem, parts_vmem, half_vmem, parts_vmem, pltpu.VMEM((2, NEIG, HALF), F32), pltpu.VMEM((CHIPS, LANES), F32), dma((3,)), dma((2,)), dma(())],
+        [h_vmem, parts_vmem, half_vmem, parts_vmem, pltpu.VMEM((2, NEIG, HALF), F32), pltpu.VMEM((1, HALF), F32), dma((3,)), dma((2,)), dma(())],
         (0, 3), (4,), limit=LIMIT_SEARCH,
     )
     r_own = to_chips(sent, 2)

time: 85.8 us -> 84.6 us (0.986)
  Pallas kernels: 38.2 us -> 36.9 us
    pallas_call x1, Pallas kernels: 8.03 us -> 7.08 us  [prepare(): pl.pallas_call(prepare_kernel, grid=(CHUNKS,), out_shape=jax.ShapeDtypeSt...]
  transfers between devices with their start and end apart: 6 -> 6, of which waited for: 4 -> 2; matrix products, arithmetic and copies ran while one was open for 1% -> 1% of each run, Pallas kernels for 31% -> 30%
where the time goes in v9:
time: 84.6 us; the launch traced here: 84.1 us
  starting transfers between devices  37.9 us (45%)
  Pallas kernels  36.9 us (44%)
  waiting for transfers between devices  5.43 us (6%)
  other arithmetic  1.73 us (2%)
  local copies, waits for them, and re-layouts  1.14 us (1%)
    all_to_all x3, starting transfers between devices, to_chips(): return lax.all_to_all(x, AXIS, 0, 0, axis_index_groups=groups, tiled=True)  34.2 us
    pallas_call x7, Pallas kernels, kernel_call(): pl.pallas_call(body, out_shape=[jax.ShapeDtypeStruct(shape, kind) for sha...  29.8 us
    pallas_call x1, Pallas kernels, prepare(): pl.pallas_call(prepare_kernel, grid=(CHUNKS,), out_shape=jax.ShapeDtypeSt...  7.08 us
    all_to_all x3, waiting for transfers between devices, to_chips(): return lax.all_to_all(x, AXIS, 0, 0, axis_index_groups=groups, tiled=True)  4.26 us
    ppermute x3, starting transfers between devices, to_core(): lax.ppermute(x, AXIS, [(device, device ^ 1) for device in range(DEVICES)])  3.68 us
  transfers between devices with their start and end apart: 6, of which 2 were waited for; matrix products, arithmetic and copies ran while one was open for 1% of the time, Pallas kernels for 30%

profile of v9, /device:TPU:1, one launch (start us, length us, event | category | flops | bytes accessed | tf_op | source)
XLA Modules:
  0.0 84.1 jit_solution(5426431342918116479)
XLA Ops:
  0.6 0.7 pad_maximum_fusion
  1.4 1.1 %broadcast_in_dim.14 = f32[64,32,108]{2,1,0:T(8,128)} broadcast(f32[32,108]{1,0:T(8,128)S(1)} %pad_maximum_fusion), dimensions={1,2} | broadcast | bytes 898560 | tf_op jit(solution)/shard_map/broadcast_in_dim | solution.py:363
  2.5 13.7 %all-to-all-start = ((f32[64,32,108]{2,1,0:T(8,128)}), f32[64,32,108]{2,1,0:T(8,128)S(1)}, u32[]{:S(2)}, u32[]{:S(2)}) async-start(f32[64,32,108]{2,1,0:T(8,128)} %broadcast_in_dim.14), calls=%async_computation | async-start | bytes 2097152 | tf_op jit(solution)/shard_map/all_to_all | solution.py:344
  16.2 1.0 %select_reduce_fusion = f32[108]{0:T(128)S(1)} fusion(f32[108,13824]{1,0:T(8,128)} %h_ref.1, s32[]{:T(128)S(6)} %select_n.34), kind=kLoop, calls=%fused_computation.1 | loop fusion | flops 34884 | bytes 47092 | tf_op jit(solution)/shard_map/reduce_sum | solution.py:355
  17.2 7.1 %prepare.1.h_ref = bf16[2,224,6912]{2,1,0:T(8,128)(2,1)} custom-call(f32[108,13824]{1,0:T(8,128)} %h_ref.1), custom_call_target="tpu_custom_call" | custom-call | flops 29859840 | bytes 14929920 | tf_op jit(solution)/shard_map/prepare/pallas_call | solution.py:94
  24.3 0.2 fusion.tile_ref
  24.5 4.3 %all-to-all-done.own_ref = f32[64,32,108]{2,1,0:T(8,128)S(1)} async-done(((f32[64,32,108]{2,1,0:T(8,128)}), f32[64,32,108]{2,1,0:T(8,128)S(1)}, u32[]{:S(2)}, u32[]{:S(2)}) %all-to-all-start) | async-done | bytes 884768 | tf_op jit(solution)/shard_map/all_to_all | solution.py:344
  28.8 1.6 %collective-permute-start = (f32[64,32,108]{2,1,0:T(8,128)S(1)}, f32[64,32,108]{2,1,0:T(8,128)S(1)}, u32[]{:S(2)}, u32[]{:S(2)}) collective-permute-start(f32[64,32,108]{2,1,0:T(8,128)S(1)} %all-to-all-done.own_ref), channel_id=1, source_target_pairs={{0,1},{1,0},{2,3},{3,2},{4,5},{5,4},{6,7},{7,6},{8,9},{9,8},{10,11... | collective-permute-start | bytes 2654216 | tf_op jit(solution)/shard_map/ppermute | solution.py:348
  30.3 3.1 %image_own.1 = (f32[224,64]{1,0:T(8,128)S(1)}, bf16[224,6912]{1,0:T(8,128)(2,1)S(1)}) custom-call(bf16[2,224,6912]{2,1,0:T(8,128)(2,1)} %prepare.1.h_ref, f32[64,32,108]{2,1,0:T(8,128)S(1)} %all-to-all-done.own_ref), custom_call_target="tpu_custom_call" | custom-call | flops 1073741824 | bytes 4194304 | tf_op jit(solution)/shard_map/image_own/pallas_call | solution.py:330
  33.4 0.0 collective-permute-done.other_ref
  33.4 1.9 %image_other.1 = (f32[16,128]{1,0:T(8,128)S(1)}, f32[64,16,128]{2,1,0:T(8,128)}) custom-call(bf16[224,6912]{1,0:T(8,128)(2,1)S(1)} %get-tuple-element.34.h_ref, f32[64,32,108]{2,1,0:T(8,128)S(1)} %collective-permute-done.other_ref, f32[224,64]{1,0:T(8,128)S(1)} %get-tuple-element.35.product_ref, f32[16,128]{1,0:T(8,128)S(1)} %fusion.tile_ref), custom_call_target="tpu_custom_call" | custom-call | flops 1073741824 | bytes 4194304 | tf_op jit(solution)/shard_map/image_other/pallas_call | solution.py:330
  35.3 10.5 %all-to-all-start.1 = ((f32[64,16,128]{2,1,0:T(8,128)}), f32[64,16,128]{2,1,0:T(8,128)S(1)}, u32[]{:S(2)}, u32[]{:S(2)}) async-start(f32[64,16,128]{2,1,0:T(8,128)} %get-tuple-element.37), calls=%async_computation.1 | async-start | bytes 1048576 | tf_op jit(solution)/shard_map/all_to_all | solution.py:344
  45.8 0.0 copy-start.2
  45.8 0.0 copy-start.3
  45.8 7.5 %previous.1 = (f32[16,128]{1,0:T(8,128)S(1)}, bf16[3,32,6912]{2,1,0:T(8,128)(2,1)}, bf16[3,32,6912]{2,1,0:T(8,128)(2,1)}, f32[32,32]{1,0:T(8,128)S(1)}) custom-call(bf16[2,224,6912]{2,1,0:T(8,128)(2,1)} %prepare.1.h_ref, f32[64,32,108]{2,1,0:T(8,128)} %copy-done, f32[64,32,108]{2,1,0:T(8,128)} %copy-done.1, f32[224,64]{1,0:T(8,128)S(1)} %get-tuple-element.35.product_ref), custom_call_target="tpu_custom_call" | custom-call | flops 6442450944 | bytes 4194304 | tf_op jit(solution)/shard_map/previous/pallas_call | solution.py:330
  53.3 1.5 %collective-permute-start.1 = (f32[64,16,128]{2,1,0:T(8,128)S(1)}, f32[64,16,128]{2,1,0:T(8,128)S(1)}, u32[]{:S(2)}, u32[]{:S(2)}) collective-permute-start(f32[64,16,128]{2,1,0:T(8,128)S(1)} %all-to-all-done.1.own_ref), channel_id=1, source_target_pairs={{0,1},{1,0},{2,3},{3,2},{4,5},{5,4},{6,7},{7,6},{8,9},{9,8},{10,11... | collective-permute-start | bytes 1572872 | tf_op jit(solution)/shard_map/ppermute | solution.py:348
  54.9 1.6 %own.1 = (bf16[32,6912]{1,0:T(8,128)(2,1)S(1)}, f32[16,6912]{1,0:T(8,128)S(1)}, f32[32,32]{1,0:T(8,128)S(1)}, f32[1,6912]{1,0:T(1,128)S(1)}) custom-call(f32[64,16,128]{2,1,0:T(8,128)S(1)} %all-to-all-done.1.own_ref, bf16[3,32,6912]{2,1,0:T(8,128)(2,1)} %get-tuple-element.41.c_hbm), custom_call_target="tpu_custom_call" | custom-call | flops 1073741824 | bytes 4194304 | tf_op jit(solution)/shard_map/own/pallas_call | solution.py:330
  56.5 0.0 collective-permute-done.1.other_ref
  56.5 6.5 %search.1 = (f32[16,128]{1,0:T(8,128)S(1)}, f32[16]{0:T(128)}, f32[16,16]{1,0:T(8,128)S(1)}, f32[64,8,128]{2,1,0:T(8,128)}, bf16[4,32,6912]{2,1,0:T(8,128)(2,1)}) custom-call(bf16[2,224,6912]{2,1,0:T(8,128)(2,1)} %prepare.1.h_ref, f32[16,6912]{1,0:T(8,128)S(1)} %get-tuple-element.42.x_own_ref, f32[64,16,128]{2,1,0:T(8,128)S(1)} %collective-permute-done.1.other_ref, ...), custom_call_target="tpu_custom_call" | custom-call | flops 6442450944 | bytes 4194304 | tf_op jit(solution)/shard_map/search/pallas_call | solution.py:330
  63.0 10.0 %all-to-all-start.2 = ((f32[64,8,128]{2,1,0:T(8,128)}), f32[64,8,128]{2,1,0:T(8,128)S(1)}, u32[]{:S(2)}, u32[]{:S(2)}) async-start(f32[64,8,128]{2,1,0:T(8,128)} %get-tuple-element.48), calls=%async_computation.2 | async-start | bytes 524288 | tf_op jit(solution)/shard_map/all_to_all | solution.py:344
  73.0 6.1 %factor.1 = (f32[48,48]{1,0:T(8,128)S(1)}, f32[48,48]{1,0:T(8,128)S(1)}) custom-call(bf16[4,32,6912]{2,1,0:T(8,128)(2,1)} %get-tuple-element.49.kept_hbm, bf16[3,32,6912]{2,1,0:T(8,128)(2,1)} %get-tuple-element.41.c_hbm, bf16[3,32,6912]{2,1,0:T(8,128)(2,1)} %get-tuple-element.50.p_hbm, f32[32,32]{1,0:T(8,128)S(1)} %get-tuple-element.51.first_ref, ...), custom_call_target="tpu_custom_call" | custom-call | flops 6442450944 | bytes 4194304 | tf_op jit(solution)/shard_map/factor/pallas_call | solution.py:330
  79.1 0.6 collective-permute-start.2
  79.7 1.2 %collective-permute-done.2.other_ref = f32[64,8,128]{2,1,0:T(8,128)S(1)} collective-permute-done((f32[64,8,128]{2,1,0:T(8,128)S(1)}, f32[64,8,128]{2,1,0:T(8,128)S(1)}, u32[]{:S(2)}, u32[]{:S(2)}) %collective-permute-start.2) | collective-permute-done | bytes 262176 | tf_op jit(solution)/shard_map/ppermute | solution.py:348
  80.9 3.2 %finish.1 = (f32[16,108]{1,0:T(8,128)}, f32[16,108]{1,0:T(8,128)}) custom-call(f32[48,48]{1,0:T(8,128)S(1)} %get-tuple-element.54.inverse_ref, f32[48,48]{1,0:T(8,128)S(1)} %get-tuple-element.55.stiff_ref, f32[64,8,128]{2,1,0:T(8,128)S(1)} %all-to-all-done.2.own_ref, f32[64,8,128]{2,1,0:T(8,128)S(1)} %collective-permute-done.2.other_ref, ...), custom_call_target="tpu_custom_call" | custom-call | flops 268435456 | bytes 4194304 | tf_op jit(solution)/shard_map/finish/pallas_call | solution.py:330
  (11 shorter events, 0.0 us)
Async XLA Ops:
  2.5 26.3 %all-to-all-start = ((f32[64,32,108]{2,1,0:T(8,128)}), f32[64,32,108]{2,1,0:T(8,128)S(1)}, u32[]{:S(2)}, u32[]{:S(2)}) async-start(f32[64,32,108]{2,1,0:T(8,128)} %broadcast_in_dim.14), calls=%async_computation | async-start | bytes 2097152 | tf_op jit(solution)/shard_map/all_to_all | solution.py:344
  28.8 4.7 %copy-start = (f32[64,32,108]{2,1,0:T(8,128)}, f32[64,32,108]{2,1,0:T(8,128)S(1)}, u32[]{:S(2)}) copy-start(f32[64,32,108]{2,1,0:T(8,128)S(1)} %all-to-all-done.own_ref) | copy-start | bytes 2654212
  28.8 4.7 %collective-permute-start = (f32[64,32,108]{2,1,0:T(8,128)S(1)}, f32[64,32,108]{2,1,0:T(8,128)S(1)}, u32[]{:S(2)}, u32[]{:S(2)}) collective-permute-start(f32[64,32,108]{2,1,0:T(8,128)S(1)} %all-to-all-done.own_ref), channel_id=1, source_target_pairs={{0,1},{1,0},{2,3},{3,2},{4,5},{5,4},{6,7},{7,6},{8,9},{9,8},{10,11... | collective-permute-start | bytes 2654216 | tf_op jit(solution)/shard_map/ppermute | solution.py:348
  33.4 12.4 %copy-start.1 = (f32[64,32,108]{2,1,0:T(8,128)}, f32[64,32,108]{2,1,0:T(8,128)S(1)}, u32[]{:S(2)}) copy-start(f32[64,32,108]{2,1,0:T(8,128)S(1)} %collective-permute-done.other_ref) | copy-start | bytes 2654212
  35.3 18.0 %all-to-all-start.1 = ((f32[64,16,128]{2,1,0:T(8,128)}), f32[64,16,128]{2,1,0:T(8,128)S(1)}, u32[]{:S(2)}, u32[]{:S(2)}) async-start(f32[64,16,128]{2,1,0:T(8,128)} %get-tuple-element.37), calls=%async_computation.1 | async-start | bytes 1048576 | tf_op jit(solution)/shard_map/all_to_all | solution.py:344
  45.8 9.0 %copy-start.2 = (f32[108,16]{0,1:T(8,128)S(1)}, f32[108,16]{0,1:T(8,128)}, u32[]{:S(2)}) copy-start(f32[108,16]{0,1:T(8,128)} %param.4) | copy-start | bytes 20740
  45.8 9.0 %copy-start.3 = (f32[108,16]{0,1:T(8,128)S(1)}, f32[108,16]{0,1:T(8,128)}, u32[]{:S(2)}) copy-start(f32[108,16]{0,1:T(8,128)} %param.5) | copy-start | bytes 20740
  53.3 3.2 %collective-permute-start.1 = (f32[64,16,128]{2,1,0:T(8,128)S(1)}, f32[64,16,128]{2,1,0:T(8,128)S(1)}, u32[]{:S(2)}, u32[]{:S(2)}) collective-permute-start(f32[64,16,128]{2,1,0:T(8,128)S(1)} %all-to-all-done.1.own_ref), channel_id=1, source_target_pairs={{0,1},{1,0},{2,3},{3,2},{4,5},{5,4},{6,7},{7,6},{8,9},{9,8},{10,11... | collective-permute-start | bytes 1572872 | tf_op jit(solution)/shard_map/ppermute | solution.py:348
  63.0 16.1 %all-to-all-start.2 = ((f32[64,8,128]{2,1,0:T(8,128)}), f32[64,8,128]{2,1,0:T(8,128)S(1)}, u32[]{:S(2)}, u32[]{:S(2)}) async-start(f32[64,8,128]{2,1,0:T(8,128)} %get-tuple-element.48), calls=%async_computation.2 | async-start | bytes 524288 | tf_op jit(solution)/shard_map/all_to_all | solution.py:344
  79.1 1.8 %collective-permute-start.2 = (f32[64,8,128]{2,1,0:T(8,128)S(1)}, f32[64,8,128]{2,1,0:T(8,128)S(1)}, u32[]{:S(2)}, u32[]{:S(2)}) collective-permute-start(f32[64,8,128]{2,1,0:T(8,128)S(1)} %all-to-all-done.2.own_ref), channel_id=1, source_target_pairs={{0,1},{1,0},{2,3},{3,2},{4,5},{5,4},{6,7},{7,6},{8,9},{9,8},{10,11... | collective-permute-start | bytes 786440 | tf_op jit(solution)/shard_map/ppermute | solution.py:348

commit v10 on v9

--- a/solution.py
+++ b/solution.py
@@ -253,7 +253,11 @@
     simage = fold_rows(product + nt(h_vmem[1], s_ref[1]))
     pvec = pvec_ref[...]
     terms = jnp.concatenate(
-        [nt_exact(simage, search), nt_exact(simage, pvec), nt_exact(pimage_ref[...], pvec), jnp.zeros((NEIG, NEIG), F32)],
+        [
+            nt_exact(simage, jnp.concatenate([search, pvec], axis=0)),
+            nt_exact(pimage_ref[...], pvec),
+            jnp.zeros((NEIG, NEIG), F32),
+        ],
         axis=1,
     )
     message = jnp.concatenate([terms[0:8], terms[8:16]], axis=1)
@@ -268,14 +272,13 @@
     for half in range(2):
         for number, source in enumerate((kept_hbm.at[half], kept_hbm.at[2 + half], c_hbm.at[half], p_hbm.at[half])):
             copies.append(started(source, all_ref.at[half, pl.ds(STACK * number, STACK)], sems.at[half, number]))
-    with_search, p_image = None, None
+    products = None
     for half in range(2):
         for copy in copies[4 * half : 4 * half + 4]:
             copy.wait()
-        terms = nt(all_ref[half], all_ref[half, :STACK])
-        with_search = terms if half == 0 else with_search + terms
-        terms = nt(all_ref[half, 3 * STACK :], all_ref[half, STACK : 2 * STACK])
-        p_image = terms if half == 0 else p_image + terms
+        terms = nt(all_ref[half], all_ref[half, : 2 * STACK])
+        products = terms if half == 0 else products + terms
+    with_search, p_image = products[:, :STACK], products[3 * STACK :, STACK:]
     ss, i_s, cs, ps = [fold(with_search[STACK * n : STACK * (n + 1)]) for n in range(4)]
     first = first_ref[...]
     row = nt_exact(jnp.concatenate([cs.T, ps.T], axis=1), first)

time: 84.6 us -> 84.5 us (level)
  no operation moved by 1% of the time
where the time goes in v10:
time: 84.5 us; the launch traced here: 84 us
  starting transfers between devices  38.2 us (45%)
  Pallas kernels  36.5 us (43%)
  waiting for transfers between devices  5.43 us (6%)
  other arithmetic  1.73 us (2%)
  local copies, waits for them, and re-layouts  1.14 us (1%)
    all_to_all x3, starting transfers between devices, to_chips(): return lax.all_to_all(x, AXIS, 0, 0, axis_index_groups=groups, tiled=True)  34.2 us
    pallas_call x7, Pallas kernels, kernel_call(): pl.pallas_call(body, out_shape=[jax.ShapeDtypeStruct(shape, kind) for sha...  29.5 us
    pallas_call x1, Pallas kernels, prepare(): pl.pallas_call(prepare_kernel, grid=(CHUNKS,), out_shape=jax.ShapeDtypeSt...  7.08 us
    all_to_all x3, waiting for transfers between devices, to_chips(): return lax.all_to_all(x, AXIS, 0, 0, axis_index_groups=groups, tiled=True)  4.26 us
    ppermute x3, starting transfers between devices, to_core(): lax.ppermute(x, AXIS, [(device, device ^ 1) for device in range(DEVICES)])  3.96 us
  transfers between devices with their start and end apart: 6, of which 2 were waited for; matrix products, arithmetic and copies ran while one was open for 1% of the time, Pallas kernels for 30%

profile of v10, /device:TPU:1, one launch (start us, length us, event | category | flops | bytes accessed | tf_op | source)
XLA Modules:
  0.0 84.0 jit_solution(2719663426250571529)
XLA Ops:
  0.6 0.7 pad_maximum_fusion
  1.4 1.1 %broadcast_in_dim.14 = f32[64,32,108]{2,1,0:T(8,128)} broadcast(f32[32,108]{1,0:T(8,128)S(1)} %pad_maximum_fusion), dimensions={1,2} | broadcast | bytes 898560 | tf_op jit(solution)/shard_map/broadcast_in_dim | solution.py:366
  2.5 13.7 %all-to-all-start = ((f32[64,32,108]{2,1,0:T(8,128)}), f32[64,32,108]{2,1,0:T(8,128)S(1)}, u32[]{:S(2)}, u32[]{:S(2)}) async-start(f32[64,32,108]{2,1,0:T(8,128)} %broadcast_in_dim.14), calls=%async_computation | async-start | bytes 2097152 | tf_op jit(solution)/shard_map/all_to_all | solution.py:347
  16.2 1.0 %select_reduce_fusion = f32[108]{0:T(128)S(1)} fusion(f32[108,13824]{1,0:T(8,128)} %h_ref.1, s32[]{:T(128)S(6)} %select_n.34), kind=kLoop, calls=%fused_computation.1 | loop fusion | flops 34884 | bytes 47092 | tf_op jit(solution)/shard_map/reduce_sum | solution.py:358
  17.2 7.1 %prepare.1.h_ref = bf16[2,224,6912]{2,1,0:T(8,128)(2,1)} custom-call(f32[108,13824]{1,0:T(8,128)} %h_ref.1), custom_call_target="tpu_custom_call" | custom-call | flops 29859840 | bytes 14929920 | tf_op jit(solution)/shard_map/prepare/pallas_call | solution.py:94
  24.3 0.2 fusion.tile_ref
  24.5 4.3 %all-to-all-done.own_ref = f32[64,32,108]{2,1,0:T(8,128)S(1)} async-done(((f32[64,32,108]{2,1,0:T(8,128)}), f32[64,32,108]{2,1,0:T(8,128)S(1)}, u32[]{:S(2)}, u32[]{:S(2)}) %all-to-all-start) | async-done | bytes 884768 | tf_op jit(solution)/shard_map/all_to_all | solution.py:347
  28.8 1.6 %collective-permute-start = (f32[64,32,108]{2,1,0:T(8,128)S(1)}, f32[64,32,108]{2,1,0:T(8,128)S(1)}, u32[]{:S(2)}, u32[]{:S(2)}) collective-permute-start(f32[64,32,108]{2,1,0:T(8,128)S(1)} %all-to-all-done.own_ref), channel_id=1, source_target_pairs={{0,1},{1,0},{2,3},{3,2},{4,5},{5,4},{6,7},{7,6},{8,9},{9,8},{10,11... | collective-permute-start | bytes 2654216 | tf_op jit(solution)/shard_map/ppermute | solution.py:351
  30.3 3.1 %image_own.1 = (f32[224,64]{1,0:T(8,128)S(1)}, bf16[224,6912]{1,0:T(8,128)(2,1)S(1)}) custom-call(bf16[2,224,6912]{2,1,0:T(8,128)(2,1)} %prepare.1.h_ref, f32[64,32,108]{2,1,0:T(8,128)S(1)} %all-to-all-done.own_ref), custom_call_target="tpu_custom_call" | custom-call | flops 1073741824 | bytes 4194304 | tf_op jit(solution)/shard_map/image_own/pallas_call | solution.py:333
  33.4 0.0 collective-permute-done.other_ref
  33.4 1.9 %image_other.1 = (f32[16,128]{1,0:T(8,128)S(1)}, f32[64,16,128]{2,1,0:T(8,128)}) custom-call(bf16[224,6912]{1,0:T(8,128)(2,1)S(1)} %get-tuple-element.34.h_ref, f32[64,32,108]{2,1,0:T(8,128)S(1)} %collective-permute-done.other_ref, f32[224,64]{1,0:T(8,128)S(1)} %get-tuple-element.35.product_ref, f32[16,128]{1,0:T(8,128)S(1)} %fusion.tile_ref), custom_call_target="tpu_custom_call" | custom-call | flops 1073741824 | bytes 4194304 | tf_op jit(solution)/shard_map/image_other/pallas_call | solution.py:333
  35.3 10.5 %all-to-all-start.1 = ((f32[64,16,128]{2,1,0:T(8,128)}), f32[64,16,128]{2,1,0:T(8,128)S(1)}, u32[]{:S(2)}, u32[]{:S(2)}) async-start(f32[64,16,128]{2,1,0:T(8,128)} %get-tuple-element.37), calls=%async_computation.1 | async-start | bytes 1048576 | tf_op jit(solution)/shard_map/all_to_all | solution.py:347
  45.8 0.0 copy-start.2
  45.8 0.0 copy-start.3
  45.8 7.5 %previous.1 = (f32[16,128]{1,0:T(8,128)S(1)}, bf16[3,32,6912]{2,1,0:T(8,128)(2,1)}, bf16[3,32,6912]{2,1,0:T(8,128)(2,1)}, f32[32,32]{1,0:T(8,128)S(1)}) custom-call(bf16[2,224,6912]{2,1,0:T(8,128)(2,1)} %prepare.1.h_ref, f32[64,32,108]{2,1,0:T(8,128)} %copy-done, f32[64,32,108]{2,1,0:T(8,128)} %copy-done.1, f32[224,64]{1,0:T(8,128)S(1)} %get-tuple-element.35.product_ref), custom_call_target="tpu_custom_call" | custom-call | flops 6442450944 | bytes 4194304 | tf_op jit(solution)/shard_map/previous/pallas_call | solution.py:333
  53.3 1.5 %collective-permute-start.1 = (f32[64,16,128]{2,1,0:T(8,128)S(1)}, f32[64,16,128]{2,1,0:T(8,128)S(1)}, u32[]{:S(2)}, u32[]{:S(2)}) collective-permute-start(f32[64,16,128]{2,1,0:T(8,128)S(1)} %all-to-all-done.1.own_ref), channel_id=1, source_target_pairs={{0,1},{1,0},{2,3},{3,2},{4,5},{5,4},{6,7},{7,6},{8,9},{9,8},{10,11... | collective-permute-start | bytes 1572872 | tf_op jit(solution)/shard_map/ppermute | solution.py:351
  54.9 1.6 %own.1 = (bf16[32,6912]{1,0:T(8,128)(2,1)S(1)}, f32[16,6912]{1,0:T(8,128)S(1)}, f32[32,32]{1,0:T(8,128)S(1)}, f32[1,6912]{1,0:T(1,128)S(1)}) custom-call(f32[64,16,128]{2,1,0:T(8,128)S(1)} %all-to-all-done.1.own_ref, bf16[3,32,6912]{2,1,0:T(8,128)(2,1)} %get-tuple-element.41.c_hbm), custom_call_target="tpu_custom_call" | custom-call | flops 1073741824 | bytes 4194304 | tf_op jit(solution)/shard_map/own/pallas_call | solution.py:333
  56.5 0.0 collective-permute-done.1.other_ref
  56.5 6.5 %search.1 = (f32[16,128]{1,0:T(8,128)S(1)}, f32[16]{0:T(128)}, f32[16,16]{1,0:T(8,128)S(1)}, f32[64,8,128]{2,1,0:T(8,128)}, bf16[4,32,6912]{2,1,0:T(8,128)(2,1)}) custom-call(bf16[2,224,6912]{2,1,0:T(8,128)(2,1)} %prepare.1.h_ref, f32[16,6912]{1,0:T(8,128)S(1)} %get-tuple-element.42.x_own_ref, f32[64,16,128]{2,1,0:T(8,128)S(1)} %collective-permute-done.1.other_ref, ...), custom_call_target="tpu_custom_call" | custom-call | flops 6442450944 | bytes 4194304 | tf_op jit(solution)/shard_map/search/pallas_call | solution.py:333
  63.0 10.0 %all-to-all-start.2 = ((f32[64,8,128]{2,1,0:T(8,128)}), f32[64,8,128]{2,1,0:T(8,128)S(1)}, u32[]{:S(2)}, u32[]{:S(2)}) async-start(f32[64,8,128]{2,1,0:T(8,128)} %get-tuple-element.48), calls=%async_computation.2 | async-start | bytes 524288 | tf_op jit(solution)/shard_map/all_to_all | solution.py:347
  73.0 5.8 %factor.1 = (f32[48,48]{1,0:T(8,128)S(1)}, f32[48,48]{1,0:T(8,128)S(1)}) custom-call(bf16[4,32,6912]{2,1,0:T(8,128)(2,1)} %get-tuple-element.49.kept_hbm, bf16[3,32,6912]{2,1,0:T(8,128)(2,1)} %get-tuple-element.41.c_hbm, bf16[3,32,6912]{2,1,0:T(8,128)(2,1)} %get-tuple-element.50.p_hbm, f32[32,32]{1,0:T(8,128)S(1)} %get-tuple-element.51.first_ref, ...), custom_call_target="tpu_custom_call" | custom-call | flops 6442450944 | bytes 4194304 | tf_op jit(solution)/shard_map/factor/pallas_call | solution.py:333
  78.8 0.9 %collective-permute-start.2 = (f32[64,8,128]{2,1,0:T(8,128)S(1)}, f32[64,8,128]{2,1,0:T(8,128)S(1)}, u32[]{:S(2)}, u32[]{:S(2)}) collective-permute-start(f32[64,8,128]{2,1,0:T(8,128)S(1)} %all-to-all-done.2.own_ref), channel_id=1, source_target_pairs={{0,1},{1,0},{2,3},{3,2},{4,5},{5,4},{6,7},{7,6},{8,9},{9,8},{10,11... | collective-permute-start | bytes 786440 | tf_op jit(solution)/shard_map/ppermute | solution.py:351
  79.7 1.2 %collective-permute-done.2.other_ref = f32[64,8,128]{2,1,0:T(8,128)S(1)} collective-permute-done((f32[64,8,128]{2,1,0:T(8,128)S(1)}, f32[64,8,128]{2,1,0:T(8,128)S(1)}, u32[]{:S(2)}, u32[]{:S(2)}) %collective-permute-start.2) | collective-permute-done | bytes 262176 | tf_op jit(solution)/shard_map/ppermute | solution.py:351
  80.8 3.2 %finish.1 = (f32[16,108]{1,0:T(8,128)}, f32[16,108]{1,0:T(8,128)}) custom-call(f32[48,48]{1,0:T(8,128)S(1)} %get-tuple-element.54.inverse_ref, f32[48,48]{1,0:T(8,128)S(1)} %get-tuple-element.55.stiff_ref, f32[64,8,128]{2,1,0:T(8,128)S(1)} %all-to-all-done.2.own_ref, f32[64,8,128]{2,1,0:T(8,128)S(1)} %collective-permute-done.2.other_ref, ...), custom_call_target="tpu_custom_call" | custom-call | flops 268435456 | bytes 4194304 | tf_op jit(solution)/shard_map/finish/pallas_call | solution.py:333
  (11 shorter events, 0.0 us)
Async XLA Ops:
  2.5 26.3 %all-to-all-start = ((f32[64,32,108]{2,1,0:T(8,128)}), f32[64,32,108]{2,1,0:T(8,128)S(1)}, u32[]{:S(2)}, u32[]{:S(2)}) async-start(f32[64,32,108]{2,1,0:T(8,128)} %broadcast_in_dim.14), calls=%async_computation | async-start | bytes 2097152 | tf_op jit(solution)/shard_map/all_to_all | solution.py:347
  28.8 4.7 %copy-start = (f32[64,32,108]{2,1,0:T(8,128)}, f32[64,32,108]{2,1,0:T(8,128)S(1)}, u32[]{:S(2)}) copy-start(f32[64,32,108]{2,1,0:T(8,128)S(1)} %all-to-all-done.own_ref) | copy-start | bytes 2654212
  28.8 4.7 %collective-permute-start = (f32[64,32,108]{2,1,0:T(8,128)S(1)}, f32[64,32,108]{2,1,0:T(8,128)S(1)}, u32[]{:S(2)}, u32[]{:S(2)}) collective-permute-start(f32[64,32,108]{2,1,0:T(8,128)S(1)} %all-to-all-done.own_ref), channel_id=1, source_target_pairs={{0,1},{1,0},{2,3},{3,2},{4,5},{5,4},{6,7},{7,6},{8,9},{9,8},{10,11... | collective-permute-start | bytes 2654216 | tf_op jit(solution)/shard_map/ppermute | solution.py:351
  33.4 12.4 %copy-start.1 = (f32[64,32,108]{2,1,0:T(8,128)}, f32[64,32,108]{2,1,0:T(8,128)S(1)}, u32[]{:S(2)}) copy-start(f32[64,32,108]{2,1,0:T(8,128)S(1)} %collective-permute-done.other_ref) | copy-start | bytes 2654212
  35.3 18.0 %all-to-all-start.1 = ((f32[64,16,128]{2,1,0:T(8,128)}), f32[64,16,128]{2,1,0:T(8,128)S(1)}, u32[]{:S(2)}, u32[]{:S(2)}) async-start(f32[64,16,128]{2,1,0:T(8,128)} %get-tuple-element.37), calls=%async_computation.1 | async-start | bytes 1048576 | tf_op jit(solution)/shard_map/all_to_all | solution.py:347
  45.8 9.0 %copy-start.2 = (f32[108,16]{0,1:T(8,128)S(1)}, f32[108,16]{0,1:T(8,128)}, u32[]{:S(2)}) copy-start(f32[108,16]{0,1:T(8,128)} %param.4) | copy-start | bytes 20740
  45.8 9.0 %copy-start.3 = (f32[108,16]{0,1:T(8,128)S(1)}, f32[108,16]{0,1:T(8,128)}, u32[]{:S(2)}) copy-start(f32[108,16]{0,1:T(8,128)} %param.5) | copy-start | bytes 20740
  53.3 3.2 %collective-permute-start.1 = (f32[64,16,128]{2,1,0:T(8,128)S(1)}, f32[64,16,128]{2,1,0:T(8,128)S(1)}, u32[]{:S(2)}, u32[]{:S(2)}) collective-permute-start(f32[64,16,128]{2,1,0:T(8,128)S(1)} %all-to-all-done.1.own_ref), channel_id=1, source_target_pairs={{0,1},{1,0},{2,3},{3,2},{4,5},{5,4},{6,7},{7,6},{8,9},{9,8},{10,11... | collective-permute-start | bytes 1572872 | tf_op jit(solution)/shard_map/ppermute | solution.py:351
  63.0 15.8 %all-to-all-start.2 = ((f32[64,8,128]{2,1,0:T(8,128)}), f32[64,8,128]{2,1,0:T(8,128)S(1)}, u32[]{:S(2)}, u32[]{:S(2)}) async-start(f32[64,8,128]{2,1,0:T(8,128)} %get-tuple-element.48), calls=%async_computation.2 | async-start | bytes 524288 | tf_op jit(solution)/shard_map/all_to_all | solution.py:347
  78.8 2.1 %collective-permute-start.2 = (f32[64,8,128]{2,1,0:T(8,128)S(1)}, f32[64,8,128]{2,1,0:T(8,128)S(1)}, u32[]{:S(2)}, u32[]{:S(2)}) collective-permute-start(f32[64,8,128]{2,1,0:T(8,128)S(1)} %all-to-all-done.2.own_ref), channel_id=1, source_target_pairs={{0,1},{1,0},{2,3},{3,2},{4,5},{5,4},{6,7},{7,6},{8,9},{9,8},{10,11... | collective-permute-start | bytes 786440 | tf_op jit(solution)/shard_map/ppermute | solution.py:351

commit v11 on v10

--- a/solution.py
+++ b/solution.py
@@ -44,13 +44,6 @@
     return high, (x - high.astype(F32)).astype(BF16)
 
 
-def split3(x):
-    high = x.astype(BF16)
-    rest = x - high.astype(F32)
-    mid = rest.astype(BF16)
-    return high, mid, (rest - mid.astype(F32)).astype(BF16)
-
-
 def nt(left, right):
     return lax.dot_general(left, right, (((1,), (1,)), ((), ())), preferred_element_type=F32)
 
@@ -223,12 +216,12 @@
     cross_t = fold(half_cross_ref[...] + nt(i_ref[...], c_ref[1]))
     cross_ref[...] = cross_t
     ritz_t = cross_t / ORDER
-    stacked = jnp.concatenate(split3(ritz_t), axis=0)
+    stacked = jnp.concatenate(split(ritz_t), axis=0)
     stacked = jnp.concatenate([stacked] * PARTS, axis=1)
     square = jnp.zeros((NEIG, 1), F32)
     for half, ref in ((0, x_own_ref), (1, resid_ref.at[1])):
         moved = jnp.dot(stacked, c_ref[half], preferred_element_type=F32)
-        moved = (moved[32:48] + moved[16:32]) + moved[0:16]
+        moved = moved[16:32] + moved[0:16]
         resid = ref[...] - moved
         resid_ref[half] = resid
         square = square + jnp.sum(resid * resid, axis=1, keepdims=True)
@@ -246,10 +239,10 @@
     search_ref[...] = search
     for half, diag in ((0, diag_ref), (1, other_diag_ref)):
         store_parts(scaled(resid_ref[half], diag[...]), s_ref.at[half])
-    kept.append(started(s_ref, kept_ref.at[pl.ds(0, 2)], sems.at[0]))
     copies[0].wait()
     product = nt(h_vmem[0], s_ref[0])
     copies[1].wait()
+    kept.append(started(s_ref, kept_ref.at[pl.ds(0, 2)], sems.at[0]))
     simage = fold_rows(product + nt(h_vmem[1], s_ref[1]))
     pvec = pvec_ref[...]
     terms = jnp.concatenate(

time: 84.5 us -> 84.8 us (level)
  no operation moved by 1% of the time
where the time goes in v11:
time: 84.8 us; the launch traced here: 84.2 us
  starting transfers between devices  38.2 us (45%)
  Pallas kernels  36.8 us (43%)
  waiting for transfers between devices  5.43 us (6%)
  other arithmetic  1.73 us (2%)
  local copies, waits for them, and re-layouts  1.14 us (1%)
    all_to_all x3, starting transfers between devices, to_chips(): return lax.all_to_all(x, AXIS, 0, 0, axis_index_groups=groups, tiled=True)  34.2 us
    pallas_call x7, Pallas kernels, kernel_call(): pl.pallas_call(body, out_shape=[jax.ShapeDtypeStruct(shape, kind) for sha...  29.7 us
    pallas_call x1, Pallas kernels, prepare(): pl.pallas_call(prepare_kernel, grid=(CHUNKS,), out_shape=jax.ShapeDtypeSt...  7.08 us
    all_to_all x3, waiting for transfers between devices, to_chips(): return lax.all_to_all(x, AXIS, 0, 0, axis_index_groups=groups, tiled=True)  4.26 us
    ppermute x3, starting transfers between devices, to_core(): lax.ppermute(x, AXIS, [(device, device ^ 1) for device in range(DEVICES)])  3.96 us
  transfers between devices with their start and end apart: 6, of which 2 were waited for; matrix products, arithmetic and copies ran while one was open for 1% of the time, Pallas kernels for 30%

profile of v11, /device:TPU:1, one launch (start us, length us, event | category | flops | bytes accessed | tf_op | source)
XLA Modules:
  0.0 84.2 jit_solution(14110426130653992711)
XLA Ops:
  0.6 0.7 pad_maximum_fusion
  1.4 1.1 %broadcast_in_dim.14 = f32[64,32,108]{2,1,0:T(8,128)} broadcast(f32[32,108]{1,0:T(8,128)S(1)} %pad_maximum_fusion), dimensions={1,2} | broadcast | bytes 898560 | tf_op jit(solution)/shard_map/broadcast_in_dim | solution.py:359
  2.5 13.7 %all-to-all-start = ((f32[64,32,108]{2,1,0:T(8,128)}), f32[64,32,108]{2,1,0:T(8,128)S(1)}, u32[]{:S(2)}, u32[]{:S(2)}) async-start(f32[64,32,108]{2,1,0:T(8,128)} %broadcast_in_dim.14), calls=%async_computation | async-start | bytes 2097152 | tf_op jit(solution)/shard_map/all_to_all | solution.py:340
  16.2 1.0 %select_reduce_fusion = f32[108]{0:T(128)S(1)} fusion(f32[108,13824]{1,0:T(8,128)} %h_ref.1, s32[]{:T(128)S(6)} %select_n.34), kind=kLoop, calls=%fused_computation.1 | loop fusion | flops 34884 | bytes 47092 | tf_op jit(solution)/shard_map/reduce_sum | solution.py:351
  17.2 7.1 %prepare.1.h_ref = bf16[2,224,6912]{2,1,0:T(8,128)(2,1)} custom-call(f32[108,13824]{1,0:T(8,128)} %h_ref.1), custom_call_target="tpu_custom_call" | custom-call | flops 29859840 | bytes 14929920 | tf_op jit(solution)/shard_map/prepare/pallas_call | solution.py:87
  24.3 0.2 fusion.tile_ref
  24.5 4.3 %all-to-all-done.own_ref = f32[64,32,108]{2,1,0:T(8,128)S(1)} async-done(((f32[64,32,108]{2,1,0:T(8,128)}), f32[64,32,108]{2,1,0:T(8,128)S(1)}, u32[]{:S(2)}, u32[]{:S(2)}) %all-to-all-start) | async-done | bytes 884768 | tf_op jit(solution)/shard_map/all_to_all | solution.py:340
  28.8 1.6 %collective-permute-start = (f32[64,32,108]{2,1,0:T(8,128)S(1)}, f32[64,32,108]{2,1,0:T(8,128)S(1)}, u32[]{:S(2)}, u32[]{:S(2)}) collective-permute-start(f32[64,32,108]{2,1,0:T(8,128)S(1)} %all-to-all-done.own_ref), channel_id=1, source_target_pairs={{0,1},{1,0},{2,3},{3,2},{4,5},{5,4},{6,7},{7,6},{8,9},{9,8},{10,11... | collective-permute-start | bytes 2654216 | tf_op jit(solution)/shard_map/ppermute | solution.py:344
  30.3 3.1 %image_own.1 = (f32[224,64]{1,0:T(8,128)S(1)}, bf16[224,6912]{1,0:T(8,128)(2,1)S(1)}) custom-call(bf16[2,224,6912]{2,1,0:T(8,128)(2,1)} %prepare.1.h_ref, f32[64,32,108]{2,1,0:T(8,128)S(1)} %all-to-all-done.own_ref), custom_call_target="tpu_custom_call" | custom-call | flops 1073741824 | bytes 4194304 | tf_op jit(solution)/shard_map/image_own/pallas_call | solution.py:326
  33.4 0.0 collective-permute-done.other_ref
  33.4 1.9 %image_other.1 = (f32[16,128]{1,0:T(8,128)S(1)}, f32[64,16,128]{2,1,0:T(8,128)}) custom-call(bf16[224,6912]{1,0:T(8,128)(2,1)S(1)} %get-tuple-element.34.h_ref, f32[64,32,108]{2,1,0:T(8,128)S(1)} %collective-permute-done.other_ref, f32[224,64]{1,0:T(8,128)S(1)} %get-tuple-element.35.product_ref, f32[16,128]{1,0:T(8,128)S(1)} %fusion.tile_ref), custom_call_target="tpu_custom_call" | custom-call | flops 1073741824 | bytes 4194304 | tf_op jit(solution)/shard_map/image_other/pallas_call | solution.py:326
  35.3 10.5 %all-to-all-start.1 = ((f32[64,16,128]{2,1,0:T(8,128)}), f32[64,16,128]{2,1,0:T(8,128)S(1)}, u32[]{:S(2)}, u32[]{:S(2)}) async-start(f32[64,16,128]{2,1,0:T(8,128)} %get-tuple-element.37), calls=%async_computation.1 | async-start | bytes 1048576 | tf_op jit(solution)/shard_map/all_to_all | solution.py:340
  45.8 0.0 copy-start.2
  45.8 0.0 copy-start.3
  45.8 7.5 %previous.1 = (f32[16,128]{1,0:T(8,128)S(1)}, bf16[3,32,6912]{2,1,0:T(8,128)(2,1)}, bf16[3,32,6912]{2,1,0:T(8,128)(2,1)}, f32[32,32]{1,0:T(8,128)S(1)}) custom-call(bf16[2,224,6912]{2,1,0:T(8,128)(2,1)} %prepare.1.h_ref, f32[64,32,108]{2,1,0:T(8,128)} %copy-done, f32[64,32,108]{2,1,0:T(8,128)} %copy-done.1, f32[224,64]{1,0:T(8,128)S(1)} %get-tuple-element.35.product_ref), custom_call_target="tpu_custom_call" | custom-call | flops 6442450944 | bytes 4194304 | tf_op jit(solution)/shard_map/previous/pallas_call | solution.py:326
  53.3 1.5 %collective-permute-start.1 = (f32[64,16,128]{2,1,0:T(8,128)S(1)}, f32[64,16,128]{2,1,0:T(8,128)S(1)}, u32[]{:S(2)}, u32[]{:S(2)}) collective-permute-start(f32[64,16,128]{2,1,0:T(8,128)S(1)} %all-to-all-done.1.own_ref), channel_id=1, source_target_pairs={{0,1},{1,0},{2,3},{3,2},{4,5},{5,4},{6,7},{7,6},{8,9},{9,8},{10,11... | collective-permute-start | bytes 1572872 | tf_op jit(solution)/shard_map/ppermute | solution.py:344
  54.9 1.6 %own.1 = (bf16[32,6912]{1,0:T(8,128)(2,1)S(1)}, f32[16,6912]{1,0:T(8,128)S(1)}, f32[32,32]{1,0:T(8,128)S(1)}, f32[1,6912]{1,0:T(1,128)S(1)}) custom-call(f32[64,16,128]{2,1,0:T(8,128)S(1)} %all-to-all-done.1.own_ref, bf16[3,32,6912]{2,1,0:T(8,128)(2,1)} %get-tuple-element.41.c_hbm), custom_call_target="tpu_custom_call" | custom-call | flops 1073741824 | bytes 4194304 | tf_op jit(solution)/shard_map/own/pallas_call | solution.py:326
  56.5 0.0 collective-permute-done.1.other_ref
  56.5 6.7 %search.1 = (f32[16,128]{1,0:T(8,128)S(1)}, f32[16]{0:T(128)}, f32[16,16]{1,0:T(8,128)S(1)}, f32[64,8,128]{2,1,0:T(8,128)}, bf16[4,32,6912]{2,1,0:T(8,128)(2,1)}) custom-call(bf16[2,224,6912]{2,1,0:T(8,128)(2,1)} %prepare.1.h_ref, f32[16,6912]{1,0:T(8,128)S(1)} %get-tuple-element.42.x_own_ref, f32[64,16,128]{2,1,0:T(8,128)S(1)} %collective-permute-done.1.other_ref, ...), custom_call_target="tpu_custom_call" | custom-call | flops 6442450944 | bytes 4194304 | tf_op jit(solution)/shard_map/search/pallas_call | solution.py:326
  63.2 10.0 %all-to-all-start.2 = ((f32[64,8,128]{2,1,0:T(8,128)}), f32[64,8,128]{2,1,0:T(8,128)S(1)}, u32[]{:S(2)}, u32[]{:S(2)}) async-start(f32[64,8,128]{2,1,0:T(8,128)} %get-tuple-element.48), calls=%async_computation.2 | async-start | bytes 524288 | tf_op jit(solution)/shard_map/all_to_all | solution.py:340
  73.2 5.8 %factor.1 = (f32[48,48]{1,0:T(8,128)S(1)}, f32[48,48]{1,0:T(8,128)S(1)}) custom-call(bf16[4,32,6912]{2,1,0:T(8,128)(2,1)} %get-tuple-element.49.kept_hbm, bf16[3,32,6912]{2,1,0:T(8,128)(2,1)} %get-tuple-element.41.c_hbm, bf16[3,32,6912]{2,1,0:T(8,128)(2,1)} %get-tuple-element.50.p_hbm, f32[32,32]{1,0:T(8,128)S(1)} %get-tuple-element.51.first_ref, ...), custom_call_target="tpu_custom_call" | custom-call | flops 6442450944 | bytes 4194304 | tf_op jit(solution)/shard_map/factor/pallas_call | solution.py:326
  79.0 0.9 %collective-permute-start.2 = (f32[64,8,128]{2,1,0:T(8,128)S(1)}, f32[64,8,128]{2,1,0:T(8,128)S(1)}, u32[]{:S(2)}, u32[]{:S(2)}) collective-permute-start(f32[64,8,128]{2,1,0:T(8,128)S(1)} %all-to-all-done.2.own_ref), channel_id=1, source_target_pairs={{0,1},{1,0},{2,3},{3,2},{4,5},{5,4},{6,7},{7,6},{8,9},{9,8},{10,11... | collective-permute-start | bytes 786440 | tf_op jit(solution)/shard_map/ppermute | solution.py:344
  79.9 1.2 %collective-permute-done.2.other_ref = f32[64,8,128]{2,1,0:T(8,128)S(1)} collective-permute-done((f32[64,8,128]{2,1,0:T(8,128)S(1)}, f32[64,8,128]{2,1,0:T(8,128)S(1)}, u32[]{:S(2)}, u32[]{:S(2)}) %collective-permute-start.2) | collective-permute-done | bytes 262176 | tf_op jit(solution)/shard_map/ppermute | solution.py:344
  81.1 3.2 %finish.1 = (f32[16,108]{1,0:T(8,128)}, f32[16,108]{1,0:T(8,128)}) custom-call(f32[48,48]{1,0:T(8,128)S(1)} %get-tuple-element.54.inverse_ref, f32[48,48]{1,0:T(8,128)S(1)} %get-tuple-element.55.stiff_ref, f32[64,8,128]{2,1,0:T(8,128)S(1)} %all-to-all-done.2.own_ref, f32[64,8,128]{2,1,0:T(8,128)S(1)} %collective-permute-done.2.other_ref, ...), custom_call_target="tpu_custom_call" | custom-call | flops 268435456 | bytes 4194304 | tf_op jit(solution)/shard_map/finish/pallas_call | solution.py:326
  (11 shorter events, 0.0 us)
Async XLA Ops:
  2.5 26.3 %all-to-all-start = ((f32[64,32,108]{2,1,0:T(8,128)}), f32[64,32,108]{2,1,0:T(8,128)S(1)}, u32[]{:S(2)}, u32[]{:S(2)}) async-start(f32[64,32,108]{2,1,0:T(8,128)} %broadcast_in_dim.14), calls=%async_computation | async-start | bytes 2097152 | tf_op jit(solution)/shard_map/all_to_all | solution.py:340
  28.8 4.7 %copy-start = (f32[64,32,108]{2,1,0:T(8,128)}, f32[64,32,108]{2,1,0:T(8,128)S(1)}, u32[]{:S(2)}) copy-start(f32[64,32,108]{2,1,0:T(8,128)S(1)} %all-to-all-done.own_ref) | copy-start | bytes 2654212
  28.8 4.7 %collective-permute-start = (f32[64,32,108]{2,1,0:T(8,128)S(1)}, f32[64,32,108]{2,1,0:T(8,128)S(1)}, u32[]{:S(2)}, u32[]{:S(2)}) collective-permute-start(f32[64,32,108]{2,1,0:T(8,128)S(1)} %all-to-all-done.own_ref), channel_id=1, source_target_pairs={{0,1},{1,0},{2,3},{3,2},{4,5},{5,4},{6,7},{7,6},{8,9},{9,8},{10,11... | collective-permute-start | bytes 2654216 | tf_op jit(solution)/shard_map/ppermute | solution.py:344
  33.4 12.4 %copy-start.1 = (f32[64,32,108]{2,1,0:T(8,128)}, f32[64,32,108]{2,1,0:T(8,128)S(1)}, u32[]{:S(2)}) copy-start(f32[64,32,108]{2,1,0:T(8,128)S(1)} %collective-permute-done.other_ref) | copy-start | bytes 2654212
  35.3 18.0 %all-to-all-start.1 = ((f32[64,16,128]{2,1,0:T(8,128)}), f32[64,16,128]{2,1,0:T(8,128)S(1)}, u32[]{:S(2)}, u32[]{:S(2)}) async-start(f32[64,16,128]{2,1,0:T(8,128)} %get-tuple-element.37), calls=%async_computation.1 | async-start | bytes 1048576 | tf_op jit(solution)/shard_map/all_to_all | solution.py:340
  45.8 9.0 %copy-start.2 = (f32[108,16]{0,1:T(8,128)S(1)}, f32[108,16]{0,1:T(8,128)}, u32[]{:S(2)}) copy-start(f32[108,16]{0,1:T(8,128)} %param.4) | copy-start | bytes 20740
  45.8 9.0 %copy-start.3 = (f32[108,16]{0,1:T(8,128)S(1)}, f32[108,16]{0,1:T(8,128)}, u32[]{:S(2)}) copy-start(f32[108,16]{0,1:T(8,128)} %param.5) | copy-start | bytes 20740
  53.3 3.2 %collective-permute-start.1 = (f32[64,16,128]{2,1,0:T(8,128)S(1)}, f32[64,16,128]{2,1,0:T(8,128)S(1)}, u32[]{:S(2)}, u32[]{:S(2)}) collective-permute-start(f32[64,16,128]{2,1,0:T(8,128)S(1)} %all-to-all-done.1.own_ref), channel_id=1, source_target_pairs={{0,1},{1,0},{2,3},{3,2},{4,5},{5,4},{6,7},{7,6},{8,9},{9,8},{10,11... | collective-permute-start | bytes 1572872 | tf_op jit(solution)/shard_map/ppermute | solution.py:344
  63.2 15.8 %all-to-all-start.2 = ((f32[64,8,128]{2,1,0:T(8,128)}), f32[64,8,128]{2,1,0:T(8,128)S(1)}, u32[]{:S(2)}, u32[]{:S(2)}) async-start(f32[64,8,128]{2,1,0:T(8,128)} %get-tuple-element.48), calls=%async_computation.2 | async-start | bytes 524288 | tf_op jit(solution)/shard_map/all_to_all | solution.py:340
  79.0 2.1 %collective-permute-start.2 = (f32[64,8,128]{2,1,0:T(8,128)S(1)}, f32[64,8,128]{2,1,0:T(8,128)S(1)}, u32[]{:S(2)}, u32[]{:S(2)}) collective-permute-start(f32[64,8,128]{2,1,0:T(8,128)S(1)} %all-to-all-done.2.own_ref), channel_id=1, source_target_pairs={{0,1},{1,0},{2,3},{3,2},{4,5},{5,4},{6,7},{7,6},{8,9},{9,8},{10,11... | collective-permute-start | bytes 786440 | tf_op jit(solution)/shard_map/ppermute | solution.py:344

commit v12 on v10

--- a/solution.py
+++ b/solution.py
@@ -16,7 +16,7 @@
 CHIPS = DEVICES // 2
 LANES = 128
 FORWARD = list(range(CHIPS))
-BACKWARD = FORWARD[::-1]
+BACKWARD = [16 * (p % 4) + 4 * (p // 16) + (p // 4) % 4 for p in FORWARD[::-1]]
 ORDERS = (BACKWARD, BACKWARD, BACKWARD)
 SLOTS = [[order.index(chip) for chip in range(CHIPS)] for order in ORDERS]
 HALF = CHIPS * ROWS

time: 84.5 us -> 84.2 us (level)
    all_to_all x3, starting transfers between devices: 34.2 us -> 33.3 us  [to_chips(): return lax.all_to_all(x, AXIS, 0, 0, axis_index_groups=groups, tiled=True)]
where the time goes in v12:
time: 84.2 us; the launch traced here: 83.7 us
  starting transfers between devices  38.1 us (45%)
  Pallas kernels  36.6 us (43%)
  waiting for transfers between devices  5.19 us (6%)
  other arithmetic  1.73 us (2%)
  local copies, waits for them, and re-layouts  1.14 us (1%)
    all_to_all x3, starting transfers between devices, to_chips(): return lax.all_to_all(x, AXIS, 0, 0, axis_index_groups=groups, tiled=True)  33.3 us
    pallas_call x7, Pallas kernels, kernel_call(): pl.pallas_call(body, out_shape=[jax.ShapeDtypeStruct(shape, kind) for sha...  29.5 us
    pallas_call x1, Pallas kernels, prepare(): pl.pallas_call(prepare_kernel, grid=(CHUNKS,), out_shape=jax.ShapeDtypeSt...  7.08 us
    ppermute x3, starting transfers between devices, to_core(): lax.ppermute(x, AXIS, [(device, device ^ 1) for device in range(DEVICES)])  4.79 us
    all_to_all x3, waiting for transfers between devices, to_chips(): return lax.all_to_all(x, AXIS, 0, 0, axis_index_groups=groups, tiled=True)  4.03 us
  transfers between devices with their start and end apart: 6, of which 2 were waited for; matrix products, arithmetic and copies ran while one was open for 1% of the time, Pallas kernels for 30%

profile of v12, /device:TPU:1, one launch (start us, length us, event | category | flops | bytes accessed | tf_op | source)
XLA Modules:
  0.0 83.7 jit_solution(7964681651164925273)
XLA Ops:
  0.6 0.7 pad_maximum_fusion
  1.4 1.1 %broadcast_in_dim.14 = f32[64,32,108]{2,1,0:T(8,128)} broadcast(f32[32,108]{1,0:T(8,128)S(1)} %pad_maximum_fusion), dimensions={1,2} | broadcast | bytes 898560 | tf_op jit(solution)/shard_map/broadcast_in_dim | solution.py:366
  2.5 13.7 %all-to-all-start = ((f32[64,32,108]{2,1,0:T(8,128)}), f32[64,32,108]{2,1,0:T(8,128)S(1)}, u32[]{:S(2)}, u32[]{:S(2)}) async-start(f32[64,32,108]{2,1,0:T(8,128)} %broadcast_in_dim.14), calls=%async_computation | async-start | bytes 2097152 | tf_op jit(solution)/shard_map/all_to_all | solution.py:347
  16.2 1.0 %select_reduce_fusion = f32[108]{0:T(128)S(1)} fusion(f32[108,13824]{1,0:T(8,128)} %h_ref.1, s32[]{:T(128)S(6)} %select_n.34), kind=kLoop, calls=%fused_computation.1 | loop fusion | flops 34884 | bytes 47092 | tf_op jit(solution)/shard_map/reduce_sum | solution.py:358
  17.2 7.1 %prepare.1.h_ref = bf16[2,224,6912]{2,1,0:T(8,128)(2,1)} custom-call(f32[108,13824]{1,0:T(8,128)} %h_ref.1), custom_call_target="tpu_custom_call" | custom-call | flops 29859840 | bytes 14929920 | tf_op jit(solution)/shard_map/prepare/pallas_call | solution.py:94
  24.3 0.2 fusion.tile_ref
  24.5 4.0 %all-to-all-done.own_ref = f32[64,32,108]{2,1,0:T(8,128)S(1)} async-done(((f32[64,32,108]{2,1,0:T(8,128)}), f32[64,32,108]{2,1,0:T(8,128)S(1)}, u32[]{:S(2)}, u32[]{:S(2)}) %all-to-all-start) | async-done | bytes 884768 | tf_op jit(solution)/shard_map/all_to_all | solution.py:347
  28.5 2.1 %collective-permute-start = (f32[64,32,108]{2,1,0:T(8,128)S(1)}, f32[64,32,108]{2,1,0:T(8,128)S(1)}, u32[]{:S(2)}, u32[]{:S(2)}) collective-permute-start(f32[64,32,108]{2,1,0:T(8,128)S(1)} %all-to-all-done.own_ref), channel_id=1, source_target_pairs={{0,1},{1,0},{2,3},{3,2},{4,5},{5,4},{6,7},{7,6},{8,9},{9,8},{10,11... | collective-permute-start | bytes 2654216 | tf_op jit(solution)/shard_map/ppermute | solution.py:351
  30.6 3.1 %image_own.1 = (f32[224,64]{1,0:T(8,128)S(1)}, bf16[224,6912]{1,0:T(8,128)(2,1)S(1)}) custom-call(bf16[2,224,6912]{2,1,0:T(8,128)(2,1)} %prepare.1.h_ref, f32[64,32,108]{2,1,0:T(8,128)S(1)} %all-to-all-done.own_ref), custom_call_target="tpu_custom_call" | custom-call | flops 1073741824 | bytes 4194304 | tf_op jit(solution)/shard_map/image_own/pallas_call | solution.py:333
  33.7 0.0 collective-permute-done.other_ref
  33.7 1.9 %image_other.1 = (f32[16,128]{1,0:T(8,128)S(1)}, f32[64,16,128]{2,1,0:T(8,128)}) custom-call(bf16[224,6912]{1,0:T(8,128)(2,1)S(1)} %get-tuple-element.34.h_ref, f32[64,32,108]{2,1,0:T(8,128)S(1)} %collective-permute-done.other_ref, f32[224,64]{1,0:T(8,128)S(1)} %get-tuple-element.35.product_ref, f32[16,128]{1,0:T(8,128)S(1)} %fusion.tile_ref), custom_call_target="tpu_custom_call" | custom-call | flops 1073741824 | bytes 4194304 | tf_op jit(solution)/shard_map/image_other/pallas_call | solution.py:333
  35.6 10.0 %all-to-all-start.1 = ((f32[64,16,128]{2,1,0:T(8,128)}), f32[64,16,128]{2,1,0:T(8,128)S(1)}, u32[]{:S(2)}, u32[]{:S(2)}) async-start(f32[64,16,128]{2,1,0:T(8,128)} %get-tuple-element.37), calls=%async_computation.1 | async-start | bytes 1048576 | tf_op jit(solution)/shard_map/all_to_all | solution.py:347
  45.6 0.0 copy-start.2
  45.6 0.0 copy-start.3
  45.7 7.5 %previous.1 = (f32[16,128]{1,0:T(8,128)S(1)}, bf16[3,32,6912]{2,1,0:T(8,128)(2,1)}, bf16[3,32,6912]{2,1,0:T(8,128)(2,1)}, f32[32,32]{1,0:T(8,128)S(1)}) custom-call(bf16[2,224,6912]{2,1,0:T(8,128)(2,1)} %prepare.1.h_ref, f32[64,32,108]{2,1,0:T(8,128)} %copy-done, f32[64,32,108]{2,1,0:T(8,128)} %copy-done.1, f32[224,64]{1,0:T(8,128)S(1)} %get-tuple-element.35.product_ref), custom_call_target="tpu_custom_call" | custom-call | flops 6442450944 | bytes 4194304 | tf_op jit(solution)/shard_map/previous/pallas_call | solution.py:333
  53.1 0.0 all-to-all-done.1.own_ref
  53.2 1.7 %collective-permute-start.1 = (f32[64,16,128]{2,1,0:T(8,128)S(1)}, f32[64,16,128]{2,1,0:T(8,128)S(1)}, u32[]{:S(2)}, u32[]{:S(2)}) collective-permute-start(f32[64,16,128]{2,1,0:T(8,128)S(1)} %all-to-all-done.1.own_ref), channel_id=1, source_target_pairs={{0,1},{1,0},{2,3},{3,2},{4,5},{5,4},{6,7},{7,6},{8,9},{9,8},{10,11... | collective-permute-start | bytes 1572872 | tf_op jit(solution)/shard_map/ppermute | solution.py:351
  54.9 1.6 %own.1 = (bf16[32,6912]{1,0:T(8,128)(2,1)S(1)}, f32[16,6912]{1,0:T(8,128)S(1)}, f32[32,32]{1,0:T(8,128)S(1)}, f32[1,6912]{1,0:T(1,128)S(1)}) custom-call(f32[64,16,128]{2,1,0:T(8,128)S(1)} %all-to-all-done.1.own_ref, bf16[3,32,6912]{2,1,0:T(8,128)(2,1)} %get-tuple-element.41.c_hbm), custom_call_target="tpu_custom_call" | custom-call | flops 1073741824 | bytes 4194304 | tf_op jit(solution)/shard_map/own/pallas_call | solution.py:333
  56.6 6.5 %search.1 = (f32[16,128]{1,0:T(8,128)S(1)}, f32[16]{0:T(128)}, f32[16,16]{1,0:T(8,128)S(1)}, f32[64,8,128]{2,1,0:T(8,128)}, bf16[4,32,6912]{2,1,0:T(8,128)(2,1)}) custom-call(bf16[2,224,6912]{2,1,0:T(8,128)(2,1)} %prepare.1.h_ref, f32[16,6912]{1,0:T(8,128)S(1)} %get-tuple-element.42.x_own_ref, f32[64,16,128]{2,1,0:T(8,128)S(1)} %collective-permute-done.1.other_ref, ...), custom_call_target="tpu_custom_call" | custom-call | flops 6442450944 | bytes 4194304 | tf_op jit(solution)/shard_map/search/pallas_call | solution.py:333
  63.1 9.6 %all-to-all-start.2 = ((f32[64,8,128]{2,1,0:T(8,128)}), f32[64,8,128]{2,1,0:T(8,128)S(1)}, u32[]{:S(2)}, u32[]{:S(2)}) async-start(f32[64,8,128]{2,1,0:T(8,128)} %get-tuple-element.48), calls=%async_computation.2 | async-start | bytes 524288 | tf_op jit(solution)/shard_map/all_to_all | solution.py:347
  72.6 5.8 %factor.1 = (f32[48,48]{1,0:T(8,128)S(1)}, f32[48,48]{1,0:T(8,128)S(1)}) custom-call(bf16[4,32,6912]{2,1,0:T(8,128)(2,1)} %get-tuple-element.49.kept_hbm, bf16[3,32,6912]{2,1,0:T(8,128)(2,1)} %get-tuple-element.41.c_hbm, bf16[3,32,6912]{2,1,0:T(8,128)(2,1)} %get-tuple-element.50.p_hbm, f32[32,32]{1,0:T(8,128)S(1)} %get-tuple-element.51.first_ref, ...), custom_call_target="tpu_custom_call" | custom-call | flops 6442450944 | bytes 4194304 | tf_op jit(solution)/shard_map/factor/pallas_call | solution.py:333
  78.4 0.9 %collective-permute-start.2 = (f32[64,8,128]{2,1,0:T(8,128)S(1)}, f32[64,8,128]{2,1,0:T(8,128)S(1)}, u32[]{:S(2)}, u32[]{:S(2)}) collective-permute-start(f32[64,8,128]{2,1,0:T(8,128)S(1)} %all-to-all-done.2.own_ref), channel_id=1, source_target_pairs={{0,1},{1,0},{2,3},{3,2},{4,5},{5,4},{6,7},{7,6},{8,9},{9,8},{10,11... | collective-permute-start | bytes 786440 | tf_op jit(solution)/shard_map/ppermute | solution.py:351
  79.4 1.2 %collective-permute-done.2.other_ref = f32[64,8,128]{2,1,0:T(8,128)S(1)} collective-permute-done((f32[64,8,128]{2,1,0:T(8,128)S(1)}, f32[64,8,128]{2,1,0:T(8,128)S(1)}, u32[]{:S(2)}, u32[]{:S(2)}) %collective-permute-start.2) | collective-permute-done | bytes 262176 | tf_op jit(solution)/shard_map/ppermute | solution.py:351
  80.5 3.2 %finish.1 = (f32[16,108]{1,0:T(8,128)}, f32[16,108]{1,0:T(8,128)}) custom-call(f32[48,48]{1,0:T(8,128)S(1)} %get-tuple-element.54.inverse_ref, f32[48,48]{1,0:T(8,128)S(1)} %get-tuple-element.55.stiff_ref, f32[64,8,128]{2,1,0:T(8,128)S(1)} %all-to-all-done.2.own_ref, f32[64,8,128]{2,1,0:T(8,128)S(1)} %collective-permute-done.2.other_ref, ...), custom_call_target="tpu_custom_call" | custom-call | flops 268435456 | bytes 4194304 | tf_op jit(solution)/shard_map/finish/pallas_call | solution.py:333
  (11 shorter events, 0.0 us)
Async XLA Ops:
  2.5 26.1 %all-to-all-start = ((f32[64,32,108]{2,1,0:T(8,128)}), f32[64,32,108]{2,1,0:T(8,128)S(1)}, u32[]{:S(2)}, u32[]{:S(2)}) async-start(f32[64,32,108]{2,1,0:T(8,128)} %broadcast_in_dim.14), calls=%async_computation | async-start | bytes 2097152 | tf_op jit(solution)/shard_map/all_to_all | solution.py:347
  28.5 5.2 %copy-start = (f32[64,32,108]{2,1,0:T(8,128)}, f32[64,32,108]{2,1,0:T(8,128)S(1)}, u32[]{:S(2)}) copy-start(f32[64,32,108]{2,1,0:T(8,128)S(1)} %all-to-all-done.own_ref) | copy-start | bytes 2654212
  28.5 5.2 %collective-permute-start = (f32[64,32,108]{2,1,0:T(8,128)S(1)}, f32[64,32,108]{2,1,0:T(8,128)S(1)}, u32[]{:S(2)}, u32[]{:S(2)}) collective-permute-start(f32[64,32,108]{2,1,0:T(8,128)S(1)} %all-to-all-done.own_ref), channel_id=1, source_target_pairs={{0,1},{1,0},{2,3},{3,2},{4,5},{5,4},{6,7},{7,6},{8,9},{9,8},{10,11... | collective-permute-start | bytes 2654216 | tf_op jit(solution)/shard_map/ppermute | solution.py:351
  33.7 11.9 %copy-start.1 = (f32[64,32,108]{2,1,0:T(8,128)}, f32[64,32,108]{2,1,0:T(8,128)S(1)}, u32[]{:S(2)}) copy-start(f32[64,32,108]{2,1,0:T(8,128)S(1)} %collective-permute-done.other_ref) | copy-start | bytes 2654212
  35.6 17.5 %all-to-all-start.1 = ((f32[64,16,128]{2,1,0:T(8,128)}), f32[64,16,128]{2,1,0:T(8,128)S(1)}, u32[]{:S(2)}, u32[]{:S(2)}) async-start(f32[64,16,128]{2,1,0:T(8,128)} %get-tuple-element.37), calls=%async_computation.1 | async-start | bytes 1048576 | tf_op jit(solution)/shard_map/all_to_all | solution.py:347
  45.6 9.3 %copy-start.2 = (f32[108,16]{0,1:T(8,128)S(1)}, f32[108,16]{0,1:T(8,128)}, u32[]{:S(2)}) copy-start(f32[108,16]{0,1:T(8,128)} %param.4) | copy-start | bytes 20740
  45.6 9.3 %copy-start.3 = (f32[108,16]{0,1:T(8,128)S(1)}, f32[108,16]{0,1:T(8,128)}, u32[]{:S(2)}) copy-start(f32[108,16]{0,1:T(8,128)} %param.5) | copy-start | bytes 20740
  53.2 3.4 %collective-permute-start.1 = (f32[64,16,128]{2,1,0:T(8,128)S(1)}, f32[64,16,128]{2,1,0:T(8,128)S(1)}, u32[]{:S(2)}, u32[]{:S(2)}) collective-permute-start(f32[64,16,128]{2,1,0:T(8,128)S(1)} %all-to-all-done.1.own_ref), channel_id=1, source_target_pairs={{0,1},{1,0},{2,3},{3,2},{4,5},{5,4},{6,7},{7,6},{8,9},{9,8},{10,11... | collective-permute-start | bytes 1572872 | tf_op jit(solution)/shard_map/ppermute | solution.py:351
  63.1 15.4 %all-to-all-start.2 = ((f32[64,8,128]{2,1,0:T(8,128)}), f32[64,8,128]{2,1,0:T(8,128)S(1)}, u32[]{:S(2)}, u32[]{:S(2)}) async-start(f32[64,8,128]{2,1,0:T(8,128)} %get-tuple-element.48), calls=%async_computation.2 | async-start | bytes 524288 | tf_op jit(solution)/shard_map/all_to_all | solution.py:347
  78.4 2.1 %collective-permute-start.2 = (f32[64,8,128]{2,1,0:T(8,128)S(1)}, f32[64,8,128]{2,1,0:T(8,128)S(1)}, u32[]{:S(2)}, u32[]{:S(2)}) collective-permute-start(f32[64,8,128]{2,1,0:T(8,128)S(1)} %all-to-all-done.2.own_ref), channel_id=1, source_target_pairs={{0,1},{1,0},{2,3},{3,2},{4,5},{5,4},{6,7},{7,6},{8,9},{9,8},{10,11... | collective-permute-start | bytes 786440 | tf_op jit(solution)/shard_map/ppermute | solution.py:351
